TPU v7x, 512 devices: a whole 4x4x16 slice. The times are simulated.
512 devices in a mesh: gx: 32 (over x, z_hi, core), yz: 16 (over z_lo, y).
Axes of the slice: x: 4, y: 4, z: 16 (z_hi: 4, z_lo: 4; z = z_hi * 4 + z_lo), core: 2. Of those that a mesh axis runs over, the one named last changes fastest.
Arguments:
- velocity: float32 [3, 64, 128, 128], P(None, 'gx', 'yz'), may hold values from -6 to 6
- viscosity: float32 [64, 128, 128], P('gx', 'yz'), may hold values from 0.1 to 1
- cotangent: float32 [3, 64, 128, 128], P(None, 'gx', 'yz'), may hold values from -6 to 6
- assignment: int32 [8192, 1], P(('gx', 'yz')), may hold values from 0 to 15; in each aligned block of 16 rows (0 to 15, 16 to 31, ...) at most 2 rows name the same one
- w_in: float32 [16, 9, 128], P('yz'), may hold values from -2 to 2
- b_in: float32 [16, 128], P('yz'), may hold values from -3 to 3
- w_mid: float32 [16, 128, 128], P('yz'), may hold values from -0.5 to 0.5
- b_mid: float32 [16, 128], P('yz'), may hold values from -3 to 3
- w_out: float32 [16, 128, 6], P('yz'), may hold values from -0.5 to 0.5
- b_out: float32 [16, 6], P('yz'), may hold values from -3 to 3
Outputs:
- predicted: float32 [3, 64, 128, 128], P(None, 'gx', 'yz')
- grad_velocity: float32 [3, 64, 128, 128], P(None, 'gx', 'yz')
- grad_w_in: float32 [16, 9, 128], P('yz')
- grad_b_in: float32 [16, 128], P('yz')
- grad_w_mid: float32 [16, 128, 128], P('yz')
- grad_b_mid: float32 [16, 128], P('yz')
- grad_w_out: float32 [16, 128, 6], P('yz')
- grad_b_out: float32 [16, 6], P('yz')
Inputs may be any that keep to these rules, and one draw needn't show every extreme that they name: `assignment`: of the 16 rows of one device, at most 2 name any one network.
All inputs are finite; a program needn't handle non-finite values.
Results may differ from a plain program's by a relative error of at most 0.00019.
Values sent between devices are 32-bit elements; how exact they have to be, the bound alone decides.
No kernel may reach another device: no remote copies, remote signals or barrier semaphores. Data moves between devices by JAX's collectives and lax.ppermute only.
A program may use at most 64 MiB of HBM per device.

v0:
```python
import jax
import jax.numpy as jnp
from jax import lax
from jax.sharding import PartitionSpec as P

SUBSTEPS = 4


step_size = 0.15
stress_scale = 0.5
stress_pairs = ((0, 3, 4), (3, 1, 5), (4, 5, 2))
highest = lax.Precision.HIGHEST


def padded_2(block, sides, width):
    for axis, dim in sides:
        count = lax.axis_size(axis)
        forward = [(i, i + 1) for i in range(count - 1)]
        forward.append((count - 1, 0))
        backward = [(target, source) for source, target in forward]
        low = lax.ppermute(
            lax.slice_in_dim(block, block.shape[dim] - width, None, axis=dim), axis, forward
        )
        high = lax.ppermute(lax.slice_in_dim(block, 0, width, axis=dim), axis, backward)
        block = jnp.concatenate([low, block, high], axis=dim)
    return block


def forward_rim(values):
    return padded_2(values, (("gx", 1), ("yz", 2)), 1)


def adjoint_rim(values):
    return padded_2(values, (("gx", 1), ("yz", 2)), 1)


def face_coefficients(padded_visc):
    center = padded_visc[1:-1, 1:-1]
    return (
        (0.5 * (center + padded_visc[2:, 1:-1]), 0.5 * (center + padded_visc[:-2, 1:-1])),
        (0.5 * (center + padded_visc[1:-1, 2:]), 0.5 * (center + padded_visc[1:-1, :-2])),
        (0.5 * (center + jnp.roll(center, -1, 2)), 0.5 * (center + jnp.roll(center, 1, 2))),
    )


def diffuse(values, coeffs, fetch_rim):
    padded = fetch_rim(values)
    center = padded[:, 1:-1, 1:-1]
    neighbours = (
        (padded[:, 2:, 1:-1], padded[:, :-2, 1:-1]),
        (padded[:, 1:-1, 2:], padded[:, 1:-1, :-2]),
        (jnp.roll(center, -1, 3), jnp.roll(center, 1, 3)),
    )
    flux_sum = jnp.zeros_like(center)
    for dimension in range(3):
        forward_coeff, backward_coeff = coeffs[dimension]
        leading, trailing = neighbours[dimension]
        flux_sum = (
            flux_sum + forward_coeff * (leading - center) - backward_coeff * (center - trailing)
        )
    return center + step_size * flux_sum


def differences(padded):
    center = padded[:, 1:-1, 1:-1]
    along_x = 0.5 * (padded[:, 2:, 1:-1] - padded[:, :-2, 1:-1])
    along_y = 0.5 * (padded[:, 1:-1, 2:] - padded[:, 1:-1, :-2])
    along_z = 0.5 * (jnp.roll(center, -1, 3) - jnp.roll(center, 1, 3))
    return (along_x, along_y, along_z)


def divergence(derivatives):
    pieces = []
    for component in range(3):
        pairs = stress_pairs[component]
        pieces.append(
            derivatives[0][pairs[0]] + derivatives[1][pairs[1]] + derivatives[2][pairs[2]]
        )
    return jnp.stack(pieces)


def stress_adjoint(derivatives):
    pieces = [jnp.zeros_like(derivatives[0][0]) for number in range(6)]
    for component in range(3):
        for dimension in range(3):
            target = stress_pairs[component][dimension]
            pieces[target] = pieces[target] + derivatives[dimension][component]
    return stress_scale * jnp.stack(pieces)


def slot_table(assignment, experts):
    owners = assignment[:, 0]
    columns = owners.shape[0]
    capacity = 2 * columns // experts
    one_hot = (owners[:, None] == jnp.arange(experts, dtype=jnp.int32)[None, :]).astype(jnp.int32)
    slot_rank = jnp.sum((jnp.cumsum(one_hot, axis=0) - one_hot) * one_hot, axis=1)
    slot_index = owners * capacity + slot_rank
    source_column = (
        jnp.zeros((experts * capacity,), jnp.int32)
        .at[slot_index]
        .set(jnp.arange(columns, dtype=jnp.int32))
    )
    occupied = jnp.zeros((experts * capacity,), jnp.float32).at[slot_index].set(1.0)
    return (slot_index, source_column, occupied, capacity)


def to_slots(values, source_column, occupied, experts, capacity):
    channels, rows_x, rows_y, cell_count = values.shape
    by_column = jnp.transpose(values, (1, 2, 0, 3)).reshape(rows_x * rows_y, channels, cell_count)
    picked = by_column[source_column] * occupied[:, None, None]
    return picked.reshape(experts, capacity, channels, cell_count)


def from_slots(buffer, slot_index, rows_x, rows_y):
    experts, capacity, channels, cell_count = buffer.shape
    picked = buffer.reshape(experts * capacity, channels, cell_count)[slot_index]
    return jnp.transpose(picked.reshape(rows_x, rows_y, channels, cell_count), (2, 0, 1, 3))


def network(features, params):
    w_in, b_in, w_mid, b_mid, w_out, b_out = params
    hidden_one = jnp.tanh(
        jnp.einsum("esfc,efh->eshc", features, w_in, precision=highest) + b_in[:, None, :, None]
    )
    hidden_two = jnp.tanh(
        jnp.einsum("eshc,ehk->eskc", hidden_one, w_mid, precision=highest) + b_mid[:, None, :, None]
    )
    stress = (
        jnp.einsum("eshc,eho->esoc", hidden_two, w_out, precision=highest) + b_out[:, None, :, None]
    )
    return (stress, hidden_one, hidden_two)


def network_grads(features, hidden_one, hidden_two, stress_grad, params):
    w_in, b_in, w_mid, b_mid, w_out, b_out = params
    grad_w_out = jnp.einsum("eshc,esoc->eho", hidden_two, stress_grad, precision=highest)
    grad_b_out = jnp.sum(stress_grad, axis=(1, 3))
    grad_second = jnp.einsum("esoc,eho->eshc", stress_grad, w_out, precision=highest) * (
        1.0 - hidden_two * hidden_two
    )
    grad_w_mid = jnp.einsum("eshc,eskc->ehk", hidden_one, grad_second, precision=highest)
    grad_b_mid = jnp.sum(grad_second, axis=(1, 3))
    grad_first = jnp.einsum("eskc,ehk->eshc", grad_second, w_mid, precision=highest) * (
        1.0 - hidden_one * hidden_one
    )
    grad_w_in = jnp.einsum("esfc,eshc->efh", features, grad_first, precision=highest)
    grad_b_in = jnp.sum(grad_first, axis=(1, 3))
    feature_grad = jnp.einsum("eshc,efh->esfc", grad_first, w_in, precision=highest)
    return (feature_grad, (grad_w_in, grad_b_in, grad_w_mid, grad_b_mid, grad_w_out, grad_b_out))


def local(velocity, viscosity, cotangent, assignment, w_in, b_in, w_mid, b_mid, w_out, b_out):
    experts = lax.axis_size("yz")
    rows_x, rows_y = (velocity.shape[1], velocity.shape[2])
    padded_visc = padded_2(viscosity, (("gx", 0), ("yz", 1)), 1)
    coeffs = face_coefficients(padded_visc)
    velocity_now = velocity
    for substep in range(SUBSTEPS):
        velocity_now = diffuse(velocity_now, coeffs, forward_rim)
    along_x, along_y, along_z = differences(forward_rim(velocity_now))
    features = jnp.stack((along_x, along_y, along_z), axis=1).reshape((9,) + velocity_now.shape[1:])
    cotangent_x, cotangent_y, cotangent_z = differences(adjoint_rim(cotangent))
    stress_grad = stress_adjoint((cotangent_x, cotangent_y, cotangent_z))
    slot_index, source_column, occupied, capacity = slot_table(assignment, experts)
    send_features = to_slots(features, source_column, occupied, experts, capacity)
    send_stress_grad = to_slots(stress_grad, source_column, occupied, experts, capacity)
    group_params = (
        lax.all_gather(w_in, "yz", axis=0, tiled=True),
        lax.all_gather(b_in, "yz", axis=0, tiled=True),
        lax.all_gather(w_mid, "yz", axis=0, tiled=True),
        lax.all_gather(b_mid, "yz", axis=0, tiled=True),
        lax.all_gather(w_out, "yz", axis=0, tiled=True),
        lax.all_gather(b_out, "yz", axis=0, tiled=True),
    )
    stress_home, hidden_one, hidden_two = network(send_features, group_params)
    feature_home, expert_grads = network_grads(
        send_features, hidden_one, hidden_two, send_stress_grad, group_params
    )
    weight_grads = (
        lax.psum_scatter(expert_grads[0], "yz", scatter_dimension=0, tiled=True),
        lax.psum_scatter(expert_grads[1], "yz", scatter_dimension=0, tiled=True),
        lax.psum_scatter(expert_grads[2], "yz", scatter_dimension=0, tiled=True),
        lax.psum_scatter(expert_grads[3], "yz", scatter_dimension=0, tiled=True),
        lax.psum_scatter(expert_grads[4], "yz", scatter_dimension=0, tiled=True),
        lax.psum_scatter(expert_grads[5], "yz", scatter_dimension=0, tiled=True),
    )
    weight_grads = lax.psum(
        (
            weight_grads[0],
            weight_grads[1],
            weight_grads[2],
            weight_grads[3],
            weight_grads[4],
            weight_grads[5],
        ),
        "gx",
    )
    stress = from_slots(stress_home, slot_index, rows_x, rows_y)
    predicted = velocity_now - stress_scale * divergence(differences(forward_rim(stress)))
    feature_grad = from_slots(feature_home, slot_index, rows_x, rows_y)
    feature_x, feature_y, feature_z = differences(adjoint_rim(feature_grad))
    adjoint = cotangent - (feature_x[0::3] + feature_y[1::3] + feature_z[2::3])
    for substep in range(SUBSTEPS):
        adjoint = diffuse(adjoint, coeffs, adjoint_rim)
    return (
        predicted,
        adjoint,
        weight_grads[0],
        weight_grads[1],
        weight_grads[2],
        weight_grads[3],
        weight_grads[4],
        weight_grads[5],
    )


def solution(mesh):
    placed = (
        P(None, "gx", "yz", None),
        P("gx", "yz", None),
        P(None, "gx", "yz", None),
        P(("gx", "yz"), None),
        P("yz", None, None),
        P("yz", None),
        P("yz", None, None),
        P("yz", None),
        P("yz", None, None),
        P("yz", None),
    )
    return jax.shard_map(
        local,
        mesh=mesh,
        in_specs=placed,
        out_specs=(
            P(None, "gx", "yz", None),
            P(None, "gx", "yz", None),
            P("yz", None, None),
            P("yz", None),
            P("yz", None, None),
            P("yz", None),
            P("yz", None, None),
            P("yz", None),
        ),
        check_vma=False,
    )
```

profile of v0, /device:TPU:24, one launch (start us, length us, event | category | flops | bytes accessed | tf_op | source)
XLA Modules:
  0.0 1073.7 jit_solution(10296638660309803701)
XLA Ops:
  8.7 14.4 %collective-permute-start = (f32[1,8,128]{2,1,0:T(8,128)S(1)}, f32[1,8,128]{2,1,0:T(8,128)S(1)}, u32[]{:S(2)}, u32[]{:S(2)}) collective-permute-start(f32[1,8,128]{2,1,0:T(8,128)S(1)} %get-tuple-element.172), channel_id=1, source_target_pairs={{16,0},{32,16},{48,32},{64,48},{80,64},{96,80},{112,96},{128,112},... | collective-permute-start | bytes 12296 | tf_op jit(solution)/shard_map/ppermute | solution.py:24
  25.7 9.6 collective-permute-start.1
  38.0 9.6 collective-permute-start.28
  57.2 33.2 %all_gather.18 = f32[16,9,128]{2,1,0:T(8,128)S(1)} all-gather(f32[1,9,128]{2,1,0:T(8,128)S(1)} %copy.105), channel_id=1, replica_groups=mesh['gx'=32,'yz'=16] {'yz'}, dimensions={0}, use_global_device_ids=true | all-gather | bytes 78336 | tf_op jit(solution)/shard_map/all_gather | solution.py:168
  90.5 41.5 %all_gather.22 = f32[16,128,6]{1,2,0:T(8,128)S(1)} all-gather(f32[1,128,6]{1,2,0:T(8,128)S(1)} %copy.106), channel_id=1, replica_groups=mesh['gx'=32,'yz'=16] {'yz'}, dimensions={0}, use_global_device_ids=true | all-gather | bytes 52224 | tf_op jit(solution)/shard_map/all_gather | solution.py:172
  132.0 36.9 %all-gather = f32[16,1,128]{2,1,0:T(1,128)S(1)} all-gather(f32[1,1,128]{2,1,0:T(1,128)} %bitcast.159), channel_id=1, replica_groups=mesh['gx'=32,'yz'=16] {'yz'}, dimensions={0}, use_global_device_ids=true | all-gather | bytes 8704 | tf_op jit(solution)/shard_map/all_gather | solution.py:169
  177.5 36.8 %all-gather.1 = f32[16,1,128]{2,1,0:T(1,128)S(1)} all-gather(f32[1,1,128]{2,1,0:T(1,128)} %bitcast.160), channel_id=1, replica_groups=mesh['gx'=32,'yz'=16] {'yz'}, dimensions={0}, use_global_device_ids=true | all-gather | bytes 8704 | tf_op jit(solution)/shard_map/all_gather | solution.py:171
  216.3 40.8 %all-gather.2 = f32[16,1,6]{2,1,0:T(1,128)S(1)} all-gather(f32[1,1,6]{2,1,0:T(1,128)} %bitcast.161), channel_id=1, replica_groups=mesh['gx'=32,'yz'=16] {'yz'}, dimensions={0}, use_global_device_ids=true | all-gather | bytes 408 | tf_op jit(solution)/shard_map/all_gather | solution.py:173
  259.9 8.2 collective-permute-done.29
  289.9 9.7 collective-permute-start.8
  314.4 9.7 collective-permute-start.12
  325.4 7.8 collective-permute-start.14
  340.8 9.7 collective-permute-start.16
  365.3 9.7 collective-permute-start.20
  408.1 6.8 fusion.12
  419.5 9.7 collective-permute-start.24
  435.2 9.7 collective-permute-start.32
  468.9 9.7 collective-permute-start.36
  478.5 91.1 %all-reduce.11.cloned.1.call-done = (f32[16,128]{1,0:T(8,128)}, f32[16,128]{1,0:T(8,128)}, f32[16,128,6]{1,2,0:T(8,128)}, f32[16,6]{1,0:T(8,128)}) async-done(((f32[16,128]{1,0:T(8,128)}, f32[16,128]{1,0:T(8,128)}, f32[16,128,6]{1,2,0:T(8,128)}, f32[16,6]{1,0:T(8,128)}), (f32[16,128]{1,0:T(8,128)}, f32[16,128]{1,0:T(8,128)}, f32[16,128,6]{1,2,0:T(8,128)}, f32[16,6]{1,0:T(8,128)})) %all-reduce.11.cloned.1.call-update) | async-done | bytes 65936
  583.7 9.7 collective-permute-start.40
  631.7 8.9 collective-permute-start.48
  656.9 88.0 %reduce-scatter.3.cloned.1.call-done = f32[1,9,128]{2,1,0:T(8,128)} async-done(((f32[16,9,128]{2,1,0:T(8,128)}), f32[1,9,128]{2,1,0:T(8,128)}) %reduce-scatter.3.cloned.1.call-update) | async-done | bytes 4624 | tf_op jit(solution)/shard_map/reduce_scatter | solution.py:180
  744.8 167.2 %all-reduce.4 = (f32[1,9,128]{2,1,0:T(8,128)S(1)}, f32[1,128]{1,0:T(1,128)}, f32[1,128]{1,0:T(1,128)}, f32[1,128,6]{1,2,0:T(8,128)S(1)}, f32[1,6]{1,0:T(1,128)}) all-reduce(f32[1,9,128]{2,1,0:T(8,128)} %reduce-scatter.3.cloned.1.call-done, f32[1,128]{1,0:T(1,128)S(1)} %get-tuple-element.183, ...), channel_id=1, replica_groups=mesh['gx'=32,'yz'=16] {'gx'}, use_global_device_ids=true, to_apply=%region_5.6 | all-reduce | flops 2182 | bytes 17456 | tf_op jit(solution)/shard_map/psum | solution.py:187
  913.2 152.5 %all-reduce.9.cloned.1.call-done = f32[1,128,128]{2,1,0:T(8,128)} async-done(((f32[1,128,128]{2,1,0:T(8,128)}), f32[1,128,128]{2,1,0:T(8,128)}) %all-reduce.9.cloned.1.call-update) | async-done | bytes 65552 | tf_op jit(solution)/shard_map/psum | solution.py:187
  (240 shorter events, 228.4 us)
Async XLA Ops:
  7.2 386.3 %all-gather.5.cloned.1.call-start = ((), (), s32[]{:S(2)}) async-start(), calls=%async_computation.2 | async-start | bytes 1114112 | tf_op jit(solution)/shard_map/all_gather | solution.py:170
  7.9 561.7 %all-reduce.11.cloned.1.call-start = ((), (), s32[]{:S(2)}) async-start(), calls=%async_computation.6 | async-start | bytes 180224
  8.7 160.9 %collective-permute-start = (f32[1,8,128]{2,1,0:T(8,128)S(1)}, f32[1,8,128]{2,1,0:T(8,128)S(1)}, u32[]{:S(2)}, u32[]{:S(2)}) collective-permute-start(f32[1,8,128]{2,1,0:T(8,128)S(1)} %get-tuple-element.172), channel_id=1, source_target_pairs={{16,0},{32,16},{48,32},{64,48},{80,64},{96,80},{112,96},{128,112},... | collective-permute-start | bytes 12296 | tf_op jit(solution)/shard_map/ppermute | solution.py:24
  23.0 145.8 %collective-permute-start.2 = (f32[1,8,128]{2,1,0:T(8,128)S(1)}, f32[1,8,128]{2,1,0:T(8,128)S(1)}, u32[]{:S(2)}, u32[]{:S(2)}) collective-permute-start(f32[1,8,128]{2,1,0:T(8,128)S(1)} %get-tuple-element.173), channel_id=1, source_target_pairs={{0,16},{16,32},{32,48},{48,64},{64,80},{80,96},{96,112},{112,128},... | collective-permute-start | bytes 12296 | tf_op jit(solution)/shard_map/ppermute | solution.py:21
  25.7 252.0 %collective-permute-start.1 = (f32[3,1,8,128]{3,2,1,0:T(8,128)S(1)}, f32[3,1,8,128]{3,2,1,0:T(8,128)S(1)}, u32[]{:S(2)}, u32[]{:S(2)}) collective-permute-start(f32[3,1,8,128]{3,2,1,0:T(8,128)S(1)} %get-tuple-element.164), channel_id=1, source_target_pairs={{16,0},{32,16},{48,32},{64,48},{80,64},{96,80},{112,96},{128,112},... | collective-permute-start | bytes 36872 | tf_op jit(solution)/shard_map/ppermute | solution.py:24
  35.3 241.6 %collective-permute-start.3 = (f32[3,1,8,128]{3,2,1,0:T(8,128)S(1)}, f32[3,1,8,128]{3,2,1,0:T(8,128)S(1)}, u32[]{:S(2)}, u32[]{:S(2)}) collective-permute-start(f32[3,1,8,128]{3,2,1,0:T(8,128)S(1)} %get-tuple-element.165), channel_id=1, source_target_pairs={{0,16},{16,32},{32,48},{48,64},{64,80},{80,96},{96,112},{112,128},... | collective-permute-start | bytes 36872 | tf_op jit(solution)/shard_map/ppermute | solution.py:21
  38.0 230.1 %collective-permute-start.28 = (f32[3,1,8,128]{3,2,1,0:T(8,128)S(1)}, f32[3,1,8,128]{3,2,1,0:T(8,128)S(1)}, u32[]{:S(2)}, u32[]{:S(2)}) collective-permute-start(f32[3,1,8,128]{3,2,1,0:T(8,128)S(1)} %get-tuple-element.132), channel_id=1, source_target_pairs={{16,0},{32,16},{48,32},{64,48},{80,64},{96,80},{112,96},{128,112},... | collective-permute-start | bytes 36872 | tf_op jit(solution)/shard_map/ppermute | solution.py:24
  169.5 87.6 %collective-permute-start.4 = (f32[4,1,128]{2,1,0:T(1,128)S(1)}, f32[4,1,128]{2,1,0:T(1,128)S(1)}, u32[]{:S(2)}, u32[]{:S(2)}) collective-permute-start(f32[4,1,128]{2,1,0:T(1,128)S(1)} %get-tuple-element.166), channel_id=1, source_target_pairs={{1,0},{2,1},{3,2},{4,3},{5,4},{6,5},{7,6},{8,7},{9,8},{10,9},{11,1... | collective-permute-start | bytes 6152 | tf_op jit(solution)/shard_map/ppermute | solution.py:24
  173.5 85.5 %collective-permute-start.6 = (f32[4,1,128]{2,1,0:T(1,128)S(1)}, f32[4,1,128]{2,1,0:T(1,128)S(1)}, u32[]{:S(2)}, u32[]{:S(2)}) collective-permute-start(f32[4,1,128]{2,1,0:T(1,128)S(1)} %get-tuple-element.167), channel_id=1, source_target_pairs={{0,1},{1,2},{2,3},{3,4},{4,5},{5,6},{6,7},{7,8},{8,9},{9,10},{10,1... | collective-permute-start | bytes 6152 | tf_op jit(solution)/shard_map/ppermute | solution.py:21
  268.9 30.6 %collective-permute-start.30 = (f32[3,4,1,128]{3,2,1,0:T(1,128)S(1)}, f32[3,4,1,128]{3,2,1,0:T(1,128)S(1)}, u32[]{:S(2)}, u32[]{:S(2)}) collective-permute-start(f32[3,4,1,128]{3,2,1,0:T(1,128)S(1)} %get-tuple-element.82), channel_id=1, source_target_pairs={{1,0},{2,1},{3,2},{4,3},{5,4},{6,5},{7,6},{8,7},{9,8},{10,9},{11,1... | collective-permute-start | bytes 18440 | tf_op jit(solution)/shard_map/ppermute | solution.py:24
  271.0 28.6 %collective-permute-start.31 = (f32[3,4,1,128]{3,2,1,0:T(1,128)S(1)}, f32[3,4,1,128]{3,2,1,0:T(1,128)S(1)}, u32[]{:S(2)}, u32[]{:S(2)}) collective-permute-start(f32[3,4,1,128]{3,2,1,0:T(1,128)S(1)} %get-tuple-element.83), channel_id=1, source_target_pairs={{0,1},{1,2},{2,3},{3,4},{4,5},{5,6},{6,7},{7,8},{8,9},{9,10},{10,1... | collective-permute-start | bytes 18440 | tf_op jit(solution)/shard_map/ppermute | solution.py:21
  288.0 12.4 %collective-permute-start.9 = (f32[3,1,8,128]{3,2,1,0:T(8,128)S(1)}, f32[3,1,8,128]{3,2,1,0:T(8,128)S(1)}, u32[]{:S(2)}, u32[]{:S(2)}) collective-permute-start(f32[3,1,8,128]{3,2,1,0:T(8,128)S(1)} %get-tuple-element.156), channel_id=1, source_target_pairs={{0,16},{16,32},{32,48},{48,64},{64,80},{80,96},{96,112},{112,128},... | collective-permute-start | bytes 36872 | tf_op jit(solution)/shard_map/ppermute | solution.py:21
  363.3 11.7 %collective-permute-start.21 = (f32[3,1,8,128]{3,2,1,0:T(8,128)S(1)}, f32[3,1,8,128]{3,2,1,0:T(8,128)S(1)}, u32[]{:S(2)}, u32[]{:S(2)}) collective-permute-start(f32[3,1,8,128]{3,2,1,0:T(8,128)S(1)} %get-tuple-element.134), channel_id=1, source_target_pairs={{0,16},{16,32},{32,48},{48,64},{64,80},{80,96},{96,112},{112,128},... | collective-permute-start | bytes 36872 | tf_op jit(solution)/shard_map/ppermute | solution.py:21
  407.9 248.2 %reduce-scatter.5.cloned.1.call-start = ((), (), s32[]{:S(2)}) async-start(), calls=%async_computation.4 | async-start | bytes 1114112 | tf_op jit(solution)/shard_map/reduce_scatter | solution.py:182
  415.0 329.9 %reduce-scatter.3.cloned.1.call-start = ((), (), s32[]{:S(2)}) async-start(), calls=%async_computation.3 | async-start | bytes 139264 | tf_op jit(solution)/shard_map/reduce_scatter | solution.py:180
  417.5 29.9 %collective-permute-start.25 = (f32[6,1,8,128]{3,2,1,0:T(8,128)S(1)}, f32[6,1,8,128]{3,2,1,0:T(8,128)S(1)}, u32[]{:S(2)}, u32[]{:S(2)}) collective-permute-start(f32[6,1,8,128]{3,2,1,0:T(8,128)S(1)} %get-tuple-element.84), channel_id=1, source_target_pairs={{0,16},{16,32},{32,48},{48,64},{64,80},{80,96},{96,112},{112,128},... | collective-permute-start | bytes 73736 | tf_op jit(solution)/shard_map/ppermute | solution.py:21
  419.5 27.8 %collective-permute-start.24 = (f32[6,1,8,128]{3,2,1,0:T(8,128)S(1)}, f32[6,1,8,128]{3,2,1,0:T(8,128)S(1)}, u32[]{:S(2)}, u32[]{:S(2)}) collective-permute-start(f32[6,1,8,128]{3,2,1,0:T(8,128)S(1)} %get-tuple-element.85), channel_id=1, source_target_pairs={{16,0},{32,16},{48,32},{64,48},{80,64},{96,80},{112,96},{128,112},... | collective-permute-start | bytes 73736 | tf_op jit(solution)/shard_map/ppermute | solution.py:24
  433.3 22.1 %collective-permute-start.33 = (f32[9,1,8,128]{3,2,1,0:T(8,128)S(1)}, f32[9,1,8,128]{3,2,1,0:T(8,128)S(1)}, u32[]{:S(2)}, u32[]{:S(2)}) collective-permute-start(f32[9,1,8,128]{3,2,1,0:T(8,128)S(1)} %get-tuple-element.68), channel_id=1, source_target_pairs={{0,16},{16,32},{32,48},{48,64},{64,80},{80,96},{96,112},{112,128},... | collective-permute-start | bytes 110600 | tf_op jit(solution)/shard_map/ppermute | solution.py:21
  435.2 20.2 %collective-permute-start.32 = (f32[9,1,8,128]{3,2,1,0:T(8,128)S(1)}, f32[9,1,8,128]{3,2,1,0:T(8,128)S(1)}, u32[]{:S(2)}, u32[]{:S(2)}) collective-permute-start(f32[9,1,8,128]{3,2,1,0:T(8,128)S(1)} %get-tuple-element.69), channel_id=1, source_target_pairs={{16,0},{32,16},{48,32},{64,48},{80,64},{96,80},{112,96},{128,112},... | collective-permute-start | bytes 110600 | tf_op jit(solution)/shard_map/ppermute | solution.py:24
  447.1 618.6 %all-reduce.9.cloned.1.call-start = ((), (), s32[]{:S(2)}) async-start(), calls=%async_computation.5 | async-start | bytes 131072 | tf_op jit(solution)/shard_map/psum | solution.py:187
  447.4 16.0 %collective-permute-start.26 = (f32[6,4,1,128]{3,2,1,0:T(1,128)S(1)}, f32[6,4,1,128]{3,2,1,0:T(1,128)S(1)}, u32[]{:S(2)}, u32[]{:S(2)}) collective-permute-start(f32[6,4,1,128]{3,2,1,0:T(1,128)S(1)} %get-tuple-element.66), channel_id=1, source_target_pairs={{1,0},{2,1},{3,2},{4,3},{5,4},{6,5},{7,6},{8,7},{9,8},{10,9},{11,1... | collective-permute-start | bytes 36872 | tf_op jit(solution)/shard_map/ppermute | solution.py:24
  466.9 105.4 %collective-permute-start.37 = (f32[3,1,8,128]{3,2,1,0:T(8,128)S(1)}, f32[3,1,8,128]{3,2,1,0:T(8,128)S(1)}, u32[]{:S(2)}, u32[]{:S(2)}) collective-permute-start(f32[3,1,8,128]{3,2,1,0:T(8,128)S(1)} %get-tuple-element.124), channel_id=1, source_target_pairs={{0,16},{16,32},{32,48},{48,64},{64,80},{80,96},{96,112},{112,128},... | collective-permute-start | bytes 36872 | tf_op jit(solution)/shard_map/ppermute | solution.py:21
  468.9 103.4 %collective-permute-start.36 = (f32[3,1,8,128]{3,2,1,0:T(8,128)S(1)}, f32[3,1,8,128]{3,2,1,0:T(8,128)S(1)}, u32[]{:S(2)}, u32[]{:S(2)}) collective-permute-start(f32[3,1,8,128]{3,2,1,0:T(8,128)S(1)} %get-tuple-element.125), channel_id=1, source_target_pairs={{16,0},{32,16},{48,32},{64,48},{80,64},{96,80},{112,96},{128,112},... | collective-permute-start | bytes 36872 | tf_op jit(solution)/shard_map/ppermute | solution.py:24
  642.0 14.1 %collective-permute-start.50 = (f32[3,4,1,128]{3,2,1,0:T(1,128)S(1)}, f32[3,4,1,128]{3,2,1,0:T(1,128)S(1)}, u32[]{:S(2)}, u32[]{:S(2)}) collective-permute-start(f32[3,4,1,128]{3,2,1,0:T(1,128)S(1)} %get-tuple-element.74), channel_id=1, source_target_pairs={{1,0},{2,1},{3,2},{4,3},{5,4},{6,5},{7,6},{8,7},{9,8},{10,9},{11,1... | collective-permute-start | bytes 18440 | tf_op jit(solution)/shard_map/ppermute | solution.py:24
  (38 other events, 368.6 us)
Sparse Core Ops, SparseCore 0:
  10.1 85.3 all-gather.4
  408.0 161.6 all-reduce.10
  572.5 83.5 reduce-scatter.4
  658.7 86.0 reduce-scatter.2
  747.6 318.0 all-reduce.8
where the time goes:
time: 1080 us; the launch traced here: 1070 us
  waiting for transfers between devices  376 us (35%)
  blocking collectives  356 us (33%)
  starting transfers between devices  262 us (24%)
  matrix products  33.3 us (3%)
  local copies, waits for them, and re-layouts  23.5 us (2%)
  between operations  14.8 us (1%)
    ppermute x26, starting transfers between devices, padded_2(): lax.ppermute(lax.slice_in_dim(block, 0, width, axis=dim), axis, backward)  186 us
    psum x1, blocking collectives, local(): lax.psum((weight_grads[0], weight_grads[1], weight_grads[2], weight_grads...  167 us
    psum x1, waiting for transfers between devices, local(): lax.psum((weight_grads[0], weight_grads[1], weight_grads[2], weight_grads...  152 us
    unnamed x6, waiting for transfers between devices  91.9 us
    reduce_scatter x1, waiting for transfers between devices, local(): lax.psum_scatter(expert_grads[0], 'yz', scatter_dimension=0, tiled=True)  88 us
    ppermute x26, starting transfers between devices, padded_2(): lax.ppermute(lax.slice_in_dim(block, block.shape[dim] - width, None, axis...  75.6 us
    all_gather x1, blocking collectives, local(): lax.all_gather(w_out, 'yz', axis=0, tiled=True)  41.5 us
    all_gather x1, blocking collectives, local(): lax.all_gather(b_out, 'yz', axis=0, tiled=True)  40.8 us
  transfers between devices with their start and end apart: 57, of which 20 were waited for; matrix products, arithmetic and copies ran while one was open for 5% of the time, Pallas kernels for 0%

commit v1 on v0

v1 whole, which is shorter than its diff:
```python
import jax
import jax.numpy as jnp
from jax import lax
from jax.sharding import PartitionSpec as P

SUBSTEPS = 4
STEP = 0.15
SCALE = 0.5
CAP = 2
PREC = lax.Precision.HIGH
AXES = ("gx", "yz")


def permute(value, target):
    n_gx, n_yz = lax.axis_size("gx"), lax.axis_size("yz")
    pairs = []
    for g in range(n_gx):
        for y in range(n_yz):
            to_g, to_y = target(g, y)
            pairs.append((g * n_yz + y, (to_g % n_gx) * n_yz + to_y % n_yz))
    return lax.ppermute(value, AXES, pairs)


def to_partner(value):
    return permute(value, lambda g, y: (g ^ 1, y))


def to_outer(value, chips):
    return permute(value, lambda g, y: (g + 2 * chips if g % 2 == 0 else g - 2 * chips, y))


def packed(pieces):
    return jnp.concatenate([p.reshape(-1, 128) for p in pieces], axis=0)


def unpacked(buffer, shapes):
    pieces, at = [], 0
    for shape in shapes:
        rows = 1
        for n in shape[:-1]:
            rows *= n
        pieces.append(buffer[at : at + rows].reshape(shape))
        at += rows
    return pieces


def swap_y(low_pieces, high_pieces):
    shapes_low = [p.shape for p in low_pieces]
    shapes_high = [p.shape for p in high_pieces]
    below = permute(packed(low_pieces), lambda g, y: (g, y + 1))
    above = permute(packed(high_pieces), lambda g, y: (g, y - 1))
    return unpacked(below, shapes_low), unpacked(above, shapes_high)


def flux_step(values, visc):
    center, own = values[:, 1:-1, 1:-1], visc[1:-1, 1:-1]

    def part(next_value, prev_value, next_visc, prev_visc):
        return (0.5 * (own + next_visc)) * (next_value - center) - (0.5 * (own + prev_visc)) * (
            center - prev_value
        )

    flux = part(values[:, 2:, 1:-1], values[:, :-2, 1:-1], visc[2:, 1:-1], visc[:-2, 1:-1])
    flux = flux + part(values[:, 1:-1, 2:], values[:, 1:-1, :-2], visc[1:-1, 2:], visc[1:-1, :-2])
    flux = flux + part(
        jnp.roll(center, -1, 3), jnp.roll(center, 1, 3), jnp.roll(own, -1, 2), jnp.roll(own, 1, 2)
    )
    return center + STEP * flux


def along_z(values):
    return 0.5 * (jnp.roll(values, -1, -1) - jnp.roll(values, 1, -1))


def slots_of(owners):
    count = owners.shape[0]
    same = owners[:, None] == owners[None, :]
    earlier = jnp.arange(count)[None, :] < jnp.arange(count)[:, None]
    rank = jnp.sum((same & earlier).astype(jnp.int32), axis=1)
    return owners * CAP + rank


def local(velocity, viscosity, cotangent, assignment, w_in, b_in, w_mid, b_mid, w_out, b_out):
    experts = lax.axis_size("yz")
    core = lax.axis_index("gx") % 2
    sign = (1 - 2 * core).astype(jnp.float32)

    def mirror(v, dim):
        return jnp.where(core == 0, v, jnp.flip(v, dim))

    fields = jnp.concatenate([mirror(velocity, 1), mirror(viscosity, 0)[None]], axis=0)
    cot = mirror(cotangent, 1)
    owners = mirror(assignment.reshape(2, 8), 0).reshape(16)
    slot = slots_of(owners)

    (f_low, c_low), (f_high, c_high) = swap_y(
        [fields[:, :, 3:], cot[:, :, 7:]], [fields[:, :, :5], cot[:, :, :1]]
    )
    wide = jnp.concatenate([f_low, fields, f_high], axis=2)
    got = to_partner(packed([wide, cot]))
    partner, c_partner = unpacked(got, [wide.shape, cot.shape])
    chip = jnp.concatenate([wide, jnp.flip(partner, 1)], axis=1)
    near = to_outer(packed([chip[:, :, 1:17], c_partner[:, 0]]), 1)
    far = to_outer(chip[:, 3, 5:13], 2)
    outer, c_outer = unpacked(near, [(4, 4, 16, 128), (3, 8, 128)])
    inner = jnp.flip(to_partner(outer[:, 1:]), 1)
    pad_y = ((0, 0), (0, 0), (1, 1), (0, 0))
    block = jnp.concatenate(
        [
            jnp.pad(far[:, None], ((0, 0), (0, 0), (5, 5), (0, 0))),
            jnp.pad(outer, pad_y),
            chip,
            jnp.pad(inner, pad_y),
        ],
        axis=1,
    )
    state, visc = block[:3], block[3]
    for substep in range(SUBSTEPS):
        state = flux_step(state, visc)
        visc = visc[1:-1, 1:-1]
    own_state = state[:, 1:3, 1:9]
    feature_x = (0.5 * sign) * (state[:, 2:, 1:9] - state[:, :2, 1:9])
    feature_y = 0.5 * (state[:, 1:3, 2:] - state[:, 1:3, :8])
    features = jnp.stack([feature_x, feature_y, along_z(own_state)], axis=1)

    c_x = jnp.concatenate([c_outer[:, None], cot, c_partner[:, 1:]], axis=1)
    c_y = jnp.concatenate([c_low, cot, c_high], axis=2)
    d_x = (0.5 * sign) * (c_x[:, 2:] - c_x[:, :2])
    d_y = 0.5 * (c_y[:, :, 2:] - c_y[:, :, :-2])
    d_z = along_z(cot)
    stress_grad = SCALE * jnp.stack(
        [d_x[0], d_y[1], d_z[2], d_y[0] + d_x[1], d_z[0] + d_x[2], d_z[1] + d_y[2]]
    )

    columns = jnp.concatenate([features.reshape(9, 16, 128), stress_grad.reshape(6, 16, 128)], axis=0)
    by_slot = slot[None, :] == jnp.arange(experts * CAP, dtype=jnp.int32)[:, None]
    source = jnp.sum(jnp.where(by_slot, jnp.arange(16, dtype=jnp.int32)[None, :], 0), axis=1)
    occupied = jnp.any(by_slot, axis=1)
    send = jnp.where(occupied[:, None, None], jnp.transpose(columns, (1, 0, 2))[source], 0.0)
    send = send.reshape(experts, CAP * 15, 128)
    recv = lax.all_to_all(send, "yz", 0, 0, tiled=True).reshape(experts * CAP, 15, 128)

    w1, w2, w3 = w_in[0], w_mid[0], w_out[0]
    x = jnp.transpose(recv[:, :9], (1, 0, 2)).reshape(9, -1)
    sg = jnp.transpose(recv[:, 9:], (1, 0, 2)).reshape(6, -1)

    def dot(a, b, ca, cb):
        return lax.dot_general(a, b, (((ca,), (cb,)), ((), ())), precision=PREC)

    h1 = jnp.tanh(dot(w1, x, 0, 0) + b_in[0][:, None])
    h2 = jnp.tanh(dot(w2, h1, 0, 0) + b_mid[0][:, None])
    stress = dot(w3, h2, 0, 0) + b_out[0][:, None]
    g2 = dot(w3, sg, 1, 0) * (1.0 - h2 * h2)
    g1 = dot(w2, g2, 1, 0) * (1.0 - h1 * h1)
    fg = dot(w1, g1, 1, 0)
    grads = [
        dot(x, g1, 1, 1),
        jnp.sum(g1, axis=1)[None],
        dot(h1, g2, 1, 1),
        jnp.sum(g2, axis=1)[None],
        dot(sg, h2, 1, 1),
        jnp.pad(jnp.sum(sg, axis=1), (0, 122))[None],
    ]

    back = jnp.concatenate([fg, stress], axis=0).reshape(15, experts * CAP, 128)
    back = jnp.transpose(back, (1, 0, 2)).reshape(experts, CAP * 15, 128)
    home = lax.all_to_all(back, "yz", 0, 0, tiled=True).reshape(experts * CAP, 15, 128)
    home = jnp.transpose(home[slot], (1, 0, 2)).reshape(15, 2, 8, 128)

    chips = lax.axis_size("gx") // 2
    vector = jnp.concatenate(grads, axis=0)
    chunk = -(-vector.shape[0] // chips)
    vector = vector + to_partner(vector)
    split = jnp.pad(vector, ((0, chunk * chips - vector.shape[0]), (0, 0))).reshape(chips, chunk, 128)
    groups = [list(range(0, 2 * chips, 2)), list(range(1, 2 * chips, 2))]
    parts = lax.all_to_all(split, "gx", 0, 0, axis_index_groups=groups, tiled=True)
    mine = jnp.sum(parts, axis=0)
    whole = lax.all_to_all(
        jnp.broadcast_to(mine, split.shape), "gx", 0, 0, axis_index_groups=groups, tiled=True
    ).reshape(-1, 128)

    fgrad = home[:9].reshape(3, 3, 2, 8, 128)
    fx, fy, fz = fgrad[:, 0], fgrad[:, 1], fgrad[:, 2]
    tau = home[9:]
    tau_x = jnp.stack([tau[0], tau[3], tau[4]])
    tau_y = jnp.stack([tau[3], tau[1], tau[5]])
    tau_z = jnp.stack([tau[4], tau[5], tau[2]])
    part = cot - along_z(fz)
    (p_low, x_low, y_low, t_low), (p_high, x_high, y_high, t_high) = swap_y(
        [part[:, :, 4:], fx[:, :, 4:], fy[:, :, 3:], tau_y[:, :, 7:]],
        [part[:, :, :4], fx[:, :, :4], fy[:, :, :5], tau_y[:, :, :1]],
    )
    fy_wide = jnp.concatenate([y_low, fy, y_high], axis=2)
    part = jnp.concatenate([p_low, part, p_high], axis=2)
    part = part - 0.5 * (fy_wide[:, :, 2:] - fy_wide[:, :, :-2])
    fx_wide = jnp.concatenate([x_low, fx, x_high], axis=2)
    got = to_partner(packed([part, fx_wide, tau_x]))
    part_other, fx_other, tau_other = unpacked(got, [part.shape, fx_wide.shape, tau_x.shape])
    part_chip = jnp.concatenate([part, jnp.flip(part_other, 1)], axis=1)
    fx_chip = jnp.concatenate([fx_wide, jnp.flip(fx_other, 1)], axis=1)
    half = 0.5 * sign
    zero = jnp.zeros_like(fx_chip[:, :1])
    fx_pad = jnp.concatenate([zero, fx_chip, zero], axis=1)
    adj_chip = part_chip - half * (fx_pad[:, 2:] - fx_pad[:, :-2])
    near = to_outer(packed([adj_chip, fx_chip[:, 3], tau_other[:, 0]]), 1)
    far = to_outer(fx_chip[:, 3, 4:12], 2)
    adj_outer, fx_outer, tau_outer = unpacked(near, [(3, 4, 16, 128), (3, 16, 128), (3, 8, 128)])
    far = jnp.pad(far, ((0, 0), (4, 4), (0, 0)))
    adj_outer = jnp.concatenate(
        [
            adj_outer[:, :1] + half * far[:, None],
            adj_outer[:, 1:3],
            adj_outer[:, 3:] - half * fx_chip[:, :1],
        ],
        axis=1,
    )
    got = to_partner(packed([adj_outer[:, 2:], fx_outer]))
    adj_inner, fx_inner = unpacked(got, [(3, 2, 16, 128), (3, 16, 128)])
    adjoint = jnp.concatenate(
        [
            adj_outer,
            adj_chip[:, :1] + half * fx_outer[:, None],
            adj_chip[:, 1:3],
            adj_chip[:, 3:] - half * fx_inner[:, None],
            jnp.flip(adj_inner, 1),
        ],
        axis=1,
    )
    visc = block[3, 1:-1, 1:-1]
    for substep in range(SUBSTEPS):
        adjoint = flux_step(adjoint, visc)
        visc = visc[1:-1, 1:-1]

    t_x = jnp.concatenate([tau_outer[:, None], tau_x, tau_other[:, 1:]], axis=1)
    t_y = jnp.concatenate([t_low, tau_y, t_high], axis=2)
    predicted = own_state - SCALE * (
        half * (t_x[:, 2:] - t_x[:, :2]) + 0.5 * (t_y[:, :, 2:] - t_y[:, :, :-2]) + along_z(tau_z)
    )
    return (
        mirror(predicted, 1),
        mirror(adjoint, 1),
        whole[None, 0:9],
        whole[None, 9],
        whole[None, 10:138],
        whole[None, 138],
        jnp.transpose(whole[139:145])[None],
        whole[None, 145, :6],
    )


def solution(mesh):
    placed = (
        P(None, "gx", "yz", None),
        P("gx", "yz", None),
        P(None, "gx", "yz", None),
        P(("gx", "yz"), None),
        P("yz", None, None),
        P("yz", None),
        P("yz", None, None),
        P("yz", None),
        P("yz", None, None),
        P("yz", None),
    )
    return jax.shard_map(
        local,
        mesh=mesh,
        in_specs=placed,
        out_specs=(
            P(None, "gx", "yz", None),
            P(None, "gx", "yz", None),
            P("yz", None, None),
            P("yz", None),
            P("yz", None, None),
            P("yz", None),
            P("yz", None, None),
            P("yz", None),
        ),
        check_vma=False,
    )
```

time: 1080 us -> 196 us (0.18)
  the two profiles are of different devices: /device:TPU:24 before, /device:TPU:121 now
where the time goes in v1:
time: 196 us; the launch traced here: 195 us
  starting transfers between devices  92.4 us (47%)
  waiting for transfers between devices  61.6 us (31%)
  local copies, waits for them, and re-layouts  17.7 us (9%)
  matrix products  10.8 us (6%)
  other arithmetic  10.6 us (5%)
  between operations  2.11 us (1%)
    ppermute x13, starting transfers between devices, permute(): return lax.ppermute(value, AXES, pairs)  63.1 us
    ppermute x13, waiting for transfers between devices, permute(): return lax.ppermute(value, AXES, pairs)  26.9 us
    all_to_all x1, waiting for transfers between devices, local(): lax.all_to_all(jnp.broadcast_to(mine, split.shape), 'gx', 0, 0, axis_inde...  13.7 us
    all_to_all x1, waiting for transfers between devices, local(): lax.all_to_all(split, 'gx', 0, 0, axis_index_groups=groups, tiled=True)  12.7 us
    all_to_all x1, starting transfers between devices, local(): lax.all_to_all(back, 'yz', 0, 0, tiled=True).reshape(experts * CAP, 15, 128)  11.7 us
    dot_general x9, matrix products, dot(): return lax.dot_general(a, b, (((ca,), (cb,)), ((), ())), precision=PREC)  10.8 us
    all_to_all x1, starting transfers between devices, local(): lax.all_to_all(split, 'gx', 0, 0, axis_index_groups=groups, tiled=True)  7.23 us
    all_to_all x1, starting transfers between devices, local(): lax.all_to_all(send, 'yz', 0, 0, tiled=True).reshape(experts * CAP, 15, 128)  6.79 us
  transfers between devices with their start and end apart: 17, of which 12 were waited for; matrix products, arithmetic and copies ran while one was open for 7% of the time, Pallas kernels for 0%

profile of v1, /device:TPU:121, one launch (start us, length us, event | category | flops | bytes accessed | tf_op | source)
XLA Modules:
  0.0 195.2 jit_solution(8526184825806712148)
XLA Ops:
  2.3 2.4 %collective-permute-start.1 = (f32[46,128]{1,0:T(8,128)S(1)}, f32[46,128]{1,0:T(8,128)S(1)}, u32[]{:S(2)}, u32[]{:S(2)}) collective-permute-start(f32[46,128]{1,0:T(8,128)S(1)} %pad_maximum_fusion.47), channel_id=1, source_target_pairs={{0,15},{1,0},{2,1},{3,2},{4,3},{5,4},{6,5},{7,6},{8,7},{9,8},{10,9... | collective-permute-start | bytes 70664 | tf_op jit(solution)/shard_map/ppermute | solution.py:21
  4.8 6.8 %collective-permute-start = (f32[46,128]{1,0:T(8,128)S(1)}, f32[46,128]{1,0:T(8,128)S(1)}, u32[]{:S(2)}, u32[]{:S(2)}) collective-permute-start(f32[46,128]{1,0:T(8,128)S(1)} %pad_maximum_fusion.46), channel_id=1, source_target_pairs={{0,1},{1,2},{2,3},{3,4},{4,5},{5,6},{6,7},{7,8},{8,9},{9,10},{10,1... | collective-permute-start | bytes 70664 | tf_op jit(solution)/shard_map/ppermute | solution.py:21
  14.5 3.1 %collective-permute-start.2 = (f32[192,128]{1,0:T(8,128)S(1)}, f32[192,128]{1,0:T(8,128)S(1)}, u32[]{:S(2)}, u32[]{:S(2)}) collective-permute-start(f32[192,128]{1,0:T(8,128)S(1)} %pad_maximum_fusion.21), channel_id=1, source_target_pairs={{0,16},{1,17},{2,18},{3,19},{4,20},{5,21},{6,22},{7,23},{8,24},{9,... | collective-permute-start | bytes 294920 | tf_op jit(solution)/shard_map/ppermute | solution.py:21
  18.6 14.9 %collective-permute-start.5 = (f32[4,8,128]{2,1,0:T(8,128)S(1)}, f32[4,8,128]{2,1,0:T(8,128)S(1)}, u32[]{:S(2)}, u32[]{:S(2)}) collective-permute-start(f32[4,8,128]{2,1,0:T(8,128)S(1)} %slice_bitcast_fusion.12), channel_id=1, source_target_pairs={{0,64},{1,65},{2,66},{3,67},{4,68},{5,69},{6,70},{7,71},{8,72},{9,... | collective-permute-start | bytes 49160 | tf_op jit(solution)/shard_map/ppermute | solution.py:21
  33.6 3.1 %collective-permute-start.3 = (f32[280,128]{1,0:T(8,128)S(1)}, f32[280,128]{1,0:T(8,128)S(1)}, u32[]{:S(2)}, u32[]{:S(2)}) collective-permute-start(f32[280,128]{1,0:T(8,128)S(1)} %pad_maximum_fusion.2), channel_id=1, source_target_pairs={{0,32},{1,33},{2,34},{3,35},{4,36},{5,37},{6,38},{7,39},{8,40},{9,... | collective-permute-start | bytes 430088 | tf_op jit(solution)/shard_map/ppermute | solution.py:21
  37.7 7.8 %collective-permute-done.3 = f32[280,128]{1,0:T(8,128)S(1)} collective-permute-done((f32[280,128]{1,0:T(8,128)S(1)}, f32[280,128]{1,0:T(8,128)S(1)}, u32[]{:S(2)}, u32[]{:S(2)}) %collective-permute-start.3) | collective-permute-done | bytes 143392 | tf_op jit(solution)/shard_map/ppermute | solution.py:21
  45.7 3.7 %collective-permute-start.4 = (f32[4,3,16,128]{3,2,1,0:T(8,128)S(1)}, f32[4,3,16,128]{3,2,1,0:T(8,128)S(1)}, u32[]{:S(2)}, u32[]{:S(2)}) collective-permute-start(f32[4,3,16,128]{3,2,1,0:T(8,128)S(1)} %slice.1262), channel_id=1, source_target_pairs={{0,16},{1,17},{2,18},{3,19},{4,20},{5,21},{6,22},{7,23},{8,24},{9,... | collective-permute-start | bytes 294920 | tf_op jit(solution)/shard_map/ppermute | solution.py:21
  58.2 6.8 %all-to-all-start = ((f32[16,30,128]{2,1,0:T(8,128)}), f32[16,30,128]{2,1,0:T(8,128)S(1)}, u32[]{:S(2)}, u32[]{:S(2)}) async-start(f32[16,30,128]{2,1,0:T(8,128)} %broadcast_select_fusion), calls=%async_computation | async-start | bytes 524288 | tf_op jit(solution)/shard_map/all_to_all | solution.py:141
  67.3 4.6 %all-to-all-done = f32[16,30,128]{2,1,0:T(8,128)S(1)} async-done(((f32[16,30,128]{2,1,0:T(8,128)}), f32[16,30,128]{2,1,0:T(8,128)S(1)}, u32[]{:S(2)}, u32[]{:S(2)}) %all-to-all-start) | async-done | bytes 245792 | tf_op jit(solution)/shard_map/all_to_all | solution.py:141
  77.8 1.9 fusion.262
  83.1 2.8 %collective-permute-start.12 = (f32[146,128]{1,0:T(8,128)S(1)}, f32[146,128]{1,0:T(8,128)S(1)}, u32[]{:S(2)}, u32[]{:S(2)}) collective-permute-start(f32[146,128]{1,0:T(8,128)S(1)} %concatenate.358), channel_id=1, source_target_pairs={{0,16},{1,17},{2,18},{3,19},{4,20},{5,21},{6,22},{7,23},{8,24},{9,... | collective-permute-start | bytes 224264 | tf_op jit(solution)/shard_map/ppermute | solution.py:21
  87.5 7.2 %all-to-all-start.2 = ((f32[16,10,128]{2,1,0:T(8,128)}), f32[16,10,128]{2,1,0:T(8,128)S(1)}, u32[]{:S(2)}, u32[]{:S(2)}) async-start(f32[16,10,128]{2,1,0:T(8,128)} %reshape.435), calls=%async_computation.2 | async-start | bytes 262144 | tf_op jit(solution)/shard_map/all_to_all | solution.py:176
  97.3 12.7 %all-to-all-done.2 = f32[16,10,128]{2,1,0:T(8,128)S(1)} async-done(((f32[16,10,128]{2,1,0:T(8,128)}), f32[16,10,128]{2,1,0:T(8,128)S(1)}, u32[]{:S(2)}, u32[]{:S(2)}) %all-to-all-start.2) | async-done | bytes 81952 | tf_op jit(solution)/shard_map/all_to_all | solution.py:176
  110.6 3.5 %all-to-all-start.3 = ((f32[16,10,128]{2,1,0:T(8,128)}), f32[16,10,128]{2,1,0:T(8,128)S(1)}, u32[]{:S(2)}, u32[]{:S(2)}) async-start(f32[16,10,128]{2,1,0:T(8,128)} %broadcast_in_dim.63), calls=%async_computation.3 | async-start | bytes 262144 | tf_op jit(solution)/shard_map/all_to_all | solution.py:178
  115.1 13.7 %all-to-all-done.3 = f32[16,10,128]{2,1,0:T(8,128)S(1)} async-done(((f32[16,10,128]{2,1,0:T(8,128)}), f32[16,10,128]{2,1,0:T(8,128)S(1)}, u32[]{:S(2)}, u32[]{:S(2)}) %all-to-all-start.3) | async-done | bytes 81952 | tf_op jit(solution)/shard_map/all_to_all | solution.py:178
  128.8 11.7 %all-to-all-start.1 = ((f32[16,30,128]{2,1,0:T(8,128)}), f32[16,30,128]{2,1,0:T(8,128)S(1)}, u32[]{:S(2)}, u32[]{:S(2)}) async-start(f32[16,30,128]{2,1,0:T(8,128)} %reshape.406), calls=%async_computation.1 | async-start | bytes 524288 | tf_op jit(solution)/shard_map/all_to_all | solution.py:167
  143.5 3.8 %all-to-all-done.1 = f32[16,30,128]{2,1,0:T(8,128)S(1)} async-done(((f32[16,30,128]{2,1,0:T(8,128)}), f32[16,30,128]{2,1,0:T(8,128)S(1)}, u32[]{:S(2)}, u32[]{:S(2)}) %all-to-all-start.1) | async-done | bytes 245792 | tf_op jit(solution)/shard_map/all_to_all | solution.py:167
  148.5 4.3 %collective-permute-start.6 = (f32[84,128]{1,0:T(8,128)S(1)}, f32[84,128]{1,0:T(8,128)S(1)}, u32[]{:S(2)}, u32[]{:S(2)}) collective-permute-start(f32[84,128]{1,0:T(8,128)S(1)} %pad_maximum_fusion.28), channel_id=1, source_target_pairs={{0,1},{1,2},{2,3},{3,4},{4,5},{5,6},{6,7},{7,8},{8,9},{9,10},{10,1... | collective-permute-start | bytes 129032 | tf_op jit(solution)/shard_map/ppermute | solution.py:21
  154.8 6.7 %collective-permute-done.7 = f32[84,128]{1,0:T(8,128)S(1)} collective-permute-done((f32[84,128]{1,0:T(8,128)S(1)}, f32[84,128]{1,0:T(8,128)S(1)}, u32[]{:S(2)}, u32[]{:S(2)}) %collective-permute-start.7) | collective-permute-done | bytes 43040 | tf_op jit(solution)/shard_map/ppermute | solution.py:21
  161.6 6.0 %collective-permute-start.8 = (f32[240,128]{1,0:T(8,128)S(1)}, f32[240,128]{1,0:T(8,128)S(1)}, u32[]{:S(2)}, u32[]{:S(2)}) collective-permute-start(f32[240,128]{1,0:T(8,128)S(1)} %pad_maximum_fusion.12), channel_id=1, source_target_pairs={{0,16},{1,17},{2,18},{3,19},{4,20},{5,21},{6,22},{7,23},{8,24},{9,... | collective-permute-start | bytes 368648 | tf_op jit(solution)/shard_map/ppermute | solution.py:21
  168.6 3.0 %collective-permute-start.11 = (f32[3,8,128]{2,1,0:T(8,128)S(1)}, f32[3,8,128]{2,1,0:T(8,128)S(1)}, u32[]{:S(2)}, u32[]{:S(2)}) collective-permute-start(f32[3,8,128]{2,1,0:T(8,128)S(1)} %slice_bitcast_fusion.13), channel_id=1, source_target_pairs={{0,64},{1,65},{2,66},{3,67},{4,68},{5,69},{6,70},{7,71},{8,72},{9,... | collective-permute-start | bytes 36872 | tf_op jit(solution)/shard_map/ppermute | solution.py:21
  171.7 5.6 %collective-permute-start.9 = (f32[264,128]{1,0:T(8,128)S(1)}, f32[264,128]{1,0:T(8,128)S(1)}, u32[]{:S(2)}, u32[]{:S(2)}) collective-permute-start(f32[264,128]{1,0:T(8,128)S(1)} %pad_maximum_fusion.3), channel_id=1, source_target_pairs={{0,32},{1,33},{2,34},{3,35},{4,36},{5,37},{6,38},{7,39},{8,40},{9,... | collective-permute-start | bytes 405512 | tf_op jit(solution)/shard_map/ppermute | solution.py:21
  177.4 8.7 %collective-permute-done.9 = f32[264,128]{1,0:T(8,128)S(1)} collective-permute-done((f32[264,128]{1,0:T(8,128)S(1)}, f32[264,128]{1,0:T(8,128)S(1)}, u32[]{:S(2)}, u32[]{:S(2)}) %collective-permute-start.9) | collective-permute-done | bytes 135200 | tf_op jit(solution)/shard_map/ppermute | solution.py:21
  186.2 5.6 %collective-permute-start.10 = (f32[144,128]{1,0:T(8,128)S(1)}, f32[144,128]{1,0:T(8,128)S(1)}, u32[]{:S(2)}, u32[]{:S(2)}) collective-permute-start(f32[144,128]{1,0:T(8,128)S(1)} %pad_maximum_fusion.24), channel_id=1, source_target_pairs={{0,16},{1,17},{2,18},{3,19},{4,20},{5,21},{6,22},{7,23},{8,24},{9,... | collective-permute-start | bytes 221192 | tf_op jit(solution)/shard_map/ppermute | solution.py:21
  (296 shorter events, 42.7 us)
Async XLA Ops:
  0.6 73.6 %copy-start = (f32[1,128,128]{2,1,0:T(8,128)S(1)}, f32[1,128,128]{2,1,0:T(8,128)}, u32[]{:S(2)}) copy-start(f32[1,128,128]{2,1,0:T(8,128)} %param.16) | copy-start | bytes 196612
  2.3 12.0 %collective-permute-start.1 = (f32[46,128]{1,0:T(8,128)S(1)}, f32[46,128]{1,0:T(8,128)S(1)}, u32[]{:S(2)}, u32[]{:S(2)}) collective-permute-start(f32[46,128]{1,0:T(8,128)S(1)} %pad_maximum_fusion.47), channel_id=1, source_target_pairs={{0,15},{1,0},{2,1},{3,2},{4,3},{5,4},{6,5},{7,6},{8,7},{9,8},{10,9... | collective-permute-start | bytes 70664 | tf_op jit(solution)/shard_map/ppermute | solution.py:21
  4.8 9.6 %collective-permute-start = (f32[46,128]{1,0:T(8,128)S(1)}, f32[46,128]{1,0:T(8,128)S(1)}, u32[]{:S(2)}, u32[]{:S(2)}) collective-permute-start(f32[46,128]{1,0:T(8,128)S(1)} %pad_maximum_fusion.46), channel_id=1, source_target_pairs={{0,1},{1,2},{2,3},{3,4},{4,5},{5,6},{6,7},{7,8},{8,9},{9,10},{10,1... | collective-permute-start | bytes 70664 | tf_op jit(solution)/shard_map/ppermute | solution.py:21
  14.5 4.1 %collective-permute-start.2 = (f32[192,128]{1,0:T(8,128)S(1)}, f32[192,128]{1,0:T(8,128)S(1)}, u32[]{:S(2)}, u32[]{:S(2)}) collective-permute-start(f32[192,128]{1,0:T(8,128)S(1)} %pad_maximum_fusion.21), channel_id=1, source_target_pairs={{0,16},{1,17},{2,18},{3,19},{4,20},{5,21},{6,22},{7,23},{8,24},{9,... | collective-permute-start | bytes 294920 | tf_op jit(solution)/shard_map/ppermute | solution.py:21
  18.6 19.0 %collective-permute-start.5 = (f32[4,8,128]{2,1,0:T(8,128)S(1)}, f32[4,8,128]{2,1,0:T(8,128)S(1)}, u32[]{:S(2)}, u32[]{:S(2)}) collective-permute-start(f32[4,8,128]{2,1,0:T(8,128)S(1)} %slice_bitcast_fusion.12), channel_id=1, source_target_pairs={{0,64},{1,65},{2,66},{3,67},{4,68},{5,69},{6,70},{7,71},{8,72},{9,... | collective-permute-start | bytes 49160 | tf_op jit(solution)/shard_map/ppermute | solution.py:21
  33.6 11.9 %collective-permute-start.3 = (f32[280,128]{1,0:T(8,128)S(1)}, f32[280,128]{1,0:T(8,128)S(1)}, u32[]{:S(2)}, u32[]{:S(2)}) collective-permute-start(f32[280,128]{1,0:T(8,128)S(1)} %pad_maximum_fusion.2), channel_id=1, source_target_pairs={{0,32},{1,33},{2,34},{3,35},{4,36},{5,37},{6,38},{7,39},{8,40},{9,... | collective-permute-start | bytes 430088 | tf_op jit(solution)/shard_map/ppermute | solution.py:21
  45.7 4.7 %collective-permute-start.4 = (f32[4,3,16,128]{3,2,1,0:T(8,128)S(1)}, f32[4,3,16,128]{3,2,1,0:T(8,128)S(1)}, u32[]{:S(2)}, u32[]{:S(2)}) collective-permute-start(f32[4,3,16,128]{3,2,1,0:T(8,128)S(1)} %slice.1262), channel_id=1, source_target_pairs={{0,16},{1,17},{2,18},{3,19},{4,20},{5,21},{6,22},{7,23},{8,24},{9,... | collective-permute-start | bytes 294920 | tf_op jit(solution)/shard_map/ppermute | solution.py:21
  56.4 10.1 %copy-start.9 = (f32[6,12,1]{2,1,0:T(8,128)S(1)}, f32[6,12,1]{2,1,0:T(8,128)}, u32[]{:S(2)}) copy-start(f32[6,12,1]{2,1,0:T(8,128)} %get-tuple-element.163) | copy-start | bytes 868
  56.4 10.1 %copy-start.10 = (f32[6,12,1]{2,1,0:T(8,128)S(1)}, f32[6,12,1]{2,1,0:T(8,128)}, u32[]{:S(2)}) copy-start(f32[6,12,1]{2,1,0:T(8,128)} %get-tuple-element.164) | copy-start | bytes 868
  56.4 10.0 %copy-start.11 = (f32[6,12,127]{2,1,0:T(8,128)S(1)}, f32[6,12,127]{2,1,0:T(8,128)}, u32[]{:S(2)}) copy-start(f32[6,12,127]{2,1,0:T(8,128)} %get-tuple-element.161) | copy-start | bytes 109732
  58.2 13.7 %all-to-all-start = ((f32[16,30,128]{2,1,0:T(8,128)}), f32[16,30,128]{2,1,0:T(8,128)S(1)}, u32[]{:S(2)}, u32[]{:S(2)}) async-start(f32[16,30,128]{2,1,0:T(8,128)} %broadcast_select_fusion), calls=%async_computation | async-start | bytes 524288 | tf_op jit(solution)/shard_map/all_to_all | solution.py:141
  80.8 14.0 %copy-start.28 = (f32[1,6]{1,0:T(1,128)S(1)}, f32[1,6]{1,0:T(1,128)}, u32[]{:S(2)}) copy-start(f32[1,6]{1,0:T(1,128)} %param.19) | copy-start | bytes 76
  83.1 3.7 %collective-permute-start.12 = (f32[146,128]{1,0:T(8,128)S(1)}, f32[146,128]{1,0:T(8,128)S(1)}, u32[]{:S(2)}, u32[]{:S(2)}) collective-permute-start(f32[146,128]{1,0:T(8,128)S(1)} %concatenate.358), channel_id=1, source_target_pairs={{0,16},{1,17},{2,18},{3,19},{4,20},{5,21},{6,22},{7,23},{8,24},{9,... | collective-permute-start | bytes 224264 | tf_op jit(solution)/shard_map/ppermute | solution.py:21
  87.5 22.4 %all-to-all-start.2 = ((f32[16,10,128]{2,1,0:T(8,128)}), f32[16,10,128]{2,1,0:T(8,128)S(1)}, u32[]{:S(2)}, u32[]{:S(2)}) async-start(f32[16,10,128]{2,1,0:T(8,128)} %reshape.435), calls=%async_computation.2 | async-start | bytes 262144 | tf_op jit(solution)/shard_map/all_to_all | solution.py:176
  97.3 43.3 %copy-start.24 = (f32[2,8,1]{2,1,0:T(8,128)S(1)}, f32[2,8,1]{2,1,0:T(8,128)}, u32[]{:S(2)}) copy-start(f32[2,8,1]{2,1,0:T(8,128)} %get-tuple-element.143) | copy-start | bytes 196
  97.3 43.3 %copy-start.25 = (f32[2,8,1]{2,1,0:T(8,128)S(1)}, f32[2,8,1]{2,1,0:T(8,128)}, u32[]{:S(2)}) copy-start(f32[2,8,1]{2,1,0:T(8,128)} %get-tuple-element.144) | copy-start | bytes 196
  110.6 18.2 %all-to-all-start.3 = ((f32[16,10,128]{2,1,0:T(8,128)}), f32[16,10,128]{2,1,0:T(8,128)S(1)}, u32[]{:S(2)}, u32[]{:S(2)}) async-start(f32[16,10,128]{2,1,0:T(8,128)} %broadcast_in_dim.63), calls=%async_computation.3 | async-start | bytes 262144 | tf_op jit(solution)/shard_map/all_to_all | solution.py:178
  128.8 18.5 %all-to-all-start.1 = ((f32[16,30,128]{2,1,0:T(8,128)}), f32[16,30,128]{2,1,0:T(8,128)S(1)}, u32[]{:S(2)}, u32[]{:S(2)}) async-start(f32[16,30,128]{2,1,0:T(8,128)} %reshape.406), calls=%async_computation.1 | async-start | bytes 524288 | tf_op jit(solution)/shard_map/all_to_all | solution.py:167
  148.5 6.2 %collective-permute-start.6 = (f32[84,128]{1,0:T(8,128)S(1)}, f32[84,128]{1,0:T(8,128)S(1)}, u32[]{:S(2)}, u32[]{:S(2)}) collective-permute-start(f32[84,128]{1,0:T(8,128)S(1)} %pad_maximum_fusion.28), channel_id=1, source_target_pairs={{0,1},{1,2},{2,3},{3,4},{4,5},{5,6},{6,7},{7,8},{8,9},{9,10},{10,1... | collective-permute-start | bytes 129032 | tf_op jit(solution)/shard_map/ppermute | solution.py:21
  152.8 8.7 %collective-permute-start.7 = (f32[84,128]{1,0:T(8,128)S(1)}, f32[84,128]{1,0:T(8,128)S(1)}, u32[]{:S(2)}, u32[]{:S(2)}) collective-permute-start(f32[84,128]{1,0:T(8,128)S(1)} %pad_maximum_fusion.29), channel_id=1, source_target_pairs={{0,15},{1,0},{2,1},{3,2},{4,3},{5,4},{6,5},{7,6},{8,7},{9,8},{10,9... | collective-permute-start | bytes 129032 | tf_op jit(solution)/shard_map/ppermute | solution.py:21
  161.6 6.9 %collective-permute-start.8 = (f32[240,128]{1,0:T(8,128)S(1)}, f32[240,128]{1,0:T(8,128)S(1)}, u32[]{:S(2)}, u32[]{:S(2)}) collective-permute-start(f32[240,128]{1,0:T(8,128)S(1)} %pad_maximum_fusion.12), channel_id=1, source_target_pairs={{0,16},{1,17},{2,18},{3,19},{4,20},{5,21},{6,22},{7,23},{8,24},{9,... | collective-permute-start | bytes 368648 | tf_op jit(solution)/shard_map/ppermute | solution.py:21
  168.6 17.5 %collective-permute-start.11 = (f32[3,8,128]{2,1,0:T(8,128)S(1)}, f32[3,8,128]{2,1,0:T(8,128)S(1)}, u32[]{:S(2)}, u32[]{:S(2)}) collective-permute-start(f32[3,8,128]{2,1,0:T(8,128)S(1)} %slice_bitcast_fusion.13), channel_id=1, source_target_pairs={{0,64},{1,65},{2,66},{3,67},{4,68},{5,69},{6,70},{7,71},{8,72},{9,... | collective-permute-start | bytes 36872 | tf_op jit(solution)/shard_map/ppermute | solution.py:21
  171.7 14.4 %collective-permute-start.9 = (f32[264,128]{1,0:T(8,128)S(1)}, f32[264,128]{1,0:T(8,128)S(1)}, u32[]{:S(2)}, u32[]{:S(2)}) collective-permute-start(f32[264,128]{1,0:T(8,128)S(1)} %pad_maximum_fusion.3), channel_id=1, source_target_pairs={{0,32},{1,33},{2,34},{3,35},{4,36},{5,37},{6,38},{7,39},{8,40},{9,... | collective-permute-start | bytes 405512 | tf_op jit(solution)/shard_map/ppermute | solution.py:21
  186.2 6.5 %collective-permute-start.10 = (f32[144,128]{1,0:T(8,128)S(1)}, f32[144,128]{1,0:T(8,128)S(1)}, u32[]{:S(2)}, u32[]{:S(2)}) collective-permute-start(f32[144,128]{1,0:T(8,128)S(1)} %pad_maximum_fusion.24), channel_id=1, source_target_pairs={{0,16},{1,17},{2,18},{3,19},{4,20},{5,21},{6,22},{7,23},{8,24},{9,... | collective-permute-start | bytes 221192 | tf_op jit(solution)/shard_map/ppermute | solution.py:21
  (23 other events, 75.8 us)

commit v2 on v1

--- a/solution.py
+++ b/solution.py
@@ -19,6 +19,10 @@
             to_g, to_y = target(g, y)
             pairs.append((g * n_yz + y, (to_g % n_gx) * n_yz + to_y % n_yz))
     return lax.ppermute(value, AXES, pairs)
+
+
+def exchange(value, axis, groups=None):
+    return lax.all_to_all(value, axis, 0, 0, axis_index_groups=groups, tiled=True)
 
 
 def to_partner(value):
@@ -80,7 +84,7 @@
     return owners * CAP + rank
 
 
-def local(velocity, viscosity, cotangent, assignment, w_in, b_in, w_mid, b_mid, w_out, b_out):
+def step(velocity, viscosity, cotangent, assignment, w_in, b_in, w_mid, b_mid, w_out, b_out):
     experts = lax.axis_size("yz")
     core = lax.axis_index("gx") % 2
     sign = (1 - 2 * core).astype(jnp.float32)
@@ -115,7 +119,7 @@
         axis=1,
     )
     state, visc = block[:3], block[3]
-    for substep in range(SUBSTEPS):
+    for _ in range(SUBSTEPS):
         state = flux_step(state, visc)
         visc = visc[1:-1, 1:-1]
     own_state = state[:, 1:3, 1:9]
@@ -138,7 +142,7 @@
     occupied = jnp.any(by_slot, axis=1)
     send = jnp.where(occupied[:, None, None], jnp.transpose(columns, (1, 0, 2))[source], 0.0)
     send = send.reshape(experts, CAP * 15, 128)
-    recv = lax.all_to_all(send, "yz", 0, 0, tiled=True).reshape(experts * CAP, 15, 128)
+    recv = exchange(send, "yz").reshape(experts * CAP, 15, 128)
 
     w1, w2, w3 = w_in[0], w_mid[0], w_out[0]
     x = jnp.transpose(recv[:, :9], (1, 0, 2)).reshape(9, -1)
@@ -164,7 +168,7 @@
 
     back = jnp.concatenate([fg, stress], axis=0).reshape(15, experts * CAP, 128)
     back = jnp.transpose(back, (1, 0, 2)).reshape(experts, CAP * 15, 128)
-    home = lax.all_to_all(back, "yz", 0, 0, tiled=True).reshape(experts * CAP, 15, 128)
+    home = exchange(back, "yz").reshape(experts * CAP, 15, 128)
     home = jnp.transpose(home[slot], (1, 0, 2)).reshape(15, 2, 8, 128)
 
     chips = lax.axis_size("gx") // 2
@@ -173,11 +177,10 @@
     vector = vector + to_partner(vector)
     split = jnp.pad(vector, ((0, chunk * chips - vector.shape[0]), (0, 0))).reshape(chips, chunk, 128)
     groups = [list(range(0, 2 * chips, 2)), list(range(1, 2 * chips, 2))]
-    parts = lax.all_to_all(split, "gx", 0, 0, axis_index_groups=groups, tiled=True)
+    split, home = lax.optimization_barrier((split, home))
+    parts = exchange(split, "gx", groups)
     mine = jnp.sum(parts, axis=0)
-    whole = lax.all_to_all(
-        jnp.broadcast_to(mine, split.shape), "gx", 0, 0, axis_index_groups=groups, tiled=True
-    ).reshape(-1, 128)
+    whole = exchange(jnp.broadcast_to(mine, split.shape), "gx", groups).reshape(-1, 128)
 
     fgrad = home[:9].reshape(3, 3, 2, 8, 128)
     fx, fy, fz = fgrad[:, 0], fgrad[:, 1], fgrad[:, 2]
@@ -227,7 +230,7 @@
         axis=1,
     )
     visc = block[3, 1:-1, 1:-1]
-    for substep in range(SUBSTEPS):
+    for _ in range(SUBSTEPS):
         adjoint = flux_step(adjoint, visc)
         visc = visc[1:-1, 1:-1]
 
@@ -262,7 +265,7 @@
         P("yz", None),
     )
     return jax.shard_map(
-        local,
+        step,
         mesh=mesh,
         in_specs=placed,
         out_specs=(

time: 196 us -> 180 us (0.918)
  the two profiles are of different devices: /device:TPU:121 before, /device:TPU:24 now
where the time goes in v2:
time: 180 us; the launch traced here: 179 us
  starting transfers between devices  80.3 us (45%)
  waiting for transfers between devices  57.9 us (32%)
  matrix products  14.8 us (8%)
  local copies, waits for them, and re-layouts  13.2 us (7%)
  other arithmetic  11.2 us (6%)
  between operations  2.04 us (1%)
    ppermute x13, starting transfers between devices, permute(): return lax.ppermute(value, AXES, pairs)  54 us
    all_to_all x4, waiting for transfers between devices, exchange(): lax.all_to_all(value, axis, 0, 0, axis_index_groups=groups, tiled=True)  35.5 us
    all_to_all x4, starting transfers between devices, exchange(): lax.all_to_all(value, axis, 0, 0, axis_index_groups=groups, tiled=True)  26.3 us
    ppermute x13, waiting for transfers between devices, permute(): return lax.ppermute(value, AXES, pairs)  22.4 us
    dot_general x9, matrix products, dot(): return lax.dot_general(a, b, (((ca,), (cb,)), ((), ())), precision=PREC)  14.8 us
  transfers between devices with their start and end apart: 17, of which 10 were waited for; matrix products, arithmetic and copies ran while one was open for 8% of the time, Pallas kernels for 0%

profile of v2, /device:TPU:24, one launch (start us, length us, event | category | flops | bytes accessed | tf_op | source)
XLA Modules:
  0.0 179.4 jit_solution(16077336436026367731)
XLA Ops:
  2.3 2.7 %collective-permute-start.1 = (f32[46,128]{1,0:T(8,128)S(1)}, f32[46,128]{1,0:T(8,128)S(1)}, u32[]{:S(2)}, u32[]{:S(2)}) collective-permute-start(f32[46,128]{1,0:T(8,128)S(1)} %pad_maximum_fusion.46), channel_id=1, source_target_pairs={{0,15},{1,0},{2,1},{3,2},{4,3},{5,4},{6,5},{7,6},{8,7},{9,8},{10,9... | collective-permute-start | bytes 70664 | tf_op jit(solution)/shard_map/ppermute | solution.py:21
  5.0 5.3 %collective-permute-start = (f32[46,128]{1,0:T(8,128)S(1)}, f32[46,128]{1,0:T(8,128)S(1)}, u32[]{:S(2)}, u32[]{:S(2)}) collective-permute-start(f32[46,128]{1,0:T(8,128)S(1)} %pad_maximum_fusion.45), channel_id=1, source_target_pairs={{0,1},{1,2},{2,3},{3,4},{4,5},{5,6},{6,7},{7,8},{8,9},{9,10},{10,1... | collective-permute-start | bytes 70664 | tf_op jit(solution)/shard_map/ppermute | solution.py:21
  13.2 1.9 %collective-permute-start.2 = (f32[192,128]{1,0:T(8,128)S(1)}, f32[192,128]{1,0:T(8,128)S(1)}, u32[]{:S(2)}, u32[]{:S(2)}) collective-permute-start(f32[192,128]{1,0:T(8,128)S(1)} %pad_maximum_fusion.21), channel_id=1, source_target_pairs={{0,16},{1,17},{2,18},{3,19},{4,20},{5,21},{6,22},{7,23},{8,24},{9,... | collective-permute-start | bytes 294920 | tf_op jit(solution)/shard_map/ppermute | solution.py:21
  16.5 15.7 %collective-permute-start.5 = (f32[4,8,128]{2,1,0:T(8,128)S(1)}, f32[4,8,128]{2,1,0:T(8,128)S(1)}, u32[]{:S(2)}, u32[]{:S(2)}) collective-permute-start(f32[4,8,128]{2,1,0:T(8,128)S(1)} %slice_bitcast_fusion.12), channel_id=1, source_target_pairs={{0,64},{1,65},{2,66},{3,67},{4,68},{5,69},{6,70},{7,71},{8,72},{9,... | collective-permute-start | bytes 49160 | tf_op jit(solution)/shard_map/ppermute | solution.py:21
  32.3 4.3 %collective-permute-start.3 = (f32[280,128]{1,0:T(8,128)S(1)}, f32[280,128]{1,0:T(8,128)S(1)}, u32[]{:S(2)}, u32[]{:S(2)}) collective-permute-start(f32[280,128]{1,0:T(8,128)S(1)} %pad_maximum_fusion.2), channel_id=1, source_target_pairs={{0,32},{1,33},{2,34},{3,35},{4,36},{5,37},{6,38},{7,39},{8,40},{9,... | collective-permute-start | bytes 430088 | tf_op jit(solution)/shard_map/ppermute | solution.py:21
  37.6 12.2 %collective-permute-done.3 = f32[280,128]{1,0:T(8,128)S(1)} collective-permute-done((f32[280,128]{1,0:T(8,128)S(1)}, f32[280,128]{1,0:T(8,128)S(1)}, u32[]{:S(2)}, u32[]{:S(2)}) %collective-permute-start.3) | collective-permute-done | bytes 143392 | tf_op jit(solution)/shard_map/ppermute | solution.py:21
  49.9 1.9 %collective-permute-start.4 = (f32[4,3,16,128]{3,2,1,0:T(8,128)S(1)}, f32[4,3,16,128]{3,2,1,0:T(8,128)S(1)}, u32[]{:S(2)}, u32[]{:S(2)}) collective-permute-start(f32[4,3,16,128]{3,2,1,0:T(8,128)S(1)} %slice.1241), channel_id=1, source_target_pairs={{0,16},{1,17},{2,18},{3,19},{4,20},{5,21},{6,22},{7,23},{8,24},{9,... | collective-permute-start | bytes 294920 | tf_op jit(solution)/shard_map/ppermute | solution.py:21
  58.5 5.5 %all-to-all-start = ((f32[16,30,128]{2,1,0:T(8,128)}), f32[16,30,128]{2,1,0:T(8,128)S(1)}, u32[]{:S(2)}, u32[]{:S(2)}) async-start(f32[16,30,128]{2,1,0:T(8,128)} %broadcast_select_fusion), calls=%async_computation | async-start | bytes 524288 | tf_op jit(solution)/shard_map/all_to_all | solution.py:25
  65.6 7.0 %all-to-all-done = f32[16,30,128]{2,1,0:T(8,128)S(1)} async-done(((f32[16,30,128]{2,1,0:T(8,128)}), f32[16,30,128]{2,1,0:T(8,128)S(1)}, u32[]{:S(2)}, u32[]{:S(2)}) %all-to-all-start) | async-done | bytes 245792 | tf_op jit(solution)/shard_map/all_to_all | solution.py:25
  73.6 2.5 %fusion.1 = f32[4096,128]{1,0:T(8,128)S(1)} fusion(f32[9,4096]{1,0:T(8,128)S(1)} %bitcast.184, f32[128]{0:T(128)} %bitcast.238, f32[1,9,128]{2,0,1:T(1,128)S(1)} %copy-done.11), kind=kOutput, calls=%fused_computation.6 | convolution fusion | flops 28835840 | bytes 2249728 | tf_op jit(solution)/shard_map/dot_general | solution.py:152
  78.4 2.3 %fusion.264 = (f32[128]{0:T(128)}, f32[4096,128]{1,0:T(8,128)S(1)}) fusion(f32[4096,128]{1,0:T(8,128)S(1)} %fusion, f32[1,128,6]{1,0,2:T(1,128)S(1)} %copy-done.12, f32[32,15,128]{2,1,0:T(8,128)S(1)} %reshape.395), kind=kOutput, calls=%fused_computation.503 | convolution fusion | flops 20971392 | bytes 4328960 | tf_op jit(solution)/shard_map/dot_general | solution.py:152
  85.4 6.2 %all-to-all-start.1 = ((f32[16,30,128]{2,1,0:T(8,128)}), f32[16,30,128]{2,1,0:T(8,128)S(1)}, u32[]{:S(2)}, u32[]{:S(2)}) async-start(f32[16,30,128]{2,1,0:T(8,128)} %reshape.400), calls=%async_computation.1 | async-start | bytes 524288 | tf_op jit(solution)/shard_map/all_to_all | solution.py:25
  92.1 2.3 %fusion.265 = f32[9,128]{1,0:T(8,128)S(1)} fusion(f32[9,4096]{1,0:T(8,128)S(1)} %bitcast.185, f32[4096,128]{1,0:T(8,128)} %copy-done.3), kind=kOutput, calls=%fused_computation.504 | convolution fusion | flops 28311552 | bytes 2249216 | tf_op jit(solution)/shard_map/dot_general | solution.py:152
  101.9 3.4 %collective-permute-start.7 = (f32[84,128]{1,0:T(8,128)S(1)}, f32[84,128]{1,0:T(8,128)S(1)}, u32[]{:S(2)}, u32[]{:S(2)}) collective-permute-start(f32[84,128]{1,0:T(8,128)S(1)} %pad_maximum_fusion.28), channel_id=1, source_target_pairs={{0,1},{1,2},{2,3},{3,4},{4,5},{5,6},{6,7},{7,8},{8,9},{9,10},{10,1... | collective-permute-start | bytes 129032 | tf_op jit(solution)/shard_map/ppermute | solution.py:21
  105.3 2.7 %collective-permute-start.8 = (f32[84,128]{1,0:T(8,128)S(1)}, f32[84,128]{1,0:T(8,128)S(1)}, u32[]{:S(2)}, u32[]{:S(2)}) collective-permute-start(f32[84,128]{1,0:T(8,128)S(1)} %pad_maximum_fusion.29), channel_id=1, source_target_pairs={{0,15},{1,0},{2,1},{3,2},{4,3},{5,4},{6,5},{7,6},{8,7},{9,8},{10,9... | collective-permute-start | bytes 129032 | tf_op jit(solution)/shard_map/ppermute | solution.py:21
  108.0 5.3 %collective-permute-done.8 = f32[84,128]{1,0:T(8,128)S(1)} collective-permute-done((f32[84,128]{1,0:T(8,128)S(1)}, f32[84,128]{1,0:T(8,128)S(1)}, u32[]{:S(2)}, u32[]{:S(2)}) %collective-permute-start.8) | collective-permute-done | bytes 43040 | tf_op jit(solution)/shard_map/ppermute | solution.py:21
  113.5 1.9 %collective-permute-start.9 = (f32[240,128]{1,0:T(8,128)S(1)}, f32[240,128]{1,0:T(8,128)S(1)}, u32[]{:S(2)}, u32[]{:S(2)}) collective-permute-start(f32[240,128]{1,0:T(8,128)S(1)} %pad_maximum_fusion.12), channel_id=1, source_target_pairs={{0,16},{1,17},{2,18},{3,19},{4,20},{5,21},{6,22},{7,23},{8,24},{9,... | collective-permute-start | bytes 368648 | tf_op jit(solution)/shard_map/ppermute | solution.py:21
  116.8 5.3 %collective-permute-start.10 = (f32[264,128]{1,0:T(8,128)S(1)}, f32[264,128]{1,0:T(8,128)S(1)}, u32[]{:S(2)}, u32[]{:S(2)}) collective-permute-start(f32[264,128]{1,0:T(8,128)S(1)} %pad_maximum_fusion.3), channel_id=1, source_target_pairs={{0,32},{1,33},{2,34},{3,35},{4,36},{5,37},{6,38},{7,39},{8,40},{9,... | collective-permute-start | bytes 405512 | tf_op jit(solution)/shard_map/ppermute | solution.py:21
  122.2 5.0 %collective-permute-start.12 = (f32[3,8,128]{2,1,0:T(8,128)S(1)}, f32[3,8,128]{2,1,0:T(8,128)S(1)}, u32[]{:S(2)}, u32[]{:S(2)}) collective-permute-start(f32[3,8,128]{2,1,0:T(8,128)S(1)} %slice_bitcast_fusion.13), channel_id=1, source_target_pairs={{0,64},{1,65},{2,66},{3,67},{4,68},{5,69},{6,70},{7,71},{8,72},{9,... | collective-permute-start | bytes 36872 | tf_op jit(solution)/shard_map/ppermute | solution.py:21
  127.3 11.1 %all-to-all-start.2 = ((f32[16,10,128]{2,1,0:T(8,128)}), f32[16,10,128]{2,1,0:T(8,128)S(1)}, u32[]{:S(2)}, u32[]{:S(2)}) async-start(f32[16,10,128]{2,1,0:T(8,128)} %reshape.398), calls=%async_computation.2 | async-start | bytes 262144 | tf_op jit(solution)/shard_map/all_to_all | solution.py:25
  138.8 1.9 %collective-permute-start.11 = (f32[144,128]{1,0:T(8,128)S(1)}, f32[144,128]{1,0:T(8,128)S(1)}, u32[]{:S(2)}, u32[]{:S(2)}) collective-permute-start(f32[144,128]{1,0:T(8,128)S(1)} %pad_maximum_fusion.24), channel_id=1, source_target_pairs={{0,16},{1,17},{2,18},{3,19},{4,20},{5,21},{6,22},{7,23},{8,24},{9,... | collective-permute-start | bytes 221192 | tf_op jit(solution)/shard_map/ppermute | solution.py:21
  141.4 13.9 %all-to-all-done.2 = f32[16,10,128]{2,1,0:T(8,128)S(1)} async-done(((f32[16,10,128]{2,1,0:T(8,128)}), f32[16,10,128]{2,1,0:T(8,128)S(1)}, u32[]{:S(2)}, u32[]{:S(2)}) %all-to-all-start.2) | async-done | bytes 81952 | tf_op jit(solution)/shard_map/all_to_all | solution.py:25
  156.0 3.5 %all-to-all-start.3 = ((f32[16,10,128]{2,1,0:T(8,128)}), f32[16,10,128]{2,1,0:T(8,128)S(1)}, u32[]{:S(2)}, u32[]{:S(2)}) async-start(f32[16,10,128]{2,1,0:T(8,128)} %broadcast_in_dim.63), calls=%async_computation.3 | async-start | bytes 262144 | tf_op jit(solution)/shard_map/all_to_all | solution.py:25
  161.9 14.6 %all-to-all-done.3 = f32[16,10,128]{2,1,0:T(8,128)S(1)} async-done(((f32[16,10,128]{2,1,0:T(8,128)}), f32[16,10,128]{2,1,0:T(8,128)S(1)}, u32[]{:S(2)}, u32[]{:S(2)}) %all-to-all-start.3) | async-done | bytes 81952 | tf_op jit(solution)/shard_map/all_to_all | solution.py:25
  (278 shorter events, 38.9 us)
Async XLA Ops:
  0.6 75.5 %copy-start = (f32[1,128,128]{2,1,0:T(8,128)S(1)}, f32[1,128,128]{2,1,0:T(8,128)}, u32[]{:S(2)}) copy-start(f32[1,128,128]{2,1,0:T(8,128)} %param.16) | copy-start | bytes 196612
  2.3 10.8 %collective-permute-start.1 = (f32[46,128]{1,0:T(8,128)S(1)}, f32[46,128]{1,0:T(8,128)S(1)}, u32[]{:S(2)}, u32[]{:S(2)}) collective-permute-start(f32[46,128]{1,0:T(8,128)S(1)} %pad_maximum_fusion.46), channel_id=1, source_target_pairs={{0,15},{1,0},{2,1},{3,2},{4,3},{5,4},{6,5},{7,6},{8,7},{9,8},{10,9... | collective-permute-start | bytes 70664 | tf_op jit(solution)/shard_map/ppermute | solution.py:21
  5.0 8.1 %collective-permute-start = (f32[46,128]{1,0:T(8,128)S(1)}, f32[46,128]{1,0:T(8,128)S(1)}, u32[]{:S(2)}, u32[]{:S(2)}) collective-permute-start(f32[46,128]{1,0:T(8,128)S(1)} %pad_maximum_fusion.45), channel_id=1, source_target_pairs={{0,1},{1,2},{2,3},{3,4},{4,5},{5,6},{6,7},{7,8},{8,9},{9,10},{10,1... | collective-permute-start | bytes 70664 | tf_op jit(solution)/shard_map/ppermute | solution.py:21
  13.2 3.2 %collective-permute-start.2 = (f32[192,128]{1,0:T(8,128)S(1)}, f32[192,128]{1,0:T(8,128)S(1)}, u32[]{:S(2)}, u32[]{:S(2)}) collective-permute-start(f32[192,128]{1,0:T(8,128)S(1)} %pad_maximum_fusion.21), channel_id=1, source_target_pairs={{0,16},{1,17},{2,18},{3,19},{4,20},{5,21},{6,22},{7,23},{8,24},{9,... | collective-permute-start | bytes 294920 | tf_op jit(solution)/shard_map/ppermute | solution.py:21
  16.5 21.0 %collective-permute-start.5 = (f32[4,8,128]{2,1,0:T(8,128)S(1)}, f32[4,8,128]{2,1,0:T(8,128)S(1)}, u32[]{:S(2)}, u32[]{:S(2)}) collective-permute-start(f32[4,8,128]{2,1,0:T(8,128)S(1)} %slice_bitcast_fusion.12), channel_id=1, source_target_pairs={{0,64},{1,65},{2,66},{3,67},{4,68},{5,69},{6,70},{7,71},{8,72},{9,... | collective-permute-start | bytes 49160 | tf_op jit(solution)/shard_map/ppermute | solution.py:21
  32.3 17.4 %collective-permute-start.3 = (f32[280,128]{1,0:T(8,128)S(1)}, f32[280,128]{1,0:T(8,128)S(1)}, u32[]{:S(2)}, u32[]{:S(2)}) collective-permute-start(f32[280,128]{1,0:T(8,128)S(1)} %pad_maximum_fusion.2), channel_id=1, source_target_pairs={{0,32},{1,33},{2,34},{3,35},{4,36},{5,37},{6,38},{7,39},{8,40},{9,... | collective-permute-start | bytes 430088 | tf_op jit(solution)/shard_map/ppermute | solution.py:21
  49.9 3.2 %collective-permute-start.4 = (f32[4,3,16,128]{3,2,1,0:T(8,128)S(1)}, f32[4,3,16,128]{3,2,1,0:T(8,128)S(1)}, u32[]{:S(2)}, u32[]{:S(2)}) collective-permute-start(f32[4,3,16,128]{3,2,1,0:T(8,128)S(1)} %slice.1241), channel_id=1, source_target_pairs={{0,16},{1,17},{2,18},{3,19},{4,20},{5,21},{6,22},{7,23},{8,24},{9,... | collective-permute-start | bytes 294920 | tf_op jit(solution)/shard_map/ppermute | solution.py:21
  58.5 14.2 %all-to-all-start = ((f32[16,30,128]{2,1,0:T(8,128)}), f32[16,30,128]{2,1,0:T(8,128)S(1)}, u32[]{:S(2)}, u32[]{:S(2)}) async-start(f32[16,30,128]{2,1,0:T(8,128)} %broadcast_select_fusion), calls=%async_computation | async-start | bytes 524288 | tf_op jit(solution)/shard_map/all_to_all | solution.py:25
  64.8 8.8 %copy-start.11 = (f32[1,9,128]{2,0,1:T(1,128)S(1)}, f32[1,9,128]{2,0,1:T(1,128)}, u32[]{:S(2)}) copy-start(f32[1,9,128]{2,0,1:T(1,128)} %param.14) | copy-start | bytes 13828
  73.3 2.8 %copy-start.16 = (f32[1,128]{1,0:T(1,128)S(1)}, f32[1,128]{1,0:T(1,128)}, u32[]{:S(2)}) copy-start(f32[1,128]{1,0:T(1,128)} %param.17) | copy-start | bytes 1540
  78.4 2.3 %copy-start.17 = (f32[1,6]{1,0:T(1,128)S(1)}, f32[1,6]{1,0:T(1,128)}, u32[]{:S(2)}) copy-start(f32[1,6]{1,0:T(1,128)} %param.19) | copy-start | bytes 76
  80.8 2.5 %copy-start.1 = (f32[4096,128]{1,0:T(8,128)}, f32[4096,128]{1,0:T(8,128)S(1)}, u32[]{:S(2)}) copy-start(f32[4096,128]{1,0:T(8,128)S(1)} %get-tuple-element.220) | copy-start | bytes 6291460
  84.2 7.4 %copy-start.18 = (f32[6]{0:T(128)S(1)}, f32[6]{0:T(128)}, u32[]{:S(2)}) copy-start(f32[6]{0:T(128)} %slice_reduce_fusion) | copy-start | bytes 76
  85.4 15.3 %all-to-all-start.1 = ((f32[16,30,128]{2,1,0:T(8,128)}), f32[16,30,128]{2,1,0:T(8,128)S(1)}, u32[]{:S(2)}, u32[]{:S(2)}) async-start(f32[16,30,128]{2,1,0:T(8,128)} %reshape.400), calls=%async_computation.1 | async-start | bytes 524288 | tf_op jit(solution)/shard_map/all_to_all | solution.py:25
  91.6 2.9 %copy-start.2 = (f32[4096,128]{1,0:T(8,128)S(1)}, f32[4096,128]{1,0:T(8,128)}, u32[]{:S(2)}) copy-start(f32[4096,128]{1,0:T(8,128)} %copy-done.1) | copy-start | bytes 6291460
  96.8 3.2 %collective-permute-start.6 = (f32[146,128]{1,0:T(8,128)S(1)}, f32[146,128]{1,0:T(8,128)S(1)}, u32[]{:S(2)}, u32[]{:S(2)}) collective-permute-start(f32[146,128]{1,0:T(8,128)S(1)} %concatenate.319), channel_id=1, source_target_pairs={{0,16},{1,17},{2,18},{3,19},{4,20},{5,21},{6,22},{7,23},{8,24},{9,... | collective-permute-start | bytes 224264 | tf_op jit(solution)/shard_map/ppermute | solution.py:21
  101.9 6.1 %collective-permute-start.7 = (f32[84,128]{1,0:T(8,128)S(1)}, f32[84,128]{1,0:T(8,128)S(1)}, u32[]{:S(2)}, u32[]{:S(2)}) collective-permute-start(f32[84,128]{1,0:T(8,128)S(1)} %pad_maximum_fusion.28), channel_id=1, source_target_pairs={{0,1},{1,2},{2,3},{3,4},{4,5},{5,6},{6,7},{7,8},{8,9},{9,10},{10,1... | collective-permute-start | bytes 129032 | tf_op jit(solution)/shard_map/ppermute | solution.py:21
  105.3 8.0 %collective-permute-start.8 = (f32[84,128]{1,0:T(8,128)S(1)}, f32[84,128]{1,0:T(8,128)S(1)}, u32[]{:S(2)}, u32[]{:S(2)}) collective-permute-start(f32[84,128]{1,0:T(8,128)S(1)} %pad_maximum_fusion.29), channel_id=1, source_target_pairs={{0,15},{1,0},{2,1},{3,2},{4,3},{5,4},{6,5},{7,6},{8,7},{9,8},{10,9... | collective-permute-start | bytes 129032 | tf_op jit(solution)/shard_map/ppermute | solution.py:21
  113.5 3.2 %collective-permute-start.9 = (f32[240,128]{1,0:T(8,128)S(1)}, f32[240,128]{1,0:T(8,128)S(1)}, u32[]{:S(2)}, u32[]{:S(2)}) collective-permute-start(f32[240,128]{1,0:T(8,128)S(1)} %pad_maximum_fusion.12), channel_id=1, source_target_pairs={{0,16},{1,17},{2,18},{3,19},{4,20},{5,21},{6,22},{7,23},{8,24},{9,... | collective-permute-start | bytes 368648 | tf_op jit(solution)/shard_map/ppermute | solution.py:21
  116.8 21.6 %collective-permute-start.10 = (f32[264,128]{1,0:T(8,128)S(1)}, f32[264,128]{1,0:T(8,128)S(1)}, u32[]{:S(2)}, u32[]{:S(2)}) collective-permute-start(f32[264,128]{1,0:T(8,128)S(1)} %pad_maximum_fusion.3), channel_id=1, source_target_pairs={{0,32},{1,33},{2,34},{3,35},{4,36},{5,37},{6,38},{7,39},{8,40},{9,... | collective-permute-start | bytes 405512 | tf_op jit(solution)/shard_map/ppermute | solution.py:21
  122.2 16.5 %collective-permute-start.12 = (f32[3,8,128]{2,1,0:T(8,128)S(1)}, f32[3,8,128]{2,1,0:T(8,128)S(1)}, u32[]{:S(2)}, u32[]{:S(2)}) collective-permute-start(f32[3,8,128]{2,1,0:T(8,128)S(1)} %slice_bitcast_fusion.13), channel_id=1, source_target_pairs={{0,64},{1,65},{2,66},{3,67},{4,68},{5,69},{6,70},{7,71},{8,72},{9,... | collective-permute-start | bytes 36872 | tf_op jit(solution)/shard_map/ppermute | solution.py:21
  127.3 28.0 %all-to-all-start.2 = ((f32[16,10,128]{2,1,0:T(8,128)}), f32[16,10,128]{2,1,0:T(8,128)S(1)}, u32[]{:S(2)}, u32[]{:S(2)}) async-start(f32[16,10,128]{2,1,0:T(8,128)} %reshape.398), calls=%async_computation.2 | async-start | bytes 262144 | tf_op jit(solution)/shard_map/all_to_all | solution.py:25
  138.8 20.8 %collective-permute-start.11 = (f32[144,128]{1,0:T(8,128)S(1)}, f32[144,128]{1,0:T(8,128)S(1)}, u32[]{:S(2)}, u32[]{:S(2)}) collective-permute-start(f32[144,128]{1,0:T(8,128)S(1)} %pad_maximum_fusion.24), channel_id=1, source_target_pairs={{0,16},{1,17},{2,18},{3,19},{4,20},{5,21},{6,22},{7,23},{8,24},{9,... | collective-permute-start | bytes 221192 | tf_op jit(solution)/shard_map/ppermute | solution.py:21
  156.0 20.6 %all-to-all-start.3 = ((f32[16,10,128]{2,1,0:T(8,128)}), f32[16,10,128]{2,1,0:T(8,128)S(1)}, u32[]{:S(2)}, u32[]{:S(2)}) async-start(f32[16,10,128]{2,1,0:T(8,128)} %broadcast_in_dim.63), calls=%async_computation.3 | async-start | bytes 262144 | tf_op jit(solution)/shard_map/all_to_all | solution.py:25
  (13 other events, 16.1 us)

commit v3 on v2

--- a/solution.py
+++ b/solution.py
@@ -29,8 +29,8 @@
     return permute(value, lambda g, y: (g ^ 1, y))
 
 
-def to_outer(value, chips):
-    return permute(value, lambda g, y: (g + 2 * chips if g % 2 == 0 else g - 2 * chips, y))
+def across(value):
+    return permute(value, lambda g, y: (g - 1 if g % 2 == 0 else g + 1, y))
 
 
 def packed(pieces):
@@ -101,12 +101,14 @@
         [fields[:, :, 3:], cot[:, :, 7:]], [fields[:, :, :5], cot[:, :, :1]]
     )
     wide = jnp.concatenate([f_low, fields, f_high], axis=2)
-    got = to_partner(packed([wide, cot]))
-    partner, c_partner = unpacked(got, [wide.shape, cot.shape])
+    got = across(packed([fields[:, 0], cot[:, 0]]))
+    f_edge, c_edge = unpacked(got, [(4, 8, 128), (3, 8, 128)])
+    got = to_partner(packed([wide, f_edge, cot[:, 1]]))
+    partner, partner_edge, c_partner = unpacked(got, [wide.shape, (4, 8, 128), (3, 8, 128)])
     chip = jnp.concatenate([wide, jnp.flip(partner, 1)], axis=1)
-    near = to_outer(packed([chip[:, :, 1:17], c_partner[:, 0]]), 1)
-    far = to_outer(chip[:, 3, 5:13], 2)
-    outer, c_outer = unpacked(near, [(4, 4, 16, 128), (3, 8, 128)])
+    got = across(packed([chip[:, :, 1:17], partner_edge]))
+    outer, far = unpacked(got, [(4, 4, 16, 128), (4, 8, 128)])
+    outer = jnp.flip(outer, 1)
     inner = jnp.flip(to_partner(outer[:, 1:]), 1)
     pad_y = ((0, 0), (0, 0), (1, 1), (0, 0))
     block = jnp.concatenate(
@@ -127,7 +129,7 @@
     feature_y = 0.5 * (state[:, 1:3, 2:] - state[:, 1:3, :8])
     features = jnp.stack([feature_x, feature_y, along_z(own_state)], axis=1)
 
-    c_x = jnp.concatenate([c_outer[:, None], cot, c_partner[:, 1:]], axis=1)
+    c_x = jnp.concatenate([c_edge[:, None], cot, c_partner[:, None]], axis=1)
     c_y = jnp.concatenate([c_low, cot, c_high], axis=2)
     d_x = (0.5 * sign) * (c_x[:, 2:] - c_x[:, :2])
     d_y = 0.5 * (c_y[:, :, 2:] - c_y[:, :, :-2])
@@ -177,7 +179,6 @@
     vector = vector + to_partner(vector)
     split = jnp.pad(vector, ((0, chunk * chips - vector.shape[0]), (0, 0))).reshape(chips, chunk, 128)
     groups = [list(range(0, 2 * chips, 2)), list(range(1, 2 * chips, 2))]
-    split, home = lax.optimization_barrier((split, home))
     parts = exchange(split, "gx", groups)
     mine = jnp.sum(parts, axis=0)
     whole = exchange(jnp.broadcast_to(mine, split.shape), "gx", groups).reshape(-1, 128)
@@ -197,25 +198,25 @@
     part = jnp.concatenate([p_low, part, p_high], axis=2)
     part = part - 0.5 * (fy_wide[:, :, 2:] - fy_wide[:, :, :-2])
     fx_wide = jnp.concatenate([x_low, fx, x_high], axis=2)
-    got = to_partner(packed([part, fx_wide, tau_x]))
-    part_other, fx_other, tau_other = unpacked(got, [part.shape, fx_wide.shape, tau_x.shape])
+    got = across(packed([fx[:, 0], tau_x[:, 0]]))
+    fx_edge, tau_outer = unpacked(got, [(3, 8, 128), (3, 8, 128)])
+    got = to_partner(packed([part, fx_wide, fx_edge, tau_x[:, 1]]))
+    part_other, fx_other, fx_far, tau_other = unpacked(
+        got, [part.shape, fx_wide.shape, (3, 8, 128), (3, 8, 128)]
+    )
     part_chip = jnp.concatenate([part, jnp.flip(part_other, 1)], axis=1)
     fx_chip = jnp.concatenate([fx_wide, jnp.flip(fx_other, 1)], axis=1)
     half = 0.5 * sign
     zero = jnp.zeros_like(fx_chip[:, :1])
     fx_pad = jnp.concatenate([zero, fx_chip, zero], axis=1)
     adj_chip = part_chip - half * (fx_pad[:, 2:] - fx_pad[:, :-2])
-    near = to_outer(packed([adj_chip, fx_chip[:, 3], tau_other[:, 0]]), 1)
-    far = to_outer(fx_chip[:, 3, 4:12], 2)
-    adj_outer, fx_outer, tau_outer = unpacked(near, [(3, 4, 16, 128), (3, 16, 128), (3, 8, 128)])
-    far = jnp.pad(far, ((0, 0), (4, 4), (0, 0)))
+    last = adj_chip[:, 3] - half * jnp.pad(fx_far, ((0, 0), (4, 4), (0, 0)))
+    send = jnp.concatenate([adj_chip[:, :3], last[:, None]], axis=1)
+    got = across(packed([send, fx_chip[:, 0]]))
+    adj_outer, fx_outer = unpacked(got, [(3, 4, 16, 128), (3, 16, 128)])
+    adj_outer = jnp.flip(adj_outer, 1)
     adj_outer = jnp.concatenate(
-        [
-            adj_outer[:, :1] + half * far[:, None],
-            adj_outer[:, 1:3],
-            adj_outer[:, 3:] - half * fx_chip[:, :1],
-        ],
-        axis=1,
+        [adj_outer[:, :3], adj_outer[:, 3:] - half * fx_chip[:, :1]], axis=1
     )
     got = to_partner(packed([adj_outer[:, 2:], fx_outer]))
     adj_inner, fx_inner = unpacked(got, [(3, 2, 16, 128), (3, 16, 128)])
@@ -234,7 +235,7 @@
         adjoint = flux_step(adjoint, visc)
         visc = visc[1:-1, 1:-1]
 
-    t_x = jnp.concatenate([tau_outer[:, None], tau_x, tau_other[:, 1:]], axis=1)
+    t_x = jnp.concatenate([tau_outer[:, None], tau_x, tau_other[:, None]], axis=1)
     t_y = jnp.concatenate([t_low, tau_y, t_high], axis=2)
     predicted = own_state - SCALE * (
         half * (t_x[:, 2:] - t_x[:, :2]) + 0.5 * (t_y[:, :, 2:] - t_y[:, :, :-2]) + along_z(tau_z)

time: 180 us -> 194 us (1.078)
  the two profiles are of different devices: /device:TPU:24 before, /device:TPU:1 now
where the time goes in v3:
time: 194 us; the launch traced here: 193 us
  starting transfers between devices  84.6 us (44%)
  waiting for transfers between devices  66.7 us (34%)
  local copies, waits for them, and re-layouts  17.7 us (9%)
  matrix products  10.8 us (6%)
  other arithmetic  10.6 us (5%)
  between operations  2.2 us (1%)
    ppermute x13, starting transfers between devices, permute(): return lax.ppermute(value, AXES, pairs)  63.8 us
    all_to_all x4, waiting for transfers between devices, exchange(): lax.all_to_all(value, axis, 0, 0, axis_index_groups=groups, tiled=True)  41.2 us
    ppermute x13, waiting for transfers between devices, permute(): return lax.ppermute(value, AXES, pairs)  25.5 us
    all_to_all x4, starting transfers between devices, exchange(): lax.all_to_all(value, axis, 0, 0, axis_index_groups=groups, tiled=True)  20.9 us
    dot_general x9, matrix products, dot(): return lax.dot_general(a, b, (((ca,), (cb,)), ((), ())), precision=PREC)  10.8 us
    slice x16, local copies, waits for them, and re-layouts, flux_step(): jnp.roll(own, -1, 2)  4.35 us
    unnamed x72, local copies, waits for them, and re-layouts  4.32 us
  transfers between devices with their start and end apart: 17, of which 13 were waited for; matrix products, arithmetic and copies ran while one was open for 7% of the time, Pallas kernels for 0%

profile of v3, /device:TPU:1, one launch (start us, length us, event | category | flops | bytes accessed | tf_op | source)
XLA Modules:
  0.0 192.7 jit_solution(12733386390378042665)
XLA Ops:
  2.3 10.2 %collective-permute-start.2 = (f32[56,128]{1,0:T(8,128)S(1)}, f32[56,128]{1,0:T(8,128)S(1)}, u32[]{:S(2)}, u32[]{:S(2)}) collective-permute-start(f32[56,128]{1,0:T(8,128)S(1)} %pad_maximum_fusion.31), channel_id=1, source_target_pairs={{0,496},{1,497},{2,498},{3,499},{4,500},{5,501},{6,502},{7,503},{8... | collective-permute-start | bytes 86024 | tf_op jit(solution)/shard_map/ppermute | solution.py:21
  12.6 8.7 %collective-permute-start.1 = (f32[46,128]{1,0:T(8,128)S(1)}, f32[46,128]{1,0:T(8,128)S(1)}, u32[]{:S(2)}, u32[]{:S(2)}) collective-permute-start(f32[46,128]{1,0:T(8,128)S(1)} %pad_maximum_fusion.49), channel_id=1, source_target_pairs={{0,15},{1,0},{2,1},{3,2},{4,3},{5,4},{6,5},{7,6},{8,7},{9,8},{10,9... | collective-permute-start | bytes 70664 | tf_op jit(solution)/shard_map/ppermute | solution.py:21
  27.0 2.8 %collective-permute-done = f32[46,128]{1,0:T(8,128)S(1)} collective-permute-done((f32[46,128]{1,0:T(8,128)S(1)}, f32[46,128]{1,0:T(8,128)S(1)}, u32[]{:S(2)}, u32[]{:S(2)}) %collective-permute-start) | collective-permute-done | bytes 23584 | tf_op jit(solution)/shard_map/ppermute | solution.py:21
  30.0 6.3 %collective-permute-start.3 = (f32[200,128]{1,0:T(8,128)S(1)}, f32[200,128]{1,0:T(8,128)S(1)}, u32[]{:S(2)}, u32[]{:S(2)}) collective-permute-start(f32[200,128]{1,0:T(8,128)S(1)} %pad_maximum_fusion.13), channel_id=1, source_target_pairs={{0,16},{1,17},{2,18},{3,19},{4,20},{5,21},{6,22},{7,23},{8,24},{9,... | collective-permute-start | bytes 307208 | tf_op jit(solution)/shard_map/ppermute | solution.py:21
  37.3 2.1 %collective-permute-start.4 = (f32[288,128]{1,0:T(8,128)S(1)}, f32[288,128]{1,0:T(8,128)S(1)}, u32[]{:S(2)}, u32[]{:S(2)}) collective-permute-start(f32[288,128]{1,0:T(8,128)S(1)} %pad_maximum_fusion.2), channel_id=1, source_target_pairs={{0,496},{1,497},{2,498},{3,499},{4,500},{5,501},{6,502},{7,503},{8... | collective-permute-start | bytes 442376 | tf_op jit(solution)/shard_map/ppermute | solution.py:21
  39.6 10.8 %collective-permute-done.4 = f32[288,128]{1,0:T(8,128)S(1)} collective-permute-done((f32[288,128]{1,0:T(8,128)S(1)}, f32[288,128]{1,0:T(8,128)S(1)}, u32[]{:S(2)}, u32[]{:S(2)}) %collective-permute-start.4) | collective-permute-done | bytes 147488 | tf_op jit(solution)/shard_map/ppermute | solution.py:21
  50.4 3.2 %collective-permute-start.5 = (f32[4,3,16,128]{3,2,1,0:T(8,128)S(1)}, f32[4,3,16,128]{3,2,1,0:T(8,128)S(1)}, u32[]{:S(2)}, u32[]{:S(2)}) collective-permute-start(f32[4,3,16,128]{3,2,1,0:T(8,128)S(1)} %slice.1009), channel_id=1, source_target_pairs={{0,16},{1,17},{2,18},{3,19},{4,20},{5,21},{6,22},{7,23},{8,24},{9,... | collective-permute-start | bytes 294920 | tf_op jit(solution)/shard_map/ppermute | solution.py:21
  62.5 4.9 %all-to-all-start = ((f32[16,30,128]{2,1,0:T(8,128)}), f32[16,30,128]{2,1,0:T(8,128)S(1)}, u32[]{:S(2)}, u32[]{:S(2)}) async-start(f32[16,30,128]{2,1,0:T(8,128)} %broadcast_select_fusion), calls=%async_computation | async-start | bytes 524288 | tf_op jit(solution)/shard_map/all_to_all | solution.py:25
  69.7 7.6 %all-to-all-done = f32[16,30,128]{2,1,0:T(8,128)S(1)} async-done(((f32[16,30,128]{2,1,0:T(8,128)}), f32[16,30,128]{2,1,0:T(8,128)S(1)}, u32[]{:S(2)}, u32[]{:S(2)}) %all-to-all-start) | async-done | bytes 245792 | tf_op jit(solution)/shard_map/all_to_all | solution.py:25
  83.1 1.9 fusion.259
  88.5 3.6 %collective-permute-start.12 = (f32[146,128]{1,0:T(8,128)S(1)}, f32[146,128]{1,0:T(8,128)S(1)}, u32[]{:S(2)}, u32[]{:S(2)}) collective-permute-start(f32[146,128]{1,0:T(8,128)S(1)} %concatenate.365), channel_id=1, source_target_pairs={{0,16},{1,17},{2,18},{3,19},{4,20},{5,21},{6,22},{7,23},{8,24},{9,... | collective-permute-start | bytes 224264 | tf_op jit(solution)/shard_map/ppermute | solution.py:21
  93.7 5.8 %all-to-all-start.2 = ((f32[16,10,128]{2,1,0:T(8,128)}), f32[16,10,128]{2,1,0:T(8,128)S(1)}, u32[]{:S(2)}, u32[]{:S(2)}) async-start(f32[16,10,128]{2,1,0:T(8,128)} %reshape.422), calls=%async_computation.2 | async-start | bytes 262144 | tf_op jit(solution)/shard_map/all_to_all | solution.py:25
  102.0 12.7 %all-to-all-done.2 = f32[16,10,128]{2,1,0:T(8,128)S(1)} async-done(((f32[16,10,128]{2,1,0:T(8,128)}), f32[16,10,128]{2,1,0:T(8,128)S(1)}, u32[]{:S(2)}, u32[]{:S(2)}) %all-to-all-start.2) | async-done | bytes 81952 | tf_op jit(solution)/shard_map/all_to_all | solution.py:25
  115.4 4.6 %all-to-all-start.3 = ((f32[16,10,128]{2,1,0:T(8,128)}), f32[16,10,128]{2,1,0:T(8,128)S(1)}, u32[]{:S(2)}, u32[]{:S(2)}) async-start(f32[16,10,128]{2,1,0:T(8,128)} %broadcast_in_dim.63), calls=%async_computation.3 | async-start | bytes 262144 | tf_op jit(solution)/shard_map/all_to_all | solution.py:25
  121.0 14.9 %all-to-all-done.3 = f32[16,10,128]{2,1,0:T(8,128)S(1)} async-done(((f32[16,10,128]{2,1,0:T(8,128)}), f32[16,10,128]{2,1,0:T(8,128)S(1)}, u32[]{:S(2)}, u32[]{:S(2)}) %all-to-all-start.3) | async-done | bytes 81952 | tf_op jit(solution)/shard_map/all_to_all | solution.py:25
  135.8 5.7 %all-to-all-start.1 = ((f32[16,30,128]{2,1,0:T(8,128)}), f32[16,30,128]{2,1,0:T(8,128)S(1)}, u32[]{:S(2)}, u32[]{:S(2)}) async-start(f32[16,30,128]{2,1,0:T(8,128)} %reshape.394), calls=%async_computation.1 | async-start | bytes 524288 | tf_op jit(solution)/shard_map/all_to_all | solution.py:25
  144.5 6.1 %all-to-all-done.1 = f32[16,30,128]{2,1,0:T(8,128)S(1)} async-done(((f32[16,30,128]{2,1,0:T(8,128)}), f32[16,30,128]{2,1,0:T(8,128)S(1)}, u32[]{:S(2)}, u32[]{:S(2)}) %all-to-all-start.1) | async-done | bytes 245792 | tf_op jit(solution)/shard_map/all_to_all | solution.py:25
  151.7 3.8 %collective-permute-start.8 = (f32[48,128]{1,0:T(8,128)S(1)}, f32[48,128]{1,0:T(8,128)S(1)}, u32[]{:S(2)}, u32[]{:S(2)}) collective-permute-start(f32[48,128]{1,0:T(8,128)S(1)} %pad_maximum_fusion.51), channel_id=1, source_target_pairs={{0,496},{1,497},{2,498},{3,499},{4,500},{5,501},{6,502},{7,503},{8... | collective-permute-start | bytes 73736 | tf_op jit(solution)/shard_map/ppermute | solution.py:21
  155.6 2.2 %collective-permute-start.6 = (f32[84,128]{1,0:T(8,128)S(1)}, f32[84,128]{1,0:T(8,128)S(1)}, u32[]{:S(2)}, u32[]{:S(2)}) collective-permute-start(f32[84,128]{1,0:T(8,128)S(1)} %pad_maximum_fusion.29), channel_id=1, source_target_pairs={{0,1},{1,2},{2,3},{3,4},{4,5},{5,6},{6,7},{7,8},{8,9},{9,10},{10,1... | collective-permute-start | bytes 129032 | tf_op jit(solution)/shard_map/ppermute | solution.py:21
  157.9 7.0 %collective-permute-start.7 = (f32[84,128]{1,0:T(8,128)S(1)}, f32[84,128]{1,0:T(8,128)S(1)}, u32[]{:S(2)}, u32[]{:S(2)}) collective-permute-start(f32[84,128]{1,0:T(8,128)S(1)} %pad_maximum_fusion.30), channel_id=1, source_target_pairs={{0,15},{1,0},{2,1},{3,2},{4,3},{5,4},{6,5},{7,6},{8,7},{9,8},{10,9... | collective-permute-start | bytes 129032 | tf_op jit(solution)/shard_map/ppermute | solution.py:21
  166.1 3.7 %collective-permute-start.9 = (f32[240,128]{1,0:T(8,128)S(1)}, f32[240,128]{1,0:T(8,128)S(1)}, u32[]{:S(2)}, u32[]{:S(2)}) collective-permute-start(f32[240,128]{1,0:T(8,128)S(1)} %pad_maximum_fusion.11), channel_id=1, source_target_pairs={{0,16},{1,17},{2,18},{3,19},{4,20},{5,21},{6,22},{7,23},{8,24},{9,... | collective-permute-start | bytes 368648 | tf_op jit(solution)/shard_map/ppermute | solution.py:21
  171.0 5.3 %collective-permute-start.10 = (f32[240,128]{1,0:T(8,128)S(1)}, f32[240,128]{1,0:T(8,128)S(1)}, u32[]{:S(2)}, u32[]{:S(2)}) collective-permute-start(f32[240,128]{1,0:T(8,128)S(1)} %pad_maximum_fusion.12), channel_id=1, source_target_pairs={{0,496},{1,497},{2,498},{3,499},{4,500},{5,501},{6,502},{7,503},{8... | collective-permute-start | bytes 368648 | tf_op jit(solution)/shard_map/ppermute | solution.py:21
  177.0 6.5 %collective-permute-done.10 = f32[240,128]{1,0:T(8,128)S(1)} collective-permute-done((f32[240,128]{1,0:T(8,128)S(1)}, f32[240,128]{1,0:T(8,128)S(1)}, u32[]{:S(2)}, u32[]{:S(2)}) %collective-permute-start.10) | collective-permute-done | bytes 122912 | tf_op jit(solution)/shard_map/ppermute | solution.py:21
  183.7 5.6 %collective-permute-start.11 = (f32[144,128]{1,0:T(8,128)S(1)}, f32[144,128]{1,0:T(8,128)S(1)}, u32[]{:S(2)}, u32[]{:S(2)}) collective-permute-start(f32[144,128]{1,0:T(8,128)S(1)} %pad_maximum_fusion.25), channel_id=1, source_target_pairs={{0,16},{1,17},{2,18},{3,19},{4,20},{5,21},{6,22},{7,23},{8,24},{9,... | collective-permute-start | bytes 221192 | tf_op jit(solution)/shard_map/ppermute | solution.py:21
  (307 shorter events, 44.4 us)
Async XLA Ops:
  0.6 79.0 %copy-start = (f32[1,128,128]{2,1,0:T(8,128)S(1)}, f32[1,128,128]{2,1,0:T(8,128)}, u32[]{:S(2)}) copy-start(f32[1,128,128]{2,1,0:T(8,128)} %param.16) | copy-start | bytes 196612
  2.3 27.6 %collective-permute-start.2 = (f32[56,128]{1,0:T(8,128)S(1)}, f32[56,128]{1,0:T(8,128)S(1)}, u32[]{:S(2)}, u32[]{:S(2)}) collective-permute-start(f32[56,128]{1,0:T(8,128)S(1)} %pad_maximum_fusion.31), channel_id=1, source_target_pairs={{0,496},{1,497},{2,498},{3,499},{4,500},{5,501},{6,502},{7,503},{8... | collective-permute-start | bytes 86024 | tf_op jit(solution)/shard_map/ppermute | solution.py:21
  12.6 14.4 %collective-permute-start.1 = (f32[46,128]{1,0:T(8,128)S(1)}, f32[46,128]{1,0:T(8,128)S(1)}, u32[]{:S(2)}, u32[]{:S(2)}) collective-permute-start(f32[46,128]{1,0:T(8,128)S(1)} %pad_maximum_fusion.49), channel_id=1, source_target_pairs={{0,15},{1,0},{2,1},{3,2},{4,3},{5,4},{6,5},{7,6},{8,7},{9,8},{10,9... | collective-permute-start | bytes 70664 | tf_op jit(solution)/shard_map/ppermute | solution.py:21
  21.3 8.5 %collective-permute-start = (f32[46,128]{1,0:T(8,128)S(1)}, f32[46,128]{1,0:T(8,128)S(1)}, u32[]{:S(2)}, u32[]{:S(2)}) collective-permute-start(f32[46,128]{1,0:T(8,128)S(1)} %pad_maximum_fusion.48), channel_id=1, source_target_pairs={{0,1},{1,2},{2,3},{3,4},{4,5},{5,6},{6,7},{7,8},{8,9},{9,10},{10,1... | collective-permute-start | bytes 70664 | tf_op jit(solution)/shard_map/ppermute | solution.py:21
  30.0 7.2 %collective-permute-start.3 = (f32[200,128]{1,0:T(8,128)S(1)}, f32[200,128]{1,0:T(8,128)S(1)}, u32[]{:S(2)}, u32[]{:S(2)}) collective-permute-start(f32[200,128]{1,0:T(8,128)S(1)} %pad_maximum_fusion.13), channel_id=1, source_target_pairs={{0,16},{1,17},{2,18},{3,19},{4,20},{5,21},{6,22},{7,23},{8,24},{9,... | collective-permute-start | bytes 307208 | tf_op jit(solution)/shard_map/ppermute | solution.py:21
  37.3 13.1 %collective-permute-start.4 = (f32[288,128]{1,0:T(8,128)S(1)}, f32[288,128]{1,0:T(8,128)S(1)}, u32[]{:S(2)}, u32[]{:S(2)}) collective-permute-start(f32[288,128]{1,0:T(8,128)S(1)} %pad_maximum_fusion.2), channel_id=1, source_target_pairs={{0,496},{1,497},{2,498},{3,499},{4,500},{5,501},{6,502},{7,503},{8... | collective-permute-start | bytes 442376 | tf_op jit(solution)/shard_map/ppermute | solution.py:21
  50.4 4.2 %collective-permute-start.5 = (f32[4,3,16,128]{3,2,1,0:T(8,128)S(1)}, f32[4,3,16,128]{3,2,1,0:T(8,128)S(1)}, u32[]{:S(2)}, u32[]{:S(2)}) collective-permute-start(f32[4,3,16,128]{3,2,1,0:T(8,128)S(1)} %slice.1009), channel_id=1, source_target_pairs={{0,16},{1,17},{2,18},{3,19},{4,20},{5,21},{6,22},{7,23},{8,24},{9,... | collective-permute-start | bytes 294920 | tf_op jit(solution)/shard_map/ppermute | solution.py:21
  60.6 8.2 %copy-start.9 = (f32[6,12,1]{2,1,0:T(8,128)S(1)}, f32[6,12,1]{2,1,0:T(8,128)}, u32[]{:S(2)}) copy-start(f32[6,12,1]{2,1,0:T(8,128)} %get-tuple-element.162) | copy-start | bytes 868
  62.5 14.8 %all-to-all-start = ((f32[16,30,128]{2,1,0:T(8,128)}), f32[16,30,128]{2,1,0:T(8,128)S(1)}, u32[]{:S(2)}, u32[]{:S(2)}) async-start(f32[16,30,128]{2,1,0:T(8,128)} %broadcast_select_fusion), calls=%async_computation | async-start | bytes 524288 | tf_op jit(solution)/shard_map/all_to_all | solution.py:25
  68.8 8.9 %copy-start.23 = (f32[1,9,128]{2,0,1:T(1,128)S(1)}, f32[1,9,128]{2,0,1:T(1,128)}, u32[]{:S(2)}) copy-start(f32[1,9,128]{2,0,1:T(1,128)} %param.14) | copy-start | bytes 13828
  68.8 8.9 %copy-start.29 = (f32[1,128]{1,0:T(1,128)S(1)}, f32[1,128]{1,0:T(1,128)}, u32[]{:S(2)}) copy-start(f32[1,128]{1,0:T(1,128)} %param.15) | copy-start | bytes 1540
  86.1 13.4 %copy-start.28 = (f32[1,6]{1,0:T(1,128)S(1)}, f32[1,6]{1,0:T(1,128)}, u32[]{:S(2)}) copy-start(f32[1,6]{1,0:T(1,128)} %param.19) | copy-start | bytes 76
  88.5 4.5 %collective-permute-start.12 = (f32[146,128]{1,0:T(8,128)S(1)}, f32[146,128]{1,0:T(8,128)S(1)}, u32[]{:S(2)}, u32[]{:S(2)}) collective-permute-start(f32[146,128]{1,0:T(8,128)S(1)} %concatenate.365), channel_id=1, source_target_pairs={{0,16},{1,17},{2,18},{3,19},{4,20},{5,21},{6,22},{7,23},{8,24},{9,... | collective-permute-start | bytes 224264 | tf_op jit(solution)/shard_map/ppermute | solution.py:21
  93.7 21.0 %all-to-all-start.2 = ((f32[16,10,128]{2,1,0:T(8,128)}), f32[16,10,128]{2,1,0:T(8,128)S(1)}, u32[]{:S(2)}, u32[]{:S(2)}) async-start(f32[16,10,128]{2,1,0:T(8,128)} %reshape.422), calls=%async_computation.2 | async-start | bytes 262144 | tf_op jit(solution)/shard_map/all_to_all | solution.py:25
  102.0 39.5 %copy-start.24 = (f32[2,8,1]{2,1,0:T(8,128)S(1)}, f32[2,8,1]{2,1,0:T(8,128)}, u32[]{:S(2)}) copy-start(f32[2,8,1]{2,1,0:T(8,128)} %get-tuple-element.142) | copy-start | bytes 196
  102.0 39.5 %copy-start.25 = (f32[2,8,1]{2,1,0:T(8,128)S(1)}, f32[2,8,1]{2,1,0:T(8,128)}, u32[]{:S(2)}) copy-start(f32[2,8,1]{2,1,0:T(8,128)} %get-tuple-element.143) | copy-start | bytes 196
  115.4 20.4 %all-to-all-start.3 = ((f32[16,10,128]{2,1,0:T(8,128)}), f32[16,10,128]{2,1,0:T(8,128)S(1)}, u32[]{:S(2)}, u32[]{:S(2)}) async-start(f32[16,10,128]{2,1,0:T(8,128)} %broadcast_in_dim.63), calls=%async_computation.3 | async-start | bytes 262144 | tf_op jit(solution)/shard_map/all_to_all | solution.py:25
  135.8 14.7 %all-to-all-start.1 = ((f32[16,30,128]{2,1,0:T(8,128)}), f32[16,30,128]{2,1,0:T(8,128)S(1)}, u32[]{:S(2)}, u32[]{:S(2)}) async-start(f32[16,30,128]{2,1,0:T(8,128)} %reshape.394), calls=%async_computation.1 | async-start | bytes 524288 | tf_op jit(solution)/shard_map/all_to_all | solution.py:25
  151.7 13.2 %collective-permute-start.8 = (f32[48,128]{1,0:T(8,128)S(1)}, f32[48,128]{1,0:T(8,128)S(1)}, u32[]{:S(2)}, u32[]{:S(2)}) collective-permute-start(f32[48,128]{1,0:T(8,128)S(1)} %pad_maximum_fusion.51), channel_id=1, source_target_pairs={{0,496},{1,497},{2,498},{3,499},{4,500},{5,501},{6,502},{7,503},{8... | collective-permute-start | bytes 73736 | tf_op jit(solution)/shard_map/ppermute | solution.py:21
  155.6 9.2 %collective-permute-start.6 = (f32[84,128]{1,0:T(8,128)S(1)}, f32[84,128]{1,0:T(8,128)S(1)}, u32[]{:S(2)}, u32[]{:S(2)}) collective-permute-start(f32[84,128]{1,0:T(8,128)S(1)} %pad_maximum_fusion.29), channel_id=1, source_target_pairs={{0,1},{1,2},{2,3},{3,4},{4,5},{5,6},{6,7},{7,8},{8,9},{9,10},{10,1... | collective-permute-start | bytes 129032 | tf_op jit(solution)/shard_map/ppermute | solution.py:21
  157.9 8.1 %collective-permute-start.7 = (f32[84,128]{1,0:T(8,128)S(1)}, f32[84,128]{1,0:T(8,128)S(1)}, u32[]{:S(2)}, u32[]{:S(2)}) collective-permute-start(f32[84,128]{1,0:T(8,128)S(1)} %pad_maximum_fusion.30), channel_id=1, source_target_pairs={{0,15},{1,0},{2,1},{3,2},{4,3},{5,4},{6,5},{7,6},{8,7},{9,8},{10,9... | collective-permute-start | bytes 129032 | tf_op jit(solution)/shard_map/ppermute | solution.py:21
  166.1 4.7 %collective-permute-start.9 = (f32[240,128]{1,0:T(8,128)S(1)}, f32[240,128]{1,0:T(8,128)S(1)}, u32[]{:S(2)}, u32[]{:S(2)}) collective-permute-start(f32[240,128]{1,0:T(8,128)S(1)} %pad_maximum_fusion.11), channel_id=1, source_target_pairs={{0,16},{1,17},{2,18},{3,19},{4,20},{5,21},{6,22},{7,23},{8,24},{9,... | collective-permute-start | bytes 368648 | tf_op jit(solution)/shard_map/ppermute | solution.py:21
  171.0 12.6 %collective-permute-start.10 = (f32[240,128]{1,0:T(8,128)S(1)}, f32[240,128]{1,0:T(8,128)S(1)}, u32[]{:S(2)}, u32[]{:S(2)}) collective-permute-start(f32[240,128]{1,0:T(8,128)S(1)} %pad_maximum_fusion.12), channel_id=1, source_target_pairs={{0,496},{1,497},{2,498},{3,499},{4,500},{5,501},{6,502},{7,503},{8... | collective-permute-start | bytes 368648 | tf_op jit(solution)/shard_map/ppermute | solution.py:21
  183.7 6.5 %collective-permute-start.11 = (f32[144,128]{1,0:T(8,128)S(1)}, f32[144,128]{1,0:T(8,128)S(1)}, u32[]{:S(2)}, u32[]{:S(2)}) collective-permute-start(f32[144,128]{1,0:T(8,128)S(1)} %pad_maximum_fusion.25), channel_id=1, source_target_pairs={{0,16},{1,17},{2,18},{3,19},{4,20},{5,21},{6,22},{7,23},{8,24},{9,... | collective-permute-start | bytes 221192 | tf_op jit(solution)/shard_map/ppermute | solution.py:21
  (23 other events, 70.7 us)

commit v4 on v3

--- a/solution.py
+++ b/solution.py
@@ -1,6 +1,8 @@
 import jax
 import jax.numpy as jnp
 from jax import lax
+from jax.experimental import pallas as pl
+from jax.experimental.pallas import tpu as pltpu
 from jax.sharding import PartitionSpec as P
 
 SUBSTEPS = 4
@@ -9,6 +11,7 @@
 CAP = 2
 PREC = lax.Precision.HIGH
 AXES = ("gx", "yz")
+INTERPRET = False
 
 
 def permute(value, target):
@@ -48,40 +51,152 @@
     return pieces
 
 
-def swap_y(low_pieces, high_pieces):
-    shapes_low = [p.shape for p in low_pieces]
-    shapes_high = [p.shape for p in high_pieces]
-    below = permute(packed(low_pieces), lambda g, y: (g, y + 1))
-    above = permute(packed(high_pieces), lambda g, y: (g, y - 1))
-    return unpacked(below, shapes_low), unpacked(above, shapes_high)
-
-
-def flux_step(values, visc):
-    center, own = values[:, 1:-1, 1:-1], visc[1:-1, 1:-1]
-
-    def part(next_value, prev_value, next_visc, prev_visc):
-        return (0.5 * (own + next_visc)) * (next_value - center) - (0.5 * (own + prev_visc)) * (
-            center - prev_value
+def swap_y(low, high):
+    below = permute(low, lambda g, y: (g, y + 1))
+    above = permute(high, lambda g, y: (g, y - 1))
+    return below, above
+
+
+def spec(space):
+    return pl.BlockSpec(memory_space=space)
+
+
+def call(kernel, outs, scratch, smem_ins, args, smem_outs=()):
+    return pl.pallas_call(
+        kernel,
+        out_shape=[jax.ShapeDtypeStruct(shape, dtype) for shape, dtype in outs],
+        in_specs=[spec(pltpu.SMEM if i in smem_ins else pltpu.VMEM) for i in range(len(args))],
+        out_specs=[spec(pltpu.SMEM if i in smem_outs else pltpu.VMEM) for i in range(len(outs))],
+        scratch_shapes=scratch,
+        interpret=INTERPRET,
+    )(*args)
+
+
+def turned(value, shift, axis):
+    return pltpu.roll(value, shift % value.shape[axis], axis)
+
+
+def coefficients(visc, rows, kx, ky, kz):
+    for i in range(rows):
+        own = visc[i]
+        ky[i] = 0.5 * (own + turned(own, -1, 0))
+        kz[i] = 0.5 * (own + turned(own, -1, 1))
+        if i + 1 < rows:
+            kx[i] = 0.5 * (own + visc[i + 1])
+
+
+def diffusion(state, other, first, last, k_at, kx, ky, kz):
+    for _ in range(SUBSTEPS):
+        first, last = first + 1, last - 1
+        for c in range(3):
+            center = state[c, first]
+            below = kx[k_at + first - 1] * (center - state[c, first - 1])
+            for i in range(first, last + 1):
+                k = k_at + i
+                upper = state[c, i + 1]
+                above = kx[k] * (upper - center)
+                y_flux = ky[k] * (turned(center, -1, 0) - center)
+                z_flux = kz[k] * (turned(center, -1, 1) - center)
+                total = (above - below) + (y_flux - turned(y_flux, 1, 0))
+                total = total + (z_flux - turned(z_flux, 1, 1))
+                other[c, i] = center + STEP * total
+                below, center = above, upper
+        state, other = other, state
+    return state
+
+
+def forward_kernel(
+    core_ref, owner_ref, fields, cot, low, high, edge, mate, near, mate_in,
+    send, own_state, visc, slot_ref,
+    work, spare, kx, ky, kz, c_wide, columns, count,
+):
+    core = core_ref[0]
+    half = 0.5 * (1 - 2 * core).astype(jnp.float32)
+    work[...] = jnp.zeros_like(work)
+    visc[...] = jnp.zeros_like(visc)
+    send[...] = jnp.zeros_like(send)
+    for f in range(4):
+        row = (lambda i, f=f: visc.at[i]) if f == 3 else (lambda i, f=f: work.at[f, i])
+        row(0)[8:16] = near[256 + f * 8 : 264 + f * 8]
+        for i in range(4):
+            at = (f * 4 + i) * 16
+            row(4 - i)[4:20] = near[at : at + 16]
+        for x in range(2):
+            at = f * 2 + x
+            row(5 + x)[3:8] = low[at * 5 : at * 5 + 5]
+            row(5 + x)[8:16] = fields[f, x]
+            row(5 + x)[16:21] = high[at * 5 : at * 5 + 5]
+            row(8 - x)[3:21] = mate[at * 18 : at * 18 + 18]
+        for j in range(3):
+            row(11 - j)[4:20] = mate_in[f, j]
+    coefficients(visc, 12, kx, ky, kz)
+    state = diffusion(work, spare, 0, 11, 0, kx, ky, kz)
+
+    for c in range(3):
+        for x in range(2):
+            at = (c * 3) * 16 + x * 8
+            own = state[c, 5 + x, 8:16]
+            own_state[c, x] = own
+            columns[at : at + 8] = half * (state[c, 6 + x, 8:16] - state[c, 4 + x, 8:16])
+            columns[at + 16 : at + 24] = 0.5 * (state[c, 5 + x, 9:17] - state[c, 5 + x, 7:15])
+            columns[at + 32 : at + 40] = 0.5 * (turned(own, -1, 1) - turned(own, 1, 1))
+    for x in range(2):
+        d = []
+        for c in range(3):
+            own = cot[c, x]
+            c_wide[7:8] = low[40 + c * 2 + x : 41 + c * 2 + x]
+            c_wide[8:16] = own
+            c_wide[16:17] = high[40 + c * 2 + x : 41 + c * 2 + x]
+            if x == 0:
+                d_x = cot[c, 1] - edge[32 + c * 8 : 40 + c * 8]
+            else:
+                d_x = mate[176 + c * 8 : 184 + c * 8] - cot[c, 0]
+            d_y = 0.5 * (c_wide[9:17] - c_wide[7:15])
+            d_z = 0.5 * (turned(own, -1, 1) - turned(own, 1, 1))
+            d.append((half * d_x, d_y, d_z))
+        grads = (
+            d[0][0], d[1][1], d[2][2],
+            d[0][1] + d[1][0], d[0][2] + d[2][0], d[1][2] + d[2][1],
         )
-
-    flux = part(values[:, 2:, 1:-1], values[:, :-2, 1:-1], visc[2:, 1:-1], visc[:-2, 1:-1])
-    flux = flux + part(values[:, 1:-1, 2:], values[:, 1:-1, :-2], visc[1:-1, 2:], visc[1:-1, :-2])
-    flux = flux + part(
-        jnp.roll(center, -1, 3), jnp.roll(center, 1, 3), jnp.roll(own, -1, 2), jnp.roll(own, 1, 2)
-    )
-    return center + STEP * flux
+        for k in range(6):
+            columns[(9 + k) * 16 + x * 8 : (9 + k) * 16 + x * 8 + 8] = SCALE * grads[k]
+    columns[240:256] = jnp.zeros((16, 128), jnp.float32)
+
+    for e in range(count.shape[0]):
+        count[e] = 0
+    for k in range(16):
+        owner = owner_ref[jnp.bitwise_xor(k, core * 8)]
+        rank = count[owner]
+        count[owner] = rank + 1
+        slot = owner * CAP + rank
+        slot_ref[k] = slot
+        send[slot] = columns[pl.ds(k, 16, stride=16)]
+
+
+def adjoint_kernel(core_ref, adjoint, visc, out, work, spare, kx, ky, kz):
+    work[...] = jnp.zeros_like(work)
+    for c in range(3):
+        for i in range(10):
+            work[c, i, 4:20] = adjoint[c, i]
+    coefficients(visc, 12, kx, ky, kz)
+    state = diffusion(work, spare, 0, 9, 1, kx, ky, kz)
+    core = core_ref[0]
+    for c in range(3):
+        for x in range(2):
+            out[c, jnp.bitwise_xor(x, core)] = state[c, 4 + x, 8:16]
+
+
+def finish_kernel(whole, w_in, b_in, w_mid, b_mid, w_out, b_out):
+    w_in[0] = whole[0:9]
+    b_in[...] = whole[9:10]
+    w_mid[0] = whole[10:138]
+    b_mid[...] = whole[138:139]
+    w_out[...] = whole[139:145]
+    b_out[...] = whole[145:146]
 
 
 def along_z(values):
     return 0.5 * (jnp.roll(values, -1, -1) - jnp.roll(values, 1, -1))
-
-
-def slots_of(owners):
-    count = owners.shape[0]
-    same = owners[:, None] == owners[None, :]
-    earlier = jnp.arange(count)[None, :] < jnp.arange(count)[:, None]
-    rank = jnp.sum((same & earlier).astype(jnp.int32), axis=1)
-    return owners * CAP + rank
 
 
 def step(velocity, viscosity, cotangent, assignment, w_in, b_in, w_mid, b_mid, w_out, b_out):
@@ -94,61 +209,44 @@
 
     fields = jnp.concatenate([mirror(velocity, 1), mirror(viscosity, 0)[None]], axis=0)
     cot = mirror(cotangent, 1)
-    owners = mirror(assignment.reshape(2, 8), 0).reshape(16)
-    slot = slots_of(owners)
-
-    (f_low, c_low), (f_high, c_high) = swap_y(
-        [fields[:, :, 3:], cot[:, :, 7:]], [fields[:, :, :5], cot[:, :, :1]]
-    )
+    core_arg = core.astype(jnp.int32).reshape(1)
+
+    edge = across(packed([fields[:, 0], cot[:, 0]]))
+    low, high = swap_y(
+        packed([fields[:, :, 3:], cot[:, :, 7:]]), packed([fields[:, :, :5], cot[:, :, :1]])
+    )
+    f_low, f_high = low[:40].reshape(4, 2, 5, 128), high[:40].reshape(4, 2, 5, 128)
     wide = jnp.concatenate([f_low, fields, f_high], axis=2)
-    got = across(packed([fields[:, 0], cot[:, 0]]))
-    f_edge, c_edge = unpacked(got, [(4, 8, 128), (3, 8, 128)])
-    got = to_partner(packed([wide, f_edge, cot[:, 1]]))
-    partner, partner_edge, c_partner = unpacked(got, [wide.shape, (4, 8, 128), (3, 8, 128)])
+    mate = to_partner(packed([wide, edge[:32], cot[:, 1]]))
+    partner = mate[:144].reshape(4, 2, 18, 128)
     chip = jnp.concatenate([wide, jnp.flip(partner, 1)], axis=1)
-    got = across(packed([chip[:, :, 1:17], partner_edge]))
-    outer, far = unpacked(got, [(4, 4, 16, 128), (4, 8, 128)])
-    outer = jnp.flip(outer, 1)
-    inner = jnp.flip(to_partner(outer[:, 1:]), 1)
-    pad_y = ((0, 0), (0, 0), (1, 1), (0, 0))
-    block = jnp.concatenate(
+    near = across(packed([chip[:, :, 1:17], mate[144:176]]))
+    pass_on = jnp.flip(near[:256].reshape(4, 4, 16, 128)[:, :3], 1)
+    mate_in = to_partner(pass_on)
+    f32, i32 = jnp.float32, jnp.int32
+    wide_rows = [pltpu.VMEM((12, 24, 128), f32)] * 3
+    send, own_state, visc, slot = call(
+        forward_kernel,
         [
-            jnp.pad(far[:, None], ((0, 0), (0, 0), (5, 5), (0, 0))),
-            jnp.pad(outer, pad_y),
-            chip,
-            jnp.pad(inner, pad_y),
+            ((experts * CAP, 16, 128), f32),
+            ((3, 2, 8, 128), f32),
+            ((12, 24, 128), f32),
+            ((16,), i32),
         ],
-        axis=1,
-    )
-    state, visc = block[:3], block[3]
-    for _ in range(SUBSTEPS):
-        state = flux_step(state, visc)
-        visc = visc[1:-1, 1:-1]
-    own_state = state[:, 1:3, 1:9]
-    feature_x = (0.5 * sign) * (state[:, 2:, 1:9] - state[:, :2, 1:9])
-    feature_y = 0.5 * (state[:, 1:3, 2:] - state[:, 1:3, :8])
-    features = jnp.stack([feature_x, feature_y, along_z(own_state)], axis=1)
-
-    c_x = jnp.concatenate([c_edge[:, None], cot, c_partner[:, None]], axis=1)
-    c_y = jnp.concatenate([c_low, cot, c_high], axis=2)
-    d_x = (0.5 * sign) * (c_x[:, 2:] - c_x[:, :2])
-    d_y = 0.5 * (c_y[:, :, 2:] - c_y[:, :, :-2])
-    d_z = along_z(cot)
-    stress_grad = SCALE * jnp.stack(
-        [d_x[0], d_y[1], d_z[2], d_y[0] + d_x[1], d_z[0] + d_x[2], d_z[1] + d_y[2]]
-    )
-
-    columns = jnp.concatenate([features.reshape(9, 16, 128), stress_grad.reshape(6, 16, 128)], axis=0)
-    by_slot = slot[None, :] == jnp.arange(experts * CAP, dtype=jnp.int32)[:, None]
-    source = jnp.sum(jnp.where(by_slot, jnp.arange(16, dtype=jnp.int32)[None, :], 0), axis=1)
-    occupied = jnp.any(by_slot, axis=1)
-    send = jnp.where(occupied[:, None, None], jnp.transpose(columns, (1, 0, 2))[source], 0.0)
-    send = send.reshape(experts, CAP * 15, 128)
-    recv = exchange(send, "yz").reshape(experts * CAP, 15, 128)
+        [pltpu.VMEM((3, 12, 24, 128), f32)] * 2
+        + wide_rows
+        + [pltpu.VMEM((24, 128), f32), pltpu.VMEM((256, 128), f32), pltpu.SMEM((experts,), i32)],
+        (0, 1),
+        (core_arg, assignment.reshape(16), fields, cot, low, high, edge, mate, near, mate_in),
+        smem_outs=(3,),
+    )
+    recv = exchange(send.reshape(experts, CAP * 16, 128), "yz")
+    recv = recv.reshape(experts * CAP, 16, 128)
 
     w1, w2, w3 = w_in[0], w_mid[0], w_out[0]
-    x = jnp.transpose(recv[:, :9], (1, 0, 2)).reshape(9, -1)
-    sg = jnp.transpose(recv[:, 9:], (1, 0, 2)).reshape(6, -1)
+    turn = jnp.transpose(recv, (1, 0, 2)).reshape(16, -1)
+    x = turn[:9]
+    sg = turn[9:15]
 
     def dot(a, b, ca, cb):
         return lax.dot_general(a, b, (((ca,), (cb,)), ((), ())), precision=PREC)
@@ -190,10 +288,13 @@
     tau_y = jnp.stack([tau[3], tau[1], tau[5]])
     tau_z = jnp.stack([tau[4], tau[5], tau[2]])
     part = cot - along_z(fz)
-    (p_low, x_low, y_low, t_low), (p_high, x_high, y_high, t_high) = swap_y(
-        [part[:, :, 4:], fx[:, :, 4:], fy[:, :, 3:], tau_y[:, :, 7:]],
-        [part[:, :, :4], fx[:, :, :4], fy[:, :, :5], tau_y[:, :, :1]],
-    )
+    low, high = swap_y(
+        packed([part[:, :, 4:], fx[:, :, 4:], fy[:, :, 3:], tau_y[:, :, 7:]]),
+        packed([part[:, :, :4], fx[:, :, :4], fy[:, :, :5], tau_y[:, :, :1]]),
+    )
+    rims = [(3, 2, 4, 128), (3, 2, 4, 128), (3, 2, 5, 128), (3, 2, 1, 128)]
+    p_low, x_low, y_low, t_low = unpacked(low, rims)
+    p_high, x_high, y_high, t_high = unpacked(high, rims)
     fy_wide = jnp.concatenate([y_low, fy, y_high], axis=2)
     part = jnp.concatenate([p_low, part, p_high], axis=2)
     part = part - 0.5 * (fy_wide[:, :, 2:] - fy_wide[:, :, :-2])
@@ -230,25 +331,43 @@
         ],
         axis=1,
     )
-    visc = block[3, 1:-1, 1:-1]
-    for _ in range(SUBSTEPS):
-        adjoint = flux_step(adjoint, visc)
-        visc = visc[1:-1, 1:-1]
+    (grad_velocity,) = call(
+        adjoint_kernel,
+        [((3, 2, 8, 128), f32)],
+        [pltpu.VMEM((3, 10, 24, 128), f32)] * 2 + wide_rows,
+        (0,),
+        (core_arg, adjoint, visc),
+    )
 
     t_x = jnp.concatenate([tau_outer[:, None], tau_x, tau_other[:, None]], axis=1)
     t_y = jnp.concatenate([t_low, tau_y, t_high], axis=2)
     predicted = own_state - SCALE * (
         half * (t_x[:, 2:] - t_x[:, :2]) + 0.5 * (t_y[:, :, 2:] - t_y[:, :, :-2]) + along_z(tau_z)
     )
+    results = call(
+        finish_kernel,
+        [
+            ((1, 9, 128), f32),
+            ((1, 128), f32),
+            ((1, 128, 128), f32),
+            ((1, 128), f32),
+            ((6, 128), f32),
+            ((1, 128), f32),
+        ],
+        [],
+        (),
+        (whole,),
+    )
+    g_w_in, g_b_in, g_w_mid, g_b_mid, g_w_out, g_b_out = results
     return (
         mirror(predicted, 1),
-        mirror(adjoint, 1),
-        whole[None, 0:9],
-        whole[None, 9],
-        whole[None, 10:138],
-        whole[None, 138],
-        jnp.transpose(whole[139:145])[None],
-        whole[None, 145, :6],
+        grad_velocity,
+        g_w_in,
+        g_b_in,
+        g_w_mid,
+        g_b_mid,
+        jnp.transpose(g_w_out)[None],
+        g_b_out[:, :6],
     )
 
 

time: 194 us -> 193 us (level)
  blocking collectives: 0 us -> 13.6 us
  waiting for transfers between devices: 66.7 us -> 54.3 us
  Pallas kernels: 0 us -> 11.2 us
  other arithmetic: 10.6 us -> 3.56 us
  local copies, waits for them, and re-layouts: 17.7 us -> 10.7 us
    all_to_all x0 -> x1, blocking collectives: none -> 13.6 us  [exchange(): lax.all_to_all(value, axis, 0, 0, axis_index_groups=groups, tiled=True)]
    pallas_call x0 -> x3, Pallas kernels: none -> 11.2 us  [call(): pl.pallas_call(kernel, out_shape=[jax.ShapeDtypeStruct(shape, dtype) for...]
    all_to_all x4 -> x3, waiting for transfers between devices: 41.2 us -> 31.8 us  [exchange(): lax.all_to_all(value, axis, 0, 0, axis_index_groups=groups, tiled=True)]
    slice x37 -> x9, local copies, waits for them, and re-layouts: 7.09 us -> 0.12 us  [the longest x1 0.05 us: step(): x = turn[:9]]
    ppermute x13, starting transfers between devices: 63.8 us -> 69.1 us  [permute(): return lax.ppermute(value, AXES, pairs)]
    all_to_all x4 -> x3, starting transfers between devices: 20.9 us -> 17.1 us  [exchange(): lax.all_to_all(value, axis, 0, 0, axis_index_groups=groups, tiled=True)]
    ppermute x13, waiting for transfers between devices: 25.5 us -> 22.5 us  [permute(): return lax.ppermute(value, AXES, pairs)]
    mul x13 -> x0, other arithmetic: 2.3 us -> none  [the longest x8 2.09 us: part(): 0.5 * (own + next_visc)]
  transfers between devices with their start and end apart: 17 -> 16, of which waited for: 13 -> 12; matrix products, arithmetic and copies ran while one was open for 7% -> 4% of each run, Pallas kernels for 0% -> 1%
where the time goes in v4:
time: 193 us; the launch traced here: 192 us
  starting transfers between devices  86.2 us (45%)
  waiting for transfers between devices  54.3 us (28%)
  blocking collectives  13.6 us (7%)
  Pallas kernels  11.2 us (6%)
  matrix products  10.8 us (6%)
  local copies, waits for them, and re-layouts  10.7 us (6%)
  other arithmetic  3.56 us (2%)
    ppermute x13, starting transfers between devices, permute(): return lax.ppermute(value, AXES, pairs)  69.1 us
    all_to_all x3, waiting for transfers between devices, exchange(): lax.all_to_all(value, axis, 0, 0, axis_index_groups=groups, tiled=True)  31.8 us
    ppermute x13, waiting for transfers between devices, permute(): return lax.ppermute(value, AXES, pairs)  22.5 us
    all_to_all x3, starting transfers between devices, exchange(): lax.all_to_all(value, axis, 0, 0, axis_index_groups=groups, tiled=True)  17.1 us
    all_to_all x1, blocking collectives, exchange(): lax.all_to_all(value, axis, 0, 0, axis_index_groups=groups, tiled=True)  13.6 us
    pallas_call x3, Pallas kernels, call(): pl.pallas_call(kernel, out_shape=[jax.ShapeDtypeStruct(shape, dtype) for...  11.2 us
    dot_general x9, matrix products, dot(): return lax.dot_general(a, b, (((ca,), (cb,)), ((), ())), precision=PREC)  10.8 us
    unnamed x45, local copies, waits for them, and re-layouts  6.2 us
  transfers between devices with their start and end apart: 16, of which 12 were waited for; matrix products, arithmetic and copies ran while one was open for 4% of the time, Pallas kernels for 1%

profile of v4, /device:TPU:1, one launch (start us, length us, event | category | flops | bytes accessed | tf_op | source)
XLA Modules:
  0.0 192.2 jit_solution(17280310343194455646)
XLA Ops:
  2.4 4.0 %collective-permute-start = (f32[46,128]{1,0:T(8,128)S(1)}, f32[46,128]{1,0:T(8,128)S(1)}, u32[]{:S(2)}, u32[]{:S(2)}) collective-permute-start(f32[46,128]{1,0:T(8,128)S(1)} %pad_maximum_fusion.39), channel_id=1, source_target_pairs={{0,1},{1,2},{2,3},{3,4},{4,5},{5,6},{6,7},{7,8},{8,9},{9,10},{10,1... | collective-permute-start | bytes 70664 | tf_op jit(solution)/shard_map/ppermute | solution.py:24
  6.4 7.4 %collective-permute-start.1 = (f32[46,128]{1,0:T(8,128)S(1)}, f32[46,128]{1,0:T(8,128)S(1)}, u32[]{:S(2)}, u32[]{:S(2)}) collective-permute-start(f32[46,128]{1,0:T(8,128)S(1)} %pad_maximum_fusion.40), channel_id=1, source_target_pairs={{0,15},{1,0},{2,1},{3,2},{4,3},{5,4},{6,5},{7,6},{8,7},{9,8},{10,9... | collective-permute-start | bytes 70664 | tf_op jit(solution)/shard_map/ppermute | solution.py:24
  13.9 9.7 %collective-permute-start.2 = (f32[56,128]{1,0:T(8,128)S(1)}, f32[56,128]{1,0:T(8,128)S(1)}, u32[]{:S(2)}, u32[]{:S(2)}) collective-permute-start(f32[56,128]{1,0:T(8,128)S(1)} %pad_maximum_fusion.26), channel_id=1, source_target_pairs={{0,496},{1,497},{2,498},{3,499},{4,500},{5,501},{6,502},{7,503},{8... | collective-permute-start | bytes 86024 | tf_op jit(solution)/shard_map/ppermute | solution.py:24
  25.2 7.0 %collective-permute-start.3 = (f32[200,128]{1,0:T(8,128)S(1)}, f32[200,128]{1,0:T(8,128)S(1)}, u32[]{:S(2)}, u32[]{:S(2)}) collective-permute-start(f32[200,128]{1,0:T(8,128)S(1)} %pad_maximum_fusion.8), channel_id=1, source_target_pairs={{0,16},{1,17},{2,18},{3,19},{4,20},{5,21},{6,22},{7,23},{8,24},{9,... | collective-permute-start | bytes 307208 | tf_op jit(solution)/shard_map/ppermute | solution.py:24
  33.2 3.1 %collective-permute-start.4 = (f32[288,128]{1,0:T(8,128)S(1)}, f32[288,128]{1,0:T(8,128)S(1)}, u32[]{:S(2)}, u32[]{:S(2)}) collective-permute-start(f32[288,128]{1,0:T(8,128)S(1)} %pad_maximum_fusion.1), channel_id=1, source_target_pairs={{0,496},{1,497},{2,498},{3,499},{4,500},{5,501},{6,502},{7,503},{8... | collective-permute-start | bytes 442376 | tf_op jit(solution)/shard_map/ppermute | solution.py:24
  36.3 9.8 %collective-permute-done.4.near = f32[288,128]{1,0:T(8,128)S(1)} collective-permute-done((f32[288,128]{1,0:T(8,128)S(1)}, f32[288,128]{1,0:T(8,128)S(1)}, u32[]{:S(2)}, u32[]{:S(2)}) %collective-permute-start.4) | collective-permute-done | bytes 147488 | tf_op jit(solution)/shard_map/ppermute | solution.py:24
  46.2 6.6 %collective-permute-start.5 = (f32[4,3,16,128]{3,2,1,0:T(8,128)S(1)}, f32[4,3,16,128]{3,2,1,0:T(8,128)S(1)}, u32[]{:S(2)}, u32[]{:S(2)}) collective-permute-start(f32[4,3,16,128]{3,2,1,0:T(8,128)S(1)} %rev.38), channel_id=1, source_target_pairs={{0,16},{1,17},{2,18},{3,19},{4,20},{5,21},{6,22},{7,23},{8,24},{9,... | collective-permute-start | bytes 294920 | tf_op jit(solution)/shard_map/ppermute | solution.py:24
  54.3 6.4 %shard_map.161 = (f32[32,16,128]{2,1,0:T(8,128)}, f32[3,2,8,128]{3,2,1,0:T(8,128)}, f32[12,24,128]{2,1,0:T(8,128)}, s32[16]{0:T(128)}) custom-call(s32[1]{0:T(128)} %bitcast.core_ref, s32[16]{0:T(128)} %bitcast.197, f32[4,2,8,128]{3,2,1,0:T(8,128)} %pad_maximum_fusion.21.fields, f32[3,2,8,128]{3,2,1,0:T(8,128)} %copy-done.4, f32[46,128]{1,0:T(8,128)} %copy-done.9, ...), custom_call_target="tpu_custom_call" | custom-call | tf_op jit(solution)/shard_map/pallas_call | solution.py:65
  60.8 13.6 %all_to_all.20 = f32[16,32,128]{2,1,0:T(8,128)S(1)} all-to-all(f32[16,32,128]{2,1,0:T(8,128)} %bitcast.161), channel_id=1, replica_groups=mesh['gx'=32,'yz'=16] {'yz'}, dimensions={0} | all-to-all | bytes 524288 | tf_op jit(solution)/shard_map/all_to_all | solution.py:28
  85.6 3.6 %collective-permute-start.12 = (f32[146,128]{1,0:T(8,128)S(1)}, f32[146,128]{1,0:T(8,128)S(1)}, u32[]{:S(2)}, u32[]{:S(2)}) collective-permute-start(f32[146,128]{1,0:T(8,128)S(1)} %concatenate.137), channel_id=1, source_target_pairs={{0,16},{1,17},{2,18},{3,19},{4,20},{5,21},{6,22},{7,23},{8,24},{9,... | collective-permute-start | bytes 224264 | tf_op jit(solution)/shard_map/ppermute | solution.py:24
  90.6 6.9 %all-to-all-start.2 = ((f32[16,10,128]{2,1,0:T(8,128)}), f32[16,10,128]{2,1,0:T(8,128)S(1)}, u32[]{:S(2)}, u32[]{:S(2)}) async-start(f32[16,10,128]{2,1,0:T(8,128)} %reshape.238), calls=%async_computation.2 | async-start | bytes 262144 | tf_op jit(solution)/shard_map/all_to_all | solution.py:28
  100.0 12.7 %all-to-all-done.2 = f32[16,10,128]{2,1,0:T(8,128)S(1)} async-done(((f32[16,10,128]{2,1,0:T(8,128)}), f32[16,10,128]{2,1,0:T(8,128)S(1)}, u32[]{:S(2)}, u32[]{:S(2)}) %all-to-all-start.2) | async-done | bytes 81952 | tf_op jit(solution)/shard_map/all_to_all | solution.py:28
  113.4 4.6 %all-to-all-start.3 = ((f32[16,10,128]{2,1,0:T(8,128)}), f32[16,10,128]{2,1,0:T(8,128)S(1)}, u32[]{:S(2)}, u32[]{:S(2)}) async-start(f32[16,10,128]{2,1,0:T(8,128)} %broadcast_in_dim.34), calls=%async_computation.3 | async-start | bytes 262144 | tf_op jit(solution)/shard_map/all_to_all | solution.py:28
  119.0 14.9 %all-to-all-done.3 = f32[16,10,128]{2,1,0:T(8,128)S(1)} async-done(((f32[16,10,128]{2,1,0:T(8,128)}), f32[16,10,128]{2,1,0:T(8,128)S(1)}, u32[]{:S(2)}, u32[]{:S(2)}) %all-to-all-start.3) | async-done | bytes 81952 | tf_op jit(solution)/shard_map/all_to_all | solution.py:28
  133.9 5.6 %all-to-all-start.1 = ((f32[16,30,128]{2,1,0:T(8,128)}), f32[16,30,128]{2,1,0:T(8,128)S(1)}, u32[]{:S(2)}, u32[]{:S(2)}) async-start(f32[16,30,128]{2,1,0:T(8,128)} %reshape.210), calls=%async_computation.1 | async-start | bytes 524288 | tf_op jit(solution)/shard_map/all_to_all | solution.py:28
  144.3 4.2 %all-to-all-done.1 = f32[16,30,128]{2,1,0:T(8,128)S(1)} async-done(((f32[16,30,128]{2,1,0:T(8,128)}), f32[16,30,128]{2,1,0:T(8,128)S(1)}, u32[]{:S(2)}, u32[]{:S(2)}) %all-to-all-start.1) | async-done | bytes 245792 | tf_op jit(solution)/shard_map/all_to_all | solution.py:28
  149.6 3.8 %collective-permute-start.8 = (f32[48,128]{1,0:T(8,128)S(1)}, f32[48,128]{1,0:T(8,128)S(1)}, u32[]{:S(2)}, u32[]{:S(2)}) collective-permute-start(f32[48,128]{1,0:T(8,128)S(1)} %pad_maximum_fusion.42), channel_id=1, source_target_pairs={{0,496},{1,497},{2,498},{3,499},{4,500},{5,501},{6,502},{7,503},{8... | collective-permute-start | bytes 73736 | tf_op jit(solution)/shard_map/ppermute | solution.py:24
  153.5 2.2 %collective-permute-start.6 = (f32[84,128]{1,0:T(8,128)S(1)}, f32[84,128]{1,0:T(8,128)S(1)}, u32[]{:S(2)}, u32[]{:S(2)}) collective-permute-start(f32[84,128]{1,0:T(8,128)S(1)} %pad_maximum_fusion.24), channel_id=1, source_target_pairs={{0,1},{1,2},{2,3},{3,4},{4,5},{5,6},{6,7},{7,8},{8,9},{9,10},{10,1... | collective-permute-start | bytes 129032 | tf_op jit(solution)/shard_map/ppermute | solution.py:24
  155.8 7.0 %collective-permute-start.7 = (f32[84,128]{1,0:T(8,128)S(1)}, f32[84,128]{1,0:T(8,128)S(1)}, u32[]{:S(2)}, u32[]{:S(2)}) collective-permute-start(f32[84,128]{1,0:T(8,128)S(1)} %pad_maximum_fusion.25), channel_id=1, source_target_pairs={{0,15},{1,0},{2,1},{3,2},{4,3},{5,4},{6,5},{7,6},{8,7},{9,8},{10,9... | collective-permute-start | bytes 129032 | tf_op jit(solution)/shard_map/ppermute | solution.py:24
  164.0 3.8 %collective-permute-start.9 = (f32[240,128]{1,0:T(8,128)S(1)}, f32[240,128]{1,0:T(8,128)S(1)}, u32[]{:S(2)}, u32[]{:S(2)}) collective-permute-start(f32[240,128]{1,0:T(8,128)S(1)} %pad_maximum_fusion.6), channel_id=1, source_target_pairs={{0,16},{1,17},{2,18},{3,19},{4,20},{5,21},{6,22},{7,23},{8,24},{9,... | collective-permute-start | bytes 368648 | tf_op jit(solution)/shard_map/ppermute | solution.py:24
  168.9 5.3 %collective-permute-start.10 = (f32[240,128]{1,0:T(8,128)S(1)}, f32[240,128]{1,0:T(8,128)S(1)}, u32[]{:S(2)}, u32[]{:S(2)}) collective-permute-start(f32[240,128]{1,0:T(8,128)S(1)} %pad_maximum_fusion.7), channel_id=1, source_target_pairs={{0,496},{1,497},{2,498},{3,499},{4,500},{5,501},{6,502},{7,503},{8... | collective-permute-start | bytes 368648 | tf_op jit(solution)/shard_map/ppermute | solution.py:24
  174.9 6.6 %collective-permute-done.10 = f32[240,128]{1,0:T(8,128)S(1)} collective-permute-done((f32[240,128]{1,0:T(8,128)S(1)}, f32[240,128]{1,0:T(8,128)S(1)}, u32[]{:S(2)}, u32[]{:S(2)}) %collective-permute-start.10) | collective-permute-done | bytes 122912 | tf_op jit(solution)/shard_map/ppermute | solution.py:24
  181.6 5.6 %collective-permute-start.11 = (f32[144,128]{1,0:T(8,128)S(1)}, f32[144,128]{1,0:T(8,128)S(1)}, u32[]{:S(2)}, u32[]{:S(2)}) collective-permute-start(f32[144,128]{1,0:T(8,128)S(1)} %pad_maximum_fusion.20), channel_id=1, source_target_pairs={{0,16},{1,17},{2,18},{3,19},{4,20},{5,21},{6,22},{7,23},{8,24},{9,... | collective-permute-start | bytes 221192 | tf_op jit(solution)/shard_map/ppermute | solution.py:24
  188.8 3.3 %shard_map.162 = f32[3,2,8,128]{3,2,1,0:T(8,128)} custom-call(s32[1]{0:T(128)} %bitcast.core_ref, f32[3,10,16,128]{3,2,1,0:T(8,128)} %copy-done.6, f32[12,24,128]{2,1,0:T(8,128)} %get-tuple-element.21.visc), custom_call_target="tpu_custom_call" | custom-call | tf_op jit(solution)/shard_map/pallas_call | solution.py:65
  (177 shorter events, 32.8 us)
Async XLA Ops:
  0.6 76.0 %copy-start = (f32[1,128,128]{2,1,0:T(8,128)S(1)}, f32[1,128,128]{2,1,0:T(8,128)}, u32[]{:S(2)}) copy-start(f32[1,128,128]{2,1,0:T(8,128)} %param.16) | copy-start | bytes 196612
  2.3 51.4 %copy-start.4 = (f32[3,2,8,128]{3,2,1,0:T(8,128)}, f32[3,2,8,128]{3,2,1,0:T(8,128)S(1)}, u32[]{:S(2)}) copy-start(f32[3,2,8,128]{3,2,1,0:T(8,128)S(1)} %get-tuple-element.105.cot) | copy-start | bytes 73732
  2.4 21.2 %collective-permute-start = (f32[46,128]{1,0:T(8,128)S(1)}, f32[46,128]{1,0:T(8,128)S(1)}, u32[]{:S(2)}, u32[]{:S(2)}) collective-permute-start(f32[46,128]{1,0:T(8,128)S(1)} %pad_maximum_fusion.39), channel_id=1, source_target_pairs={{0,1},{1,2},{2,3},{3,4},{4,5},{5,6},{6,7},{7,8},{8,9},{9,10},{10,1... | collective-permute-start | bytes 70664 | tf_op jit(solution)/shard_map/ppermute | solution.py:24
  6.4 17.2 %collective-permute-start.1 = (f32[46,128]{1,0:T(8,128)S(1)}, f32[46,128]{1,0:T(8,128)S(1)}, u32[]{:S(2)}, u32[]{:S(2)}) collective-permute-start(f32[46,128]{1,0:T(8,128)S(1)} %pad_maximum_fusion.40), channel_id=1, source_target_pairs={{0,15},{1,0},{2,1},{3,2},{4,3},{5,4},{6,5},{7,6},{8,7},{9,8},{10,9... | collective-permute-start | bytes 70664 | tf_op jit(solution)/shard_map/ppermute | solution.py:24
  13.9 11.3 %collective-permute-start.2 = (f32[56,128]{1,0:T(8,128)S(1)}, f32[56,128]{1,0:T(8,128)S(1)}, u32[]{:S(2)}, u32[]{:S(2)}) collective-permute-start(f32[56,128]{1,0:T(8,128)S(1)} %pad_maximum_fusion.26), channel_id=1, source_target_pairs={{0,496},{1,497},{2,498},{3,499},{4,500},{5,501},{6,502},{7,503},{8... | collective-permute-start | bytes 86024 | tf_op jit(solution)/shard_map/ppermute | solution.py:24
  23.6 30.1 %copy-start.9 = (f32[46,128]{1,0:T(8,128)}, f32[46,128]{1,0:T(8,128)S(1)}, u32[]{:S(2)}) copy-start(f32[46,128]{1,0:T(8,128)S(1)} %collective-permute-done.low) | copy-start | bytes 70660
  23.6 30.1 %copy-start.10 = (f32[46,128]{1,0:T(8,128)}, f32[46,128]{1,0:T(8,128)S(1)}, u32[]{:S(2)}) copy-start(f32[46,128]{1,0:T(8,128)S(1)} %collective-permute-done.1.high) | copy-start | bytes 70660
  25.2 7.9 %collective-permute-start.3 = (f32[200,128]{1,0:T(8,128)S(1)}, f32[200,128]{1,0:T(8,128)S(1)}, u32[]{:S(2)}, u32[]{:S(2)}) collective-permute-start(f32[200,128]{1,0:T(8,128)S(1)} %pad_maximum_fusion.8), channel_id=1, source_target_pairs={{0,16},{1,17},{2,18},{3,19},{4,20},{5,21},{6,22},{7,23},{8,24},{9,... | collective-permute-start | bytes 307208 | tf_op jit(solution)/shard_map/ppermute | solution.py:24
  33.1 41.7 %copy-start.12 = (f32[1,9,128]{2,0,1:T(1,128)S(1)}, f32[1,9,128]{2,0,1:T(1,128)}, u32[]{:S(2)}) copy-start(f32[1,9,128]{2,0,1:T(1,128)} %param.14) | copy-start | bytes 13828
  33.1 41.7 %copy-start.17 = (f32[1,128]{1,0:T(1,128)S(1)}, f32[1,128]{1,0:T(1,128)}, u32[]{:S(2)}) copy-start(f32[1,128]{1,0:T(1,128)} %param.15) | copy-start | bytes 1540
  33.2 12.9 %collective-permute-start.4 = (f32[288,128]{1,0:T(8,128)S(1)}, f32[288,128]{1,0:T(8,128)S(1)}, u32[]{:S(2)}, u32[]{:S(2)}) collective-permute-start(f32[288,128]{1,0:T(8,128)S(1)} %pad_maximum_fusion.1), channel_id=1, source_target_pairs={{0,496},{1,497},{2,498},{3,499},{4,500},{5,501},{6,502},{7,503},{8... | collective-permute-start | bytes 442376 | tf_op jit(solution)/shard_map/ppermute | solution.py:24
  46.2 7.5 %collective-permute-start.5 = (f32[4,3,16,128]{3,2,1,0:T(8,128)S(1)}, f32[4,3,16,128]{3,2,1,0:T(8,128)S(1)}, u32[]{:S(2)}, u32[]{:S(2)}) collective-permute-start(f32[4,3,16,128]{3,2,1,0:T(8,128)S(1)} %rev.38), channel_id=1, source_target_pairs={{0,16},{1,17},{2,18},{3,19},{4,20},{5,21},{6,22},{7,23},{8,24},{9,... | collective-permute-start | bytes 294920 | tf_op jit(solution)/shard_map/ppermute | solution.py:24
  85.6 4.3 %collective-permute-start.12 = (f32[146,128]{1,0:T(8,128)S(1)}, f32[146,128]{1,0:T(8,128)S(1)}, u32[]{:S(2)}, u32[]{:S(2)}) collective-permute-start(f32[146,128]{1,0:T(8,128)S(1)} %concatenate.137), channel_id=1, source_target_pairs={{0,16},{1,17},{2,18},{3,19},{4,20},{5,21},{6,22},{7,23},{8,24},{9,... | collective-permute-start | bytes 224264 | tf_op jit(solution)/shard_map/ppermute | solution.py:24
  90.6 22.2 %all-to-all-start.2 = ((f32[16,10,128]{2,1,0:T(8,128)}), f32[16,10,128]{2,1,0:T(8,128)S(1)}, u32[]{:S(2)}, u32[]{:S(2)}) async-start(f32[16,10,128]{2,1,0:T(8,128)} %reshape.238), calls=%async_computation.2 | async-start | bytes 262144 | tf_op jit(solution)/shard_map/all_to_all | solution.py:28
  100.0 39.5 %copy-start.18 = (s32[16]{0:T(128)S(1)}, s32[16]{0:T(128)}, u32[]{:S(2)}) copy-start(s32[16]{0:T(128)} %get-tuple-element.20) | copy-start | bytes 196
  113.4 20.5 %all-to-all-start.3 = ((f32[16,10,128]{2,1,0:T(8,128)}), f32[16,10,128]{2,1,0:T(8,128)S(1)}, u32[]{:S(2)}, u32[]{:S(2)}) async-start(f32[16,10,128]{2,1,0:T(8,128)} %broadcast_in_dim.34), calls=%async_computation.3 | async-start | bytes 262144 | tf_op jit(solution)/shard_map/all_to_all | solution.py:28
  118.1 35.3 %copy-start.5 = (f32[3,2,8,128]{3,2,1,0:T(8,128)S(1)}, f32[3,2,8,128]{3,2,1,0:T(8,128)}, u32[]{:S(2)}) copy-start(f32[3,2,8,128]{3,2,1,0:T(8,128)} %copy-done.4) | copy-start | bytes 73732
  133.9 14.6 %all-to-all-start.1 = ((f32[16,30,128]{2,1,0:T(8,128)}), f32[16,30,128]{2,1,0:T(8,128)S(1)}, u32[]{:S(2)}, u32[]{:S(2)}) async-start(f32[16,30,128]{2,1,0:T(8,128)} %reshape.210), calls=%async_computation.1 | async-start | bytes 524288 | tf_op jit(solution)/shard_map/all_to_all | solution.py:28
  149.6 13.2 %collective-permute-start.8 = (f32[48,128]{1,0:T(8,128)S(1)}, f32[48,128]{1,0:T(8,128)S(1)}, u32[]{:S(2)}, u32[]{:S(2)}) collective-permute-start(f32[48,128]{1,0:T(8,128)S(1)} %pad_maximum_fusion.42), channel_id=1, source_target_pairs={{0,496},{1,497},{2,498},{3,499},{4,500},{5,501},{6,502},{7,503},{8... | collective-permute-start | bytes 73736 | tf_op jit(solution)/shard_map/ppermute | solution.py:24
  153.5 9.2 %collective-permute-start.6 = (f32[84,128]{1,0:T(8,128)S(1)}, f32[84,128]{1,0:T(8,128)S(1)}, u32[]{:S(2)}, u32[]{:S(2)}) collective-permute-start(f32[84,128]{1,0:T(8,128)S(1)} %pad_maximum_fusion.24), channel_id=1, source_target_pairs={{0,1},{1,2},{2,3},{3,4},{4,5},{5,6},{6,7},{7,8},{8,9},{9,10},{10,1... | collective-permute-start | bytes 129032 | tf_op jit(solution)/shard_map/ppermute | solution.py:24
  155.8 8.1 %collective-permute-start.7 = (f32[84,128]{1,0:T(8,128)S(1)}, f32[84,128]{1,0:T(8,128)S(1)}, u32[]{:S(2)}, u32[]{:S(2)}) collective-permute-start(f32[84,128]{1,0:T(8,128)S(1)} %pad_maximum_fusion.25), channel_id=1, source_target_pairs={{0,15},{1,0},{2,1},{3,2},{4,3},{5,4},{6,5},{7,6},{8,7},{9,8},{10,9... | collective-permute-start | bytes 129032 | tf_op jit(solution)/shard_map/ppermute | solution.py:24
  164.0 4.7 %collective-permute-start.9 = (f32[240,128]{1,0:T(8,128)S(1)}, f32[240,128]{1,0:T(8,128)S(1)}, u32[]{:S(2)}, u32[]{:S(2)}) collective-permute-start(f32[240,128]{1,0:T(8,128)S(1)} %pad_maximum_fusion.6), channel_id=1, source_target_pairs={{0,16},{1,17},{2,18},{3,19},{4,20},{5,21},{6,22},{7,23},{8,24},{9,... | collective-permute-start | bytes 368648 | tf_op jit(solution)/shard_map/ppermute | solution.py:24
  168.9 12.6 %collective-permute-start.10 = (f32[240,128]{1,0:T(8,128)S(1)}, f32[240,128]{1,0:T(8,128)S(1)}, u32[]{:S(2)}, u32[]{:S(2)}) collective-permute-start(f32[240,128]{1,0:T(8,128)S(1)} %pad_maximum_fusion.7), channel_id=1, source_target_pairs={{0,496},{1,497},{2,498},{3,499},{4,500},{5,501},{6,502},{7,503},{8... | collective-permute-start | bytes 368648 | tf_op jit(solution)/shard_map/ppermute | solution.py:24
  181.6 6.5 %collective-permute-start.11 = (f32[144,128]{1,0:T(8,128)S(1)}, f32[144,128]{1,0:T(8,128)S(1)}, u32[]{:S(2)}, u32[]{:S(2)}) collective-permute-start(f32[144,128]{1,0:T(8,128)S(1)} %pad_maximum_fusion.20), channel_id=1, source_target_pairs={{0,16},{1,17},{2,18},{3,19},{4,20},{5,21},{6,22},{7,23},{8,24},{9,... | collective-permute-start | bytes 221192 | tf_op jit(solution)/shard_map/ppermute | solution.py:24
  (11 other events, 117.0 us)

commit v5 on v4

--- a/solution.py
+++ b/solution.py
@@ -61,10 +61,19 @@
     return pl.BlockSpec(memory_space=space)
 
 
-def call(kernel, outs, scratch, smem_ins, args, smem_outs=()):
+def call(kernel, outs, scratch, smem_ins, args, smem_outs=(), vmem_outs=()):
+    if not INTERPRET:
+        args = [
+            arg if i in smem_ins else pltpu.with_memory_space_constraint(arg, pltpu.VMEM)
+            for i, arg in enumerate(args)
+        ]
+    vmem_outs = () if INTERPRET else vmem_outs
     return pl.pallas_call(
         kernel,
-        out_shape=[jax.ShapeDtypeStruct(shape, dtype) for shape, dtype in outs],
+        out_shape=[
+            (pltpu.VMEM if i in vmem_outs else jax.ShapeDtypeStruct)(shape, dtype)
+            for i, (shape, dtype) in enumerate(outs)
+        ],
         in_specs=[spec(pltpu.SMEM if i in smem_ins else pltpu.VMEM) for i in range(len(args))],
         out_specs=[spec(pltpu.SMEM if i in smem_outs else pltpu.VMEM) for i in range(len(outs))],
         scratch_shapes=scratch,
@@ -187,11 +196,13 @@
 
 
 def finish_kernel(whole, w_in, b_in, w_mid, b_mid, w_out, b_out):
-    w_in[0] = whole[0:9]
+    for i in range(9):
+        w_in[i] = whole[i : i + 1]
+    for i in range(6):
+        w_out[i] = whole[139 + i : 140 + i]
     b_in[...] = whole[9:10]
     w_mid[0] = whole[10:138]
     b_mid[...] = whole[138:139]
-    w_out[...] = whole[139:145]
     b_out[...] = whole[145:146]
 
 
@@ -239,6 +250,7 @@
         (0, 1),
         (core_arg, assignment.reshape(16), fields, cot, low, high, edge, mate, near, mate_in),
         smem_outs=(3,),
+        vmem_outs=(1, 2),
     )
     recv = exchange(send.reshape(experts, CAP * 16, 128), "yz")
     recv = recv.reshape(experts * CAP, 16, 128)
@@ -347,11 +359,11 @@
     results = call(
         finish_kernel,
         [
-            ((1, 9, 128), f32),
+            ((9, 1, 128), f32),
             ((1, 128), f32),
             ((1, 128, 128), f32),
             ((1, 128), f32),
-            ((6, 128), f32),
+            ((6, 1, 128), f32),
             ((1, 128), f32),
         ],
         [],
@@ -362,11 +374,11 @@
     return (
         mirror(predicted, 1),
         grad_velocity,
-        g_w_in,
+        jnp.transpose(g_w_in, (1, 0, 2)),
         g_b_in,
         g_w_mid,
         g_b_mid,
-        jnp.transpose(g_w_out)[None],
+        jnp.transpose(g_w_out, (1, 2, 0)),
         g_b_out[:, :6],
     )
 

time: 193 us -> 191 us (0.990)
  waiting for transfers between devices: 54.3 us -> 59.2 us
  local copies, waits for them, and re-layouts: 10.7 us -> 6.19 us
  Pallas kernels: 11.2 us -> 8.97 us
    all_to_all x3, waiting for transfers between devices: 31.8 us -> 35.9 us  [exchange(): lax.all_to_all(value, axis, 0, 0, axis_index_groups=groups, tiled=True)]
    unnamed x45 -> x23, local copies, waits for them, and re-layouts: 6.2 us -> 2.31 us
    pallas_call x3, Pallas kernels: 11.2 us -> 8.97 us  [call(): pl.pallas_call(kernel, out_shape=[(pltpu.VMEM if i in vmem_outs else jax....]
  transfers between devices with their start and end apart: 16 -> 16, of which waited for: 12 -> 12; matrix products, arithmetic and copies ran while one was open for 4% -> 2% of each run, Pallas kernels for 1% -> 0%
where the time goes in v5:
time: 191 us; the launch traced here: 190 us
  starting transfers between devices  86.2 us (45%)
  waiting for transfers between devices  59.2 us (31%)
  blocking collectives  13.6 us (7%)
  matrix products  10.8 us (6%)
  Pallas kernels  8.97 us (5%)
  local copies, waits for them, and re-layouts  6.19 us (3%)
  other arithmetic  2.94 us (2%)
    ppermute x13, starting transfers between devices, permute(): return lax.ppermute(value, AXES, pairs)  68.9 us
    all_to_all x3, waiting for transfers between devices, exchange(): lax.all_to_all(value, axis, 0, 0, axis_index_groups=groups, tiled=True)  35.9 us
    ppermute x13, waiting for transfers between devices, permute(): return lax.ppermute(value, AXES, pairs)  23.3 us
    all_to_all x3, starting transfers between devices, exchange(): lax.all_to_all(value, axis, 0, 0, axis_index_groups=groups, tiled=True)  17.3 us
    all_to_all x1, blocking collectives, exchange(): lax.all_to_all(value, axis, 0, 0, axis_index_groups=groups, tiled=True)  13.6 us
    dot_general x9, matrix products, dot(): return lax.dot_general(a, b, (((ca,), (cb,)), ((), ())), precision=PREC)  10.8 us
    pallas_call x3, Pallas kernels, call(): pl.pallas_call(kernel, out_shape=[(pltpu.VMEM if i in vmem_outs else jax....  8.97 us
  transfers between devices with their start and end apart: 16, of which 12 were waited for; matrix products, arithmetic and copies ran while one was open for 2% of the time, Pallas kernels for 0%

profile of v5, /device:TPU:1, one launch (start us, length us, event | category | flops | bytes accessed | tf_op | source)
XLA Modules:
  0.0 189.5 jit_solution(16900451751980235991)
XLA Ops:
  2.4 4.0 %collective-permute-start = (f32[46,128]{1,0:T(8,128)S(1)}, f32[46,128]{1,0:T(8,128)S(1)}, u32[]{:S(2)}, u32[]{:S(2)}) collective-permute-start(f32[46,128]{1,0:T(8,128)S(1)} %pad_maximum_fusion.39), channel_id=1, source_target_pairs={{0,1},{1,2},{2,3},{3,4},{4,5},{5,6},{6,7},{7,8},{8,9},{9,10},{10,1... | collective-permute-start | bytes 70664 | tf_op jit(solution)/shard_map/ppermute | solution.py:24
  6.4 7.4 %collective-permute-start.1 = (f32[46,128]{1,0:T(8,128)S(1)}, f32[46,128]{1,0:T(8,128)S(1)}, u32[]{:S(2)}, u32[]{:S(2)}) collective-permute-start(f32[46,128]{1,0:T(8,128)S(1)} %pad_maximum_fusion.40), channel_id=1, source_target_pairs={{0,15},{1,0},{2,1},{3,2},{4,3},{5,4},{6,5},{7,6},{8,7},{9,8},{10,9... | collective-permute-start | bytes 70664 | tf_op jit(solution)/shard_map/ppermute | solution.py:24
  13.9 9.7 %collective-permute-start.2 = (f32[56,128]{1,0:T(8,128)S(1)}, f32[56,128]{1,0:T(8,128)S(1)}, u32[]{:S(2)}, u32[]{:S(2)}) collective-permute-start(f32[56,128]{1,0:T(8,128)S(1)} %pad_maximum_fusion.26), channel_id=1, source_target_pairs={{0,496},{1,497},{2,498},{3,499},{4,500},{5,501},{6,502},{7,503},{8... | collective-permute-start | bytes 86024 | tf_op jit(solution)/shard_map/ppermute | solution.py:24
  25.2 7.0 %collective-permute-start.3 = (f32[200,128]{1,0:T(8,128)S(1)}, f32[200,128]{1,0:T(8,128)S(1)}, u32[]{:S(2)}, u32[]{:S(2)}) collective-permute-start(f32[200,128]{1,0:T(8,128)S(1)} %pad_maximum_fusion.8), channel_id=1, source_target_pairs={{0,16},{1,17},{2,18},{3,19},{4,20},{5,21},{6,22},{7,23},{8,24},{9,... | collective-permute-start | bytes 307208 | tf_op jit(solution)/shard_map/ppermute | solution.py:24
  33.2 3.1 %collective-permute-start.4 = (f32[288,128]{1,0:T(8,128)S(1)}, f32[288,128]{1,0:T(8,128)S(1)}, u32[]{:S(2)}, u32[]{:S(2)}) collective-permute-start(f32[288,128]{1,0:T(8,128)S(1)} %pad_maximum_fusion.1), channel_id=1, source_target_pairs={{0,496},{1,497},{2,498},{3,499},{4,500},{5,501},{6,502},{7,503},{8... | collective-permute-start | bytes 442376 | tf_op jit(solution)/shard_map/ppermute | solution.py:24
  36.3 9.8 %collective-permute-done.4.near = f32[288,128]{1,0:T(8,128)S(1)} collective-permute-done((f32[288,128]{1,0:T(8,128)S(1)}, f32[288,128]{1,0:T(8,128)S(1)}, u32[]{:S(2)}, u32[]{:S(2)}) %collective-permute-start.4) | collective-permute-done | bytes 147488 | tf_op jit(solution)/shard_map/ppermute | solution.py:24
  46.1 6.6 %collective-permute-start.5 = (f32[4,3,16,128]{3,2,1,0:T(8,128)S(1)}, f32[4,3,16,128]{3,2,1,0:T(8,128)S(1)}, u32[]{:S(2)}, u32[]{:S(2)}) collective-permute-start(f32[4,3,16,128]{3,2,1,0:T(8,128)S(1)} %rev.38), channel_id=1, source_target_pairs={{0,16},{1,17},{2,18},{3,19},{4,20},{5,21},{6,22},{7,23},{8,24},{9,... | collective-permute-start | bytes 294920 | tf_op jit(solution)/shard_map/ppermute | solution.py:24
  53.7 5.9 %shard_map.161 = (f32[32,16,128]{2,1,0:T(8,128)}, f32[3,2,8,128]{3,2,1,0:T(8,128)S(1)}, f32[12,24,128]{2,1,0:T(8,128)S(1)}, s32[16]{0:T(128)}) custom-call(s32[1]{0:T(128)} %bitcast.core_ref, s32[16]{0:T(128)} %bitcast.195, f32[4,2,8,128]{3,2,1,0:T(8,128)S(1)} %pad_maximum_fusion.21.fields, f32[3,2,8,128]{3,2,1,0:T(8,128)S(1)} %get-tuple-element.81.cot, ...), custom_call_target="tpu_custom_call" | custom-call | tf_op jit(solution)/shard_map/pallas_call | solution.py:71
  59.6 13.6 %all_to_all.20 = f32[16,32,128]{2,1,0:T(8,128)S(1)} all-to-all(f32[16,32,128]{2,1,0:T(8,128)} %bitcast.160), channel_id=1, replica_groups=mesh['gx'=32,'yz'=16] {'yz'}, dimensions={0} | all-to-all | bytes 524288 | tf_op jit(solution)/shard_map/all_to_all | solution.py:28
  84.4 3.4 %collective-permute-start.12 = (f32[146,128]{1,0:T(8,128)S(1)}, f32[146,128]{1,0:T(8,128)S(1)}, u32[]{:S(2)}, u32[]{:S(2)}) collective-permute-start(f32[146,128]{1,0:T(8,128)S(1)} %concatenate.137), channel_id=1, source_target_pairs={{0,16},{1,17},{2,18},{3,19},{4,20},{5,21},{6,22},{7,23},{8,24},{9,... | collective-permute-start | bytes 224264 | tf_op jit(solution)/shard_map/ppermute | solution.py:24
  89.4 7.1 %all-to-all-start.2 = ((f32[16,10,128]{2,1,0:T(8,128)}), f32[16,10,128]{2,1,0:T(8,128)S(1)}, u32[]{:S(2)}, u32[]{:S(2)}) async-start(f32[16,10,128]{2,1,0:T(8,128)} %reshape.238), calls=%async_computation.2 | async-start | bytes 262144 | tf_op jit(solution)/shard_map/all_to_all | solution.py:28
  99.1 12.7 %all-to-all-done.2 = f32[16,10,128]{2,1,0:T(8,128)S(1)} async-done(((f32[16,10,128]{2,1,0:T(8,128)}), f32[16,10,128]{2,1,0:T(8,128)S(1)}, u32[]{:S(2)}, u32[]{:S(2)}) %all-to-all-start.2) | async-done | bytes 81952 | tf_op jit(solution)/shard_map/all_to_all | solution.py:28
  112.5 4.6 %all-to-all-start.3 = ((f32[16,10,128]{2,1,0:T(8,128)}), f32[16,10,128]{2,1,0:T(8,128)S(1)}, u32[]{:S(2)}, u32[]{:S(2)}) async-start(f32[16,10,128]{2,1,0:T(8,128)} %broadcast_in_dim.31), calls=%async_computation.3 | async-start | bytes 262144 | tf_op jit(solution)/shard_map/all_to_all | solution.py:28
  118.1 14.9 %all-to-all-done.3 = f32[16,10,128]{2,1,0:T(8,128)S(1)} async-done(((f32[16,10,128]{2,1,0:T(8,128)}), f32[16,10,128]{2,1,0:T(8,128)S(1)}, u32[]{:S(2)}, u32[]{:S(2)}) %all-to-all-start.3) | async-done | bytes 81952 | tf_op jit(solution)/shard_map/all_to_all | solution.py:28
  132.9 5.6 %all-to-all-start.1 = ((f32[16,30,128]{2,1,0:T(8,128)}), f32[16,30,128]{2,1,0:T(8,128)S(1)}, u32[]{:S(2)}, u32[]{:S(2)}) async-start(f32[16,30,128]{2,1,0:T(8,128)} %reshape.210), calls=%async_computation.1 | async-start | bytes 524288 | tf_op jit(solution)/shard_map/all_to_all | solution.py:28
  139.3 8.3 %all-to-all-done.1 = f32[16,30,128]{2,1,0:T(8,128)S(1)} async-done(((f32[16,30,128]{2,1,0:T(8,128)}), f32[16,30,128]{2,1,0:T(8,128)S(1)}, u32[]{:S(2)}, u32[]{:S(2)}) %all-to-all-start.1) | async-done | bytes 245792 | tf_op jit(solution)/shard_map/all_to_all | solution.py:28
  148.6 3.8 %collective-permute-start.8 = (f32[48,128]{1,0:T(8,128)S(1)}, f32[48,128]{1,0:T(8,128)S(1)}, u32[]{:S(2)}, u32[]{:S(2)}) collective-permute-start(f32[48,128]{1,0:T(8,128)S(1)} %pad_maximum_fusion.42), channel_id=1, source_target_pairs={{0,496},{1,497},{2,498},{3,499},{4,500},{5,501},{6,502},{7,503},{8... | collective-permute-start | bytes 73736 | tf_op jit(solution)/shard_map/ppermute | solution.py:24
  152.6 2.2 %collective-permute-start.6 = (f32[84,128]{1,0:T(8,128)S(1)}, f32[84,128]{1,0:T(8,128)S(1)}, u32[]{:S(2)}, u32[]{:S(2)}) collective-permute-start(f32[84,128]{1,0:T(8,128)S(1)} %pad_maximum_fusion.24), channel_id=1, source_target_pairs={{0,1},{1,2},{2,3},{3,4},{4,5},{5,6},{6,7},{7,8},{8,9},{9,10},{10,1... | collective-permute-start | bytes 129032 | tf_op jit(solution)/shard_map/ppermute | solution.py:24
  154.8 7.0 %collective-permute-start.7 = (f32[84,128]{1,0:T(8,128)S(1)}, f32[84,128]{1,0:T(8,128)S(1)}, u32[]{:S(2)}, u32[]{:S(2)}) collective-permute-start(f32[84,128]{1,0:T(8,128)S(1)} %pad_maximum_fusion.25), channel_id=1, source_target_pairs={{0,15},{1,0},{2,1},{3,2},{4,3},{5,4},{6,5},{7,6},{8,7},{9,8},{10,9... | collective-permute-start | bytes 129032 | tf_op jit(solution)/shard_map/ppermute | solution.py:24
  163.0 3.8 %collective-permute-start.9 = (f32[240,128]{1,0:T(8,128)S(1)}, f32[240,128]{1,0:T(8,128)S(1)}, u32[]{:S(2)}, u32[]{:S(2)}) collective-permute-start(f32[240,128]{1,0:T(8,128)S(1)} %pad_maximum_fusion.6), channel_id=1, source_target_pairs={{0,16},{1,17},{2,18},{3,19},{4,20},{5,21},{6,22},{7,23},{8,24},{9,... | collective-permute-start | bytes 368648 | tf_op jit(solution)/shard_map/ppermute | solution.py:24
  167.9 5.3 %collective-permute-start.10 = (f32[240,128]{1,0:T(8,128)S(1)}, f32[240,128]{1,0:T(8,128)S(1)}, u32[]{:S(2)}, u32[]{:S(2)}) collective-permute-start(f32[240,128]{1,0:T(8,128)S(1)} %pad_maximum_fusion.7), channel_id=1, source_target_pairs={{0,496},{1,497},{2,498},{3,499},{4,500},{5,501},{6,502},{7,503},{8... | collective-permute-start | bytes 368648 | tf_op jit(solution)/shard_map/ppermute | solution.py:24
  173.9 6.6 %collective-permute-done.10 = f32[240,128]{1,0:T(8,128)S(1)} collective-permute-done((f32[240,128]{1,0:T(8,128)S(1)}, f32[240,128]{1,0:T(8,128)S(1)}, u32[]{:S(2)}, u32[]{:S(2)}) %collective-permute-start.10) | collective-permute-done | bytes 122912 | tf_op jit(solution)/shard_map/ppermute | solution.py:24
  180.6 5.6 %collective-permute-start.11 = (f32[144,128]{1,0:T(8,128)S(1)}, f32[144,128]{1,0:T(8,128)S(1)}, u32[]{:S(2)}, u32[]{:S(2)}) collective-permute-start(f32[144,128]{1,0:T(8,128)S(1)} %pad_maximum_fusion.20), channel_id=1, source_target_pairs={{0,16},{1,17},{2,18},{3,19},{4,20},{5,21},{6,22},{7,23},{8,24},{9,... | collective-permute-start | bytes 221192 | tf_op jit(solution)/shard_map/ppermute | solution.py:24
  187.2 2.4 %shard_map.162 = f32[3,2,8,128]{3,2,1,0:T(8,128)} custom-call(s32[1]{0:T(128)} %bitcast.core_ref, f32[3,10,16,128]{3,2,1,0:T(8,128)S(1)} %reverse_dynamic-update-slice_fusion.adjoint, f32[12,24,128]{2,1,0:T(8,128)S(1)} %get-tuple-element.21.visc), custom_call_target="tpu_custom_call" | custom-call | tf_op jit(solution)/shard_map/pallas_call | solution.py:71
  (155 shorter events, 27.6 us)
Async XLA Ops:
  0.6 74.9 %copy-start = (f32[1,128,128]{2,1,0:T(8,128)S(1)}, f32[1,128,128]{2,1,0:T(8,128)}, u32[]{:S(2)}) copy-start(f32[1,128,128]{2,1,0:T(8,128)} %param.16) | copy-start | bytes 196612
  2.4 21.2 %collective-permute-start = (f32[46,128]{1,0:T(8,128)S(1)}, f32[46,128]{1,0:T(8,128)S(1)}, u32[]{:S(2)}, u32[]{:S(2)}) collective-permute-start(f32[46,128]{1,0:T(8,128)S(1)} %pad_maximum_fusion.39), channel_id=1, source_target_pairs={{0,1},{1,2},{2,3},{3,4},{4,5},{5,6},{6,7},{7,8},{8,9},{9,10},{10,1... | collective-permute-start | bytes 70664 | tf_op jit(solution)/shard_map/ppermute | solution.py:24
  6.4 17.2 %collective-permute-start.1 = (f32[46,128]{1,0:T(8,128)S(1)}, f32[46,128]{1,0:T(8,128)S(1)}, u32[]{:S(2)}, u32[]{:S(2)}) collective-permute-start(f32[46,128]{1,0:T(8,128)S(1)} %pad_maximum_fusion.40), channel_id=1, source_target_pairs={{0,15},{1,0},{2,1},{3,2},{4,3},{5,4},{6,5},{7,6},{8,7},{9,8},{10,9... | collective-permute-start | bytes 70664 | tf_op jit(solution)/shard_map/ppermute | solution.py:24
  13.9 11.3 %collective-permute-start.2 = (f32[56,128]{1,0:T(8,128)S(1)}, f32[56,128]{1,0:T(8,128)S(1)}, u32[]{:S(2)}, u32[]{:S(2)}) collective-permute-start(f32[56,128]{1,0:T(8,128)S(1)} %pad_maximum_fusion.26), channel_id=1, source_target_pairs={{0,496},{1,497},{2,498},{3,499},{4,500},{5,501},{6,502},{7,503},{8... | collective-permute-start | bytes 86024 | tf_op jit(solution)/shard_map/ppermute | solution.py:24
  25.2 7.9 %collective-permute-start.3 = (f32[200,128]{1,0:T(8,128)S(1)}, f32[200,128]{1,0:T(8,128)S(1)}, u32[]{:S(2)}, u32[]{:S(2)}) collective-permute-start(f32[200,128]{1,0:T(8,128)S(1)} %pad_maximum_fusion.8), channel_id=1, source_target_pairs={{0,16},{1,17},{2,18},{3,19},{4,20},{5,21},{6,22},{7,23},{8,24},{9,... | collective-permute-start | bytes 307208 | tf_op jit(solution)/shard_map/ppermute | solution.py:24
  33.1 40.5 %copy-start.3 = (f32[1,9,128]{2,0,1:T(1,128)S(1)}, f32[1,9,128]{2,0,1:T(1,128)}, u32[]{:S(2)}) copy-start(f32[1,9,128]{2,0,1:T(1,128)} %param.14) | copy-start | bytes 13828
  33.1 40.6 %copy-start.7 = (f32[1,128]{1,0:T(1,128)S(1)}, f32[1,128]{1,0:T(1,128)}, u32[]{:S(2)}) copy-start(f32[1,128]{1,0:T(1,128)} %param.15) | copy-start | bytes 1540
  33.2 12.9 %collective-permute-start.4 = (f32[288,128]{1,0:T(8,128)S(1)}, f32[288,128]{1,0:T(8,128)S(1)}, u32[]{:S(2)}, u32[]{:S(2)}) collective-permute-start(f32[288,128]{1,0:T(8,128)S(1)} %pad_maximum_fusion.1), channel_id=1, source_target_pairs={{0,496},{1,497},{2,498},{3,499},{4,500},{5,501},{6,502},{7,503},{8... | collective-permute-start | bytes 442376 | tf_op jit(solution)/shard_map/ppermute | solution.py:24
  46.1 7.5 %collective-permute-start.5 = (f32[4,3,16,128]{3,2,1,0:T(8,128)S(1)}, f32[4,3,16,128]{3,2,1,0:T(8,128)S(1)}, u32[]{:S(2)}, u32[]{:S(2)}) collective-permute-start(f32[4,3,16,128]{3,2,1,0:T(8,128)S(1)} %rev.38), channel_id=1, source_target_pairs={{0,16},{1,17},{2,18},{3,19},{4,20},{5,21},{6,22},{7,23},{8,24},{9,... | collective-permute-start | bytes 294920 | tf_op jit(solution)/shard_map/ppermute | solution.py:24
  59.6 15.9 %copy-start.5 = (f32[1,128]{1,0:T(1,128)S(1)}, f32[1,128]{1,0:T(1,128)}, u32[]{:S(2)}) copy-start(f32[1,128]{1,0:T(1,128)} %param.17) | copy-start | bytes 1540
  82.0 1.4 copy-start.1
  82.0 14.5 %copy-start.6 = (f32[1,6]{1,0:T(1,128)S(1)}, f32[1,6]{1,0:T(1,128)}, u32[]{:S(2)}) copy-start(f32[1,6]{1,0:T(1,128)} %param.19) | copy-start | bytes 76
  84.4 4.3 %collective-permute-start.12 = (f32[146,128]{1,0:T(8,128)S(1)}, f32[146,128]{1,0:T(8,128)S(1)}, u32[]{:S(2)}, u32[]{:S(2)}) collective-permute-start(f32[146,128]{1,0:T(8,128)S(1)} %concatenate.137), channel_id=1, source_target_pairs={{0,16},{1,17},{2,18},{3,19},{4,20},{5,21},{6,22},{7,23},{8,24},{9,... | collective-permute-start | bytes 224264 | tf_op jit(solution)/shard_map/ppermute | solution.py:24
  89.4 22.4 %all-to-all-start.2 = ((f32[16,10,128]{2,1,0:T(8,128)}), f32[16,10,128]{2,1,0:T(8,128)S(1)}, u32[]{:S(2)}, u32[]{:S(2)}) async-start(f32[16,10,128]{2,1,0:T(8,128)} %reshape.238), calls=%async_computation.2 | async-start | bytes 262144 | tf_op jit(solution)/shard_map/all_to_all | solution.py:28
  96.5 1.6 copy-start.2
  99.1 39.5 %copy-start.8 = (s32[16]{0:T(128)S(1)}, s32[16]{0:T(128)}, u32[]{:S(2)}) copy-start(s32[16]{0:T(128)} %get-tuple-element.20) | copy-start | bytes 196
  112.5 20.5 %all-to-all-start.3 = ((f32[16,10,128]{2,1,0:T(8,128)}), f32[16,10,128]{2,1,0:T(8,128)S(1)}, u32[]{:S(2)}, u32[]{:S(2)}) async-start(f32[16,10,128]{2,1,0:T(8,128)} %broadcast_in_dim.31), calls=%async_computation.3 | async-start | bytes 262144 | tf_op jit(solution)/shard_map/all_to_all | solution.py:28
  132.9 14.6 %all-to-all-start.1 = ((f32[16,30,128]{2,1,0:T(8,128)}), f32[16,30,128]{2,1,0:T(8,128)S(1)}, u32[]{:S(2)}, u32[]{:S(2)}) async-start(f32[16,30,128]{2,1,0:T(8,128)} %reshape.210), calls=%async_computation.1 | async-start | bytes 524288 | tf_op jit(solution)/shard_map/all_to_all | solution.py:28
  148.6 13.2 %collective-permute-start.8 = (f32[48,128]{1,0:T(8,128)S(1)}, f32[48,128]{1,0:T(8,128)S(1)}, u32[]{:S(2)}, u32[]{:S(2)}) collective-permute-start(f32[48,128]{1,0:T(8,128)S(1)} %pad_maximum_fusion.42), channel_id=1, source_target_pairs={{0,496},{1,497},{2,498},{3,499},{4,500},{5,501},{6,502},{7,503},{8... | collective-permute-start | bytes 73736 | tf_op jit(solution)/shard_map/ppermute | solution.py:24
  152.6 9.2 %collective-permute-start.6 = (f32[84,128]{1,0:T(8,128)S(1)}, f32[84,128]{1,0:T(8,128)S(1)}, u32[]{:S(2)}, u32[]{:S(2)}) collective-permute-start(f32[84,128]{1,0:T(8,128)S(1)} %pad_maximum_fusion.24), channel_id=1, source_target_pairs={{0,1},{1,2},{2,3},{3,4},{4,5},{5,6},{6,7},{7,8},{8,9},{9,10},{10,1... | collective-permute-start | bytes 129032 | tf_op jit(solution)/shard_map/ppermute | solution.py:24
  154.8 8.1 %collective-permute-start.7 = (f32[84,128]{1,0:T(8,128)S(1)}, f32[84,128]{1,0:T(8,128)S(1)}, u32[]{:S(2)}, u32[]{:S(2)}) collective-permute-start(f32[84,128]{1,0:T(8,128)S(1)} %pad_maximum_fusion.25), channel_id=1, source_target_pairs={{0,15},{1,0},{2,1},{3,2},{4,3},{5,4},{6,5},{7,6},{8,7},{9,8},{10,9... | collective-permute-start | bytes 129032 | tf_op jit(solution)/shard_map/ppermute | solution.py:24
  163.0 4.7 %collective-permute-start.9 = (f32[240,128]{1,0:T(8,128)S(1)}, f32[240,128]{1,0:T(8,128)S(1)}, u32[]{:S(2)}, u32[]{:S(2)}) collective-permute-start(f32[240,128]{1,0:T(8,128)S(1)} %pad_maximum_fusion.6), channel_id=1, source_target_pairs={{0,16},{1,17},{2,18},{3,19},{4,20},{5,21},{6,22},{7,23},{8,24},{9,... | collective-permute-start | bytes 368648 | tf_op jit(solution)/shard_map/ppermute | solution.py:24
  167.9 12.6 %collective-permute-start.10 = (f32[240,128]{1,0:T(8,128)S(1)}, f32[240,128]{1,0:T(8,128)S(1)}, u32[]{:S(2)}, u32[]{:S(2)}) collective-permute-start(f32[240,128]{1,0:T(8,128)S(1)} %pad_maximum_fusion.7), channel_id=1, source_target_pairs={{0,496},{1,497},{2,498},{3,499},{4,500},{5,501},{6,502},{7,503},{8... | collective-permute-start | bytes 368648 | tf_op jit(solution)/shard_map/ppermute | solution.py:24
  180.6 6.5 %collective-permute-start.11 = (f32[144,128]{1,0:T(8,128)S(1)}, f32[144,128]{1,0:T(8,128)S(1)}, u32[]{:S(2)}, u32[]{:S(2)}) collective-permute-start(f32[144,128]{1,0:T(8,128)S(1)} %pad_maximum_fusion.20), channel_id=1, source_target_pairs={{0,16},{1,17},{2,18},{3,19},{4,20},{5,21},{6,22},{7,23},{8,24},{9,... | collective-permute-start | bytes 221192 | tf_op jit(solution)/shard_map/ppermute | solution.py:24
  (1 other events, 0.7 us)

commit v6 on v5

--- a/solution.py
+++ b/solution.py
@@ -12,6 +12,8 @@
 PREC = lax.Precision.HIGH
 AXES = ("gx", "yz")
 INTERPRET = False
+NEAR_WIDTH = (16, 14, 12, 10, 8)
+NEAR_AT = (0, 64, 120, 168, 208)
 
 
 def permute(value, target):
@@ -114,41 +116,23 @@
     return state
 
 
-def forward_kernel(
-    core_ref, owner_ref, fields, cot, low, high, edge, mate, near, mate_in,
-    send, own_state, visc, slot_ref,
-    work, spare, kx, ky, kz, c_wide, columns, count,
+def placed(core, owner_ref, slot_ref, count):
+    for e in range(count.shape[0]):
+        count[e] = 0
+    for k in range(16):
+        owner = owner_ref[jnp.bitwise_xor(k, core * 8)]
+        rank = count[owner]
+        count[owner] = rank + 1
+        slot_ref[k] = owner * CAP + rank
+
+
+def stress_kernel(
+    core_ref, owner_ref, cot, low, high, edge, mate, send, slot_ref, c_wide, columns, count
 ):
     core = core_ref[0]
     half = 0.5 * (1 - 2 * core).astype(jnp.float32)
-    work[...] = jnp.zeros_like(work)
-    visc[...] = jnp.zeros_like(visc)
     send[...] = jnp.zeros_like(send)
-    for f in range(4):
-        row = (lambda i, f=f: visc.at[i]) if f == 3 else (lambda i, f=f: work.at[f, i])
-        row(0)[8:16] = near[256 + f * 8 : 264 + f * 8]
-        for i in range(4):
-            at = (f * 4 + i) * 16
-            row(4 - i)[4:20] = near[at : at + 16]
-        for x in range(2):
-            at = f * 2 + x
-            row(5 + x)[3:8] = low[at * 5 : at * 5 + 5]
-            row(5 + x)[8:16] = fields[f, x]
-            row(5 + x)[16:21] = high[at * 5 : at * 5 + 5]
-            row(8 - x)[3:21] = mate[at * 18 : at * 18 + 18]
-        for j in range(3):
-            row(11 - j)[4:20] = mate_in[f, j]
-    coefficients(visc, 12, kx, ky, kz)
-    state = diffusion(work, spare, 0, 11, 0, kx, ky, kz)
-
-    for c in range(3):
-        for x in range(2):
-            at = (c * 3) * 16 + x * 8
-            own = state[c, 5 + x, 8:16]
-            own_state[c, x] = own
-            columns[at : at + 8] = half * (state[c, 6 + x, 8:16] - state[c, 4 + x, 8:16])
-            columns[at + 16 : at + 24] = 0.5 * (state[c, 5 + x, 9:17] - state[c, 5 + x, 7:15])
-            columns[at + 32 : at + 40] = 0.5 * (turned(own, -1, 1) - turned(own, 1, 1))
+    placed(core, owner_ref, slot_ref, count)
     for x in range(2):
         d = []
         for c in range(3):
@@ -168,18 +152,46 @@
             d[0][1] + d[1][0], d[0][2] + d[2][0], d[1][2] + d[2][1],
         )
         for k in range(6):
-            columns[(9 + k) * 16 + x * 8 : (9 + k) * 16 + x * 8 + 8] = SCALE * grads[k]
-    columns[240:256] = jnp.zeros((16, 128), jnp.float32)
-
-    for e in range(count.shape[0]):
-        count[e] = 0
+            columns[k * 16 + x * 8 : k * 16 + x * 8 + 8] = SCALE * grads[k]
     for k in range(16):
-        owner = owner_ref[jnp.bitwise_xor(k, core * 8)]
-        rank = count[owner]
-        count[owner] = rank + 1
-        slot = owner * CAP + rank
-        slot_ref[k] = slot
-        send[slot] = columns[pl.ds(k, 16, stride=16)]
+        send[slot_ref[k]] = columns[pl.ds(k, 6, stride=16)]
+
+
+def forward_kernel(
+    core_ref, slot_ref, fields, low, high, mate, near, mate_in,
+    send, own_state, visc,
+    work, spare, kx, ky, kz, columns,
+):
+    half = 0.5 * (1 - 2 * core_ref[0]).astype(jnp.float32)
+    work[...] = jnp.zeros_like(work)
+    visc[...] = jnp.zeros_like(visc)
+    send[...] = jnp.zeros_like(send)
+    for f in range(4):
+        row = (lambda i, f=f: visc.at[i]) if f == 3 else (lambda i, f=f: work.at[f, i])
+        for j in range(5):
+            at = NEAR_AT[j] + f * NEAR_WIDTH[j]
+            row(4 - j)[4 + j : 20 - j] = near[at : at + NEAR_WIDTH[j]]
+            if j < 3:
+                row(9 + j)[4 + j : 20 - j] = mate_in[at : at + NEAR_WIDTH[j]]
+        for x in range(2):
+            at = f * 2 + x
+            row(5 + x)[3:8] = low[at * 5 : at * 5 + 5]
+            row(5 + x)[8:16] = fields[f, x]
+            row(5 + x)[16:21] = high[at * 5 : at * 5 + 5]
+            row(8 - x)[3:21] = mate[at * 18 : at * 18 + 18]
+    coefficients(visc, 12, kx, ky, kz)
+    state = diffusion(work, spare, 0, 11, 0, kx, ky, kz)
+
+    for c in range(3):
+        for x in range(2):
+            at = (c * 3) * 16 + x * 8
+            own = state[c, 5 + x, 8:16]
+            own_state[c, x] = own
+            columns[at : at + 8] = half * (state[c, 6 + x, 8:16] - state[c, 4 + x, 8:16])
+            columns[at + 16 : at + 24] = 0.5 * (state[c, 5 + x, 9:17] - state[c, 5 + x, 7:15])
+            columns[at + 32 : at + 40] = 0.5 * (turned(own, -1, 1) - turned(own, 1, 1))
+    for k in range(16):
+        send[slot_ref[k]] = columns[pl.ds(k, 9, stride=16)]
 
 
 def adjoint_kernel(core_ref, adjoint, visc, out, work, spare, kx, ky, kz):
@@ -231,34 +243,33 @@
     mate = to_partner(packed([wide, edge[:32], cot[:, 1]]))
     partner = mate[:144].reshape(4, 2, 18, 128)
     chip = jnp.concatenate([wide, jnp.flip(partner, 1)], axis=1)
-    near = across(packed([chip[:, :, 1:17], mate[144:176]]))
-    pass_on = jnp.flip(near[:256].reshape(4, 4, 16, 128)[:, :3], 1)
-    mate_in = to_partner(pass_on)
+    reach = [chip[:, j, 1 + j : 17 - j] for j in range(4)]
+    near = across(packed(reach + [mate[144:176]]))
+    mate_in = to_partner(near[:168])
     f32, i32 = jnp.float32, jnp.int32
+    send_grad, slot = call(
+        stress_kernel,
+        [((experts * CAP, 6, 128), f32), ((16,), i32)],
+        [pltpu.VMEM((24, 128), f32), pltpu.VMEM((128, 128), f32), pltpu.SMEM((experts,), i32)],
+        (0, 1),
+        (core_arg, assignment.reshape(16), cot, low, high, edge, mate),
+        smem_outs=(1,),
+    )
+    got_grad = exchange(send_grad.reshape(experts, CAP * 6, 128), "yz")
     wide_rows = [pltpu.VMEM((12, 24, 128), f32)] * 3
-    send, own_state, visc, slot = call(
+    send, own_state, visc = call(
         forward_kernel,
-        [
-            ((experts * CAP, 16, 128), f32),
-            ((3, 2, 8, 128), f32),
-            ((12, 24, 128), f32),
-            ((16,), i32),
-        ],
-        [pltpu.VMEM((3, 12, 24, 128), f32)] * 2
-        + wide_rows
-        + [pltpu.VMEM((24, 128), f32), pltpu.VMEM((256, 128), f32), pltpu.SMEM((experts,), i32)],
+        [((experts * CAP, 9, 128), f32), ((3, 2, 8, 128), f32), ((12, 24, 128), f32)],
+        [pltpu.VMEM((3, 12, 24, 128), f32)] * 2 + wide_rows + [pltpu.VMEM((256, 128), f32)],
         (0, 1),
-        (core_arg, assignment.reshape(16), fields, cot, low, high, edge, mate, near, mate_in),
-        smem_outs=(3,),
+        (core_arg, slot, fields, low, high, mate, near, mate_in),
         vmem_outs=(1, 2),
     )
-    recv = exchange(send.reshape(experts, CAP * 16, 128), "yz")
-    recv = recv.reshape(experts * CAP, 16, 128)
+    recv = exchange(send.reshape(experts, CAP * 9, 128), "yz")
+    x = jnp.transpose(recv.reshape(experts * CAP, 9, 128), (1, 0, 2)).reshape(9, -1)
+    sg = jnp.transpose(got_grad.reshape(experts * CAP, 6, 128), (1, 0, 2)).reshape(6, -1)
 
     w1, w2, w3 = w_in[0], w_mid[0], w_out[0]
-    turn = jnp.transpose(recv, (1, 0, 2)).reshape(16, -1)
-    x = turn[:9]
-    sg = turn[9:15]
 
     def dot(a, b, ca, cb):
         return lax.dot_general(a, b, (((ca,), (cb,)), ((), ())), precision=PREC)

time: 191 us -> 200 us (1.047)
  blocking collectives: 13.6 us -> 0 us
  starting transfers between devices: 86.2 us -> 99.4 us
  waiting for transfers between devices: 59.2 us -> 65 us
  local copies, waits for them, and re-layouts: 6.19 us -> 9.51 us
    all_to_all x1 -> x0, blocking collectives: 13.6 us -> none  [exchange(): lax.all_to_all(value, axis, 0, 0, axis_index_groups=groups, tiled=True)]
    all_to_all x3 -> x5, starting transfers between devices: 17.3 us -> 30.4 us  [exchange(): lax.all_to_all(value, axis, 0, 0, axis_index_groups=groups, tiled=True)]
    all_to_all x3 -> x5, waiting for transfers between devices: 35.9 us -> 44.6 us  [exchange(): lax.all_to_all(value, axis, 0, 0, axis_index_groups=groups, tiled=True)]
    reshape x0 -> x4, local copies, waits for them, and re-layouts: none -> 3.25 us  [the longest x1 1.65 us: step(): recv = exchange(send.reshape(experts, CAP * 9, 128), 'yz')]
    ppermute x13, waiting for transfers between devices: 23.3 us -> 20.5 us  [permute(): return lax.ppermute(value, AXES, pairs)]
    pallas_call x3 -> x4, Pallas kernels: 8.97 us -> 9.93 us  [call(): pl.pallas_call(kernel, out_shape=[(pltpu.VMEM if i in vmem_outs else jax....]
  transfers between devices with their start and end apart: 16 -> 18, of which waited for: 12 -> 13; matrix products, arithmetic and copies ran while one was open for 2% -> 3% of each run, Pallas kernels for 0% -> 3%
where the time goes in v6:
time: 200 us; the launch traced here: 199 us
  starting transfers between devices  99.4 us (50%)
  waiting for transfers between devices  65 us (32%)
  matrix products  10.9 us (5%)
  Pallas kernels  9.93 us (5%)
  local copies, waits for them, and re-layouts  9.51 us (5%)
  other arithmetic  2.89 us (1%)
    ppermute x13, starting transfers between devices, permute(): return lax.ppermute(value, AXES, pairs)  69 us
    all_to_all x5, waiting for transfers between devices, exchange(): lax.all_to_all(value, axis, 0, 0, axis_index_groups=groups, tiled=True)  44.6 us
    all_to_all x5, starting transfers between devices, exchange(): lax.all_to_all(value, axis, 0, 0, axis_index_groups=groups, tiled=True)  30.4 us
    ppermute x13, waiting for transfers between devices, permute(): return lax.ppermute(value, AXES, pairs)  20.5 us
    dot_general x9, matrix products, dot(): return lax.dot_general(a, b, (((ca,), (cb,)), ((), ())), precision=PREC)  10.9 us
    pallas_call x4, Pallas kernels, call(): pl.pallas_call(kernel, out_shape=[(pltpu.VMEM if i in vmem_outs else jax....  9.93 us
  transfers between devices with their start and end apart: 18, of which 13 were waited for; matrix products, arithmetic and copies ran while one was open for 3% of the time, Pallas kernels for 3%

profile of v6, /device:TPU:1, one launch (start us, length us, event | category | flops | bytes accessed | tf_op | source)
XLA Modules:
  0.0 199.4 jit_solution(17324420947730586169)
XLA Ops:
  2.4 4.0 %collective-permute-start = (f32[46,128]{1,0:T(8,128)S(1)}, f32[46,128]{1,0:T(8,128)S(1)}, u32[]{:S(2)}, u32[]{:S(2)}) collective-permute-start(f32[46,128]{1,0:T(8,128)S(1)} %pad_maximum_fusion.34), channel_id=1, source_target_pairs={{0,1},{1,2},{2,3},{3,4},{4,5},{5,6},{6,7},{7,8},{8,9},{9,10},{10,1... | collective-permute-start | bytes 70664 | tf_op jit(solution)/shard_map/ppermute | solution.py:26
  6.4 7.4 %collective-permute-start.1 = (f32[46,128]{1,0:T(8,128)S(1)}, f32[46,128]{1,0:T(8,128)S(1)}, u32[]{:S(2)}, u32[]{:S(2)}) collective-permute-start(f32[46,128]{1,0:T(8,128)S(1)} %pad_maximum_fusion.35), channel_id=1, source_target_pairs={{0,15},{1,0},{2,1},{3,2},{4,3},{5,4},{6,5},{7,6},{8,7},{9,8},{10,9... | collective-permute-start | bytes 70664 | tf_op jit(solution)/shard_map/ppermute | solution.py:26
  13.9 9.7 %collective-permute-start.2 = (f32[56,128]{1,0:T(8,128)S(1)}, f32[56,128]{1,0:T(8,128)S(1)}, u32[]{:S(2)}, u32[]{:S(2)}) collective-permute-start(f32[56,128]{1,0:T(8,128)S(1)} %pad_maximum_fusion.21), channel_id=1, source_target_pairs={{0,496},{1,497},{2,498},{3,499},{4,500},{5,501},{6,502},{7,503},{8... | collective-permute-start | bytes 86024 | tf_op jit(solution)/shard_map/ppermute | solution.py:26
  25.2 7.0 %collective-permute-start.3 = (f32[200,128]{1,0:T(8,128)S(1)}, f32[200,128]{1,0:T(8,128)S(1)}, u32[]{:S(2)}, u32[]{:S(2)}) collective-permute-start(f32[200,128]{1,0:T(8,128)S(1)} %pad_maximum_fusion.3), channel_id=1, source_target_pairs={{0,16},{1,17},{2,18},{3,19},{4,20},{5,21},{6,22},{7,23},{8,24},{9,... | collective-permute-start | bytes 307208 | tf_op jit(solution)/shard_map/ppermute | solution.py:26
  36.2 3.6 %all-to-all-start = ((f32[16,12,128]{2,1,0:T(8,128)}), f32[16,12,128]{2,1,0:T(8,128)S(1)}, u32[]{:S(2)}, u32[]{:S(2)}) async-start(f32[16,12,128]{2,1,0:T(8,128)} %reshape.209), calls=%async_computation | async-start | bytes 262144 | tf_op jit(solution)/shard_map/all_to_all | solution.py:30
  39.9 3.1 %collective-permute-start.4 = (f32[240,128]{1,0:T(8,128)S(1)}, f32[240,128]{1,0:T(8,128)S(1)}, u32[]{:S(2)}, u32[]{:S(2)}) collective-permute-start(f32[240,128]{1,0:T(8,128)S(1)} %constant_dynamic-update-slice_fusion), channel_id=1, source_target_pairs={{0,496},{1,497},{2,498},{3,499},{4,500},{5,501},{6,502},{7,503},{8... | collective-permute-start | bytes 368648 | tf_op jit(solution)/shard_map/ppermute | solution.py:26
  43.0 7.0 %collective-permute-done.4.near = f32[240,128]{1,0:T(8,128)S(1)} collective-permute-done((f32[240,128]{1,0:T(8,128)S(1)}, f32[240,128]{1,0:T(8,128)S(1)}, u32[]{:S(2)}, u32[]{:S(2)}) %collective-permute-start.4) | collective-permute-done | bytes 122912 | tf_op jit(solution)/shard_map/ppermute | solution.py:26
  50.0 6.6 %collective-permute-start.5 = (f32[168,128]{1,0:T(8,128)S(1)}, f32[168,128]{1,0:T(8,128)S(1)}, u32[]{:S(2)}, u32[]{:S(2)}) collective-permute-start(f32[168,128]{1,0:T(8,128)S(1)} %slice.400), channel_id=1, source_target_pairs={{0,16},{1,17},{2,18},{3,19},{4,20},{5,21},{6,22},{7,23},{8,24},{9,... | collective-permute-start | bytes 258056 | tf_op jit(solution)/shard_map/ppermute | solution.py:26
  57.5 5.5 %shard_map.162 = (f32[32,9,128]{2,1,0:T(8,128)}, f32[3,2,8,128]{3,2,1,0:T(8,128)S(1)}, f32[12,24,128]{2,1,0:T(8,128)S(1)}) custom-call(s32[1]{0:T(128)} %bitcast.core_ref, s32[16]{0:T(128)} %get-tuple-element.19.slot_ref, f32[4,2,8,128]{3,2,1,0:T(8,128)S(1)} %pad_maximum_fusion.16.fields, f32[46,128]{1,0:T(8,128)S(1)} %collective-permute-done.low, ...), custom_call_target="tpu_custom_call" | custom-call | tf_op jit(solution)/shard_map/pallas_call | solution.py:73
  64.6 8.8 %all-to-all-start.1 = ((f32[16,18,128]{2,1,0:T(8,128)}), f32[16,18,128]{2,1,0:T(8,128)S(1)}, u32[]{:S(2)}, u32[]{:S(2)}) async-start(f32[16,18,128]{2,1,0:T(8,128)} %reshape.212), calls=%async_computation.1 | async-start | bytes 393216 | tf_op jit(solution)/shard_map/all_to_all | solution.py:30
  73.7 8.6 %all-to-all-done.1 = f32[16,18,128]{2,1,0:T(8,128)S(1)} async-done(((f32[16,18,128]{2,1,0:T(8,128)}), f32[16,18,128]{2,1,0:T(8,128)S(1)}, u32[]{:S(2)}, u32[]{:S(2)}) %all-to-all-start.1) | async-done | bytes 147488 | tf_op jit(solution)/shard_map/all_to_all | solution.py:30
  93.5 3.6 %collective-permute-start.12 = (f32[146,128]{1,0:T(8,128)S(1)}, f32[146,128]{1,0:T(8,128)S(1)}, u32[]{:S(2)}, u32[]{:S(2)}) collective-permute-start(f32[146,128]{1,0:T(8,128)S(1)} %concatenate.133), channel_id=1, source_target_pairs={{0,16},{1,17},{2,18},{3,19},{4,20},{5,21},{6,22},{7,23},{8,24},{9,... | collective-permute-start | bytes 224264 | tf_op jit(solution)/shard_map/ppermute | solution.py:26
  98.7 7.8 %all-to-all-start.3 = ((f32[16,10,128]{2,1,0:T(8,128)}), f32[16,10,128]{2,1,0:T(8,128)S(1)}, u32[]{:S(2)}, u32[]{:S(2)}) async-start(f32[16,10,128]{2,1,0:T(8,128)} %reshape.244), calls=%async_computation.3 | async-start | bytes 262144 | tf_op jit(solution)/shard_map/all_to_all | solution.py:30
  109.0 12.7 %all-to-all-done.3 = f32[16,10,128]{2,1,0:T(8,128)S(1)} async-done(((f32[16,10,128]{2,1,0:T(8,128)}), f32[16,10,128]{2,1,0:T(8,128)S(1)}, u32[]{:S(2)}, u32[]{:S(2)}) %all-to-all-start.3) | async-done | bytes 81952 | tf_op jit(solution)/shard_map/all_to_all | solution.py:30
  122.4 4.3 %all-to-all-start.4 = ((f32[16,10,128]{2,1,0:T(8,128)}), f32[16,10,128]{2,1,0:T(8,128)S(1)}, u32[]{:S(2)}, u32[]{:S(2)}) async-start(f32[16,10,128]{2,1,0:T(8,128)} %broadcast_in_dim.31), calls=%async_computation.4 | async-start | bytes 262144 | tf_op jit(solution)/shard_map/all_to_all | solution.py:30
  127.8 14.8 %all-to-all-done.4 = f32[16,10,128]{2,1,0:T(8,128)S(1)} async-done(((f32[16,10,128]{2,1,0:T(8,128)}), f32[16,10,128]{2,1,0:T(8,128)S(1)}, u32[]{:S(2)}, u32[]{:S(2)}) %all-to-all-start.4) | async-done | bytes 81952 | tf_op jit(solution)/shard_map/all_to_all | solution.py:30
  142.6 5.8 %all-to-all-start.2 = ((f32[16,30,128]{2,1,0:T(8,128)}), f32[16,30,128]{2,1,0:T(8,128)S(1)}, u32[]{:S(2)}, u32[]{:S(2)}) async-start(f32[16,30,128]{2,1,0:T(8,128)} %reshape.216), calls=%async_computation.2 | async-start | bytes 524288 | tf_op jit(solution)/shard_map/all_to_all | solution.py:30
  149.1 8.3 %all-to-all-done.2 = f32[16,30,128]{2,1,0:T(8,128)S(1)} async-done(((f32[16,30,128]{2,1,0:T(8,128)}), f32[16,30,128]{2,1,0:T(8,128)S(1)}, u32[]{:S(2)}, u32[]{:S(2)}) %all-to-all-start.2) | async-done | bytes 245792 | tf_op jit(solution)/shard_map/all_to_all | solution.py:30
  158.5 3.6 %collective-permute-start.8 = (f32[48,128]{1,0:T(8,128)S(1)}, f32[48,128]{1,0:T(8,128)S(1)}, u32[]{:S(2)}, u32[]{:S(2)}) collective-permute-start(f32[48,128]{1,0:T(8,128)S(1)} %pad_maximum_fusion.37), channel_id=1, source_target_pairs={{0,496},{1,497},{2,498},{3,499},{4,500},{5,501},{6,502},{7,503},{8... | collective-permute-start | bytes 73736 | tf_op jit(solution)/shard_map/ppermute | solution.py:26
  164.4 7.0 %collective-permute-start.7 = (f32[84,128]{1,0:T(8,128)S(1)}, f32[84,128]{1,0:T(8,128)S(1)}, u32[]{:S(2)}, u32[]{:S(2)}) collective-permute-start(f32[84,128]{1,0:T(8,128)S(1)} %pad_maximum_fusion.20), channel_id=1, source_target_pairs={{0,15},{1,0},{2,1},{3,2},{4,3},{5,4},{6,5},{7,6},{8,7},{9,8},{10,9... | collective-permute-start | bytes 129032 | tf_op jit(solution)/shard_map/ppermute | solution.py:26
  172.7 4.0 %collective-permute-start.9 = (f32[240,128]{1,0:T(8,128)S(1)}, f32[240,128]{1,0:T(8,128)S(1)}, u32[]{:S(2)}, u32[]{:S(2)}) collective-permute-start(f32[240,128]{1,0:T(8,128)S(1)} %pad_maximum_fusion.1), channel_id=1, source_target_pairs={{0,16},{1,17},{2,18},{3,19},{4,20},{5,21},{6,22},{7,23},{8,24},{9,... | collective-permute-start | bytes 368648 | tf_op jit(solution)/shard_map/ppermute | solution.py:26
  177.7 5.3 %collective-permute-start.10 = (f32[240,128]{1,0:T(8,128)S(1)}, f32[240,128]{1,0:T(8,128)S(1)}, u32[]{:S(2)}, u32[]{:S(2)}) collective-permute-start(f32[240,128]{1,0:T(8,128)S(1)} %pad_maximum_fusion.2), channel_id=1, source_target_pairs={{0,496},{1,497},{2,498},{3,499},{4,500},{5,501},{6,502},{7,503},{8... | collective-permute-start | bytes 368648 | tf_op jit(solution)/shard_map/ppermute | solution.py:26
  183.8 6.5 %collective-permute-done.10 = f32[240,128]{1,0:T(8,128)S(1)} collective-permute-done((f32[240,128]{1,0:T(8,128)S(1)}, f32[240,128]{1,0:T(8,128)S(1)}, u32[]{:S(2)}, u32[]{:S(2)}) %collective-permute-start.10) | collective-permute-done | bytes 122912 | tf_op jit(solution)/shard_map/ppermute | solution.py:26
  190.4 5.6 %collective-permute-start.11 = (f32[144,128]{1,0:T(8,128)S(1)}, f32[144,128]{1,0:T(8,128)S(1)}, u32[]{:S(2)}, u32[]{:S(2)}) collective-permute-start(f32[144,128]{1,0:T(8,128)S(1)} %pad_maximum_fusion.15), channel_id=1, source_target_pairs={{0,16},{1,17},{2,18},{3,19},{4,20},{5,21},{6,22},{7,23},{8,24},{9,... | collective-permute-start | bytes 221192 | tf_op jit(solution)/shard_map/ppermute | solution.py:26
  (171 shorter events, 36.9 us)
Async XLA Ops:
  0.6 83.9 %copy-start = (f32[1,128,128]{2,1,0:T(8,128)S(1)}, f32[1,128,128]{2,1,0:T(8,128)}, u32[]{:S(2)}) copy-start(f32[1,128,128]{2,1,0:T(8,128)} %param.16) | copy-start | bytes 196612
  2.4 21.2 %collective-permute-start = (f32[46,128]{1,0:T(8,128)S(1)}, f32[46,128]{1,0:T(8,128)S(1)}, u32[]{:S(2)}, u32[]{:S(2)}) collective-permute-start(f32[46,128]{1,0:T(8,128)S(1)} %pad_maximum_fusion.34), channel_id=1, source_target_pairs={{0,1},{1,2},{2,3},{3,4},{4,5},{5,6},{6,7},{7,8},{8,9},{9,10},{10,1... | collective-permute-start | bytes 70664 | tf_op jit(solution)/shard_map/ppermute | solution.py:26
  6.4 17.2 %collective-permute-start.1 = (f32[46,128]{1,0:T(8,128)S(1)}, f32[46,128]{1,0:T(8,128)S(1)}, u32[]{:S(2)}, u32[]{:S(2)}) collective-permute-start(f32[46,128]{1,0:T(8,128)S(1)} %pad_maximum_fusion.35), channel_id=1, source_target_pairs={{0,15},{1,0},{2,1},{3,2},{4,3},{5,4},{6,5},{7,6},{8,7},{9,8},{10,9... | collective-permute-start | bytes 70664 | tf_op jit(solution)/shard_map/ppermute | solution.py:26
  13.9 11.3 %collective-permute-start.2 = (f32[56,128]{1,0:T(8,128)S(1)}, f32[56,128]{1,0:T(8,128)S(1)}, u32[]{:S(2)}, u32[]{:S(2)}) collective-permute-start(f32[56,128]{1,0:T(8,128)S(1)} %pad_maximum_fusion.21), channel_id=1, source_target_pairs={{0,496},{1,497},{2,498},{3,499},{4,500},{5,501},{6,502},{7,503},{8... | collective-permute-start | bytes 86024 | tf_op jit(solution)/shard_map/ppermute | solution.py:26
  25.2 7.9 %collective-permute-start.3 = (f32[200,128]{1,0:T(8,128)S(1)}, f32[200,128]{1,0:T(8,128)S(1)}, u32[]{:S(2)}, u32[]{:S(2)}) collective-permute-start(f32[200,128]{1,0:T(8,128)S(1)} %pad_maximum_fusion.3), channel_id=1, source_target_pairs={{0,16},{1,17},{2,18},{3,19},{4,20},{5,21},{6,22},{7,23},{8,24},{9,... | collective-permute-start | bytes 307208 | tf_op jit(solution)/shard_map/ppermute | solution.py:26
  36.2 46.5 %copy-start.3 = (f32[1,9,128]{2,0,1:T(1,128)S(1)}, f32[1,9,128]{2,0,1:T(1,128)}, u32[]{:S(2)}) copy-start(f32[1,9,128]{2,0,1:T(1,128)} %param.14) | copy-start | bytes 13828
  36.2 46.5 %copy-start.8 = (f32[1,128]{1,0:T(1,128)S(1)}, f32[1,128]{1,0:T(1,128)}, u32[]{:S(2)}) copy-start(f32[1,128]{1,0:T(1,128)} %param.15) | copy-start | bytes 1540
  36.2 28.4 %all-to-all-start = ((f32[16,12,128]{2,1,0:T(8,128)}), f32[16,12,128]{2,1,0:T(8,128)S(1)}, u32[]{:S(2)}, u32[]{:S(2)}) async-start(f32[16,12,128]{2,1,0:T(8,128)} %reshape.209), calls=%async_computation | async-start | bytes 262144 | tf_op jit(solution)/shard_map/all_to_all | solution.py:30
  39.9 10.1 %collective-permute-start.4 = (f32[240,128]{1,0:T(8,128)S(1)}, f32[240,128]{1,0:T(8,128)S(1)}, u32[]{:S(2)}, u32[]{:S(2)}) collective-permute-start(f32[240,128]{1,0:T(8,128)S(1)} %constant_dynamic-update-slice_fusion), channel_id=1, source_target_pairs={{0,496},{1,497},{2,498},{3,499},{4,500},{5,501},{6,502},{7,503},{8... | collective-permute-start | bytes 368648 | tf_op jit(solution)/shard_map/ppermute | solution.py:26
  50.0 7.5 %collective-permute-start.5 = (f32[168,128]{1,0:T(8,128)S(1)}, f32[168,128]{1,0:T(8,128)S(1)}, u32[]{:S(2)}, u32[]{:S(2)}) collective-permute-start(f32[168,128]{1,0:T(8,128)S(1)} %slice.400), channel_id=1, source_target_pairs={{0,16},{1,17},{2,18},{3,19},{4,20},{5,21},{6,22},{7,23},{8,24},{9,... | collective-permute-start | bytes 258056 | tf_op jit(solution)/shard_map/ppermute | solution.py:26
  64.6 17.7 %all-to-all-start.1 = ((f32[16,18,128]{2,1,0:T(8,128)}), f32[16,18,128]{2,1,0:T(8,128)S(1)}, u32[]{:S(2)}, u32[]{:S(2)}) async-start(f32[16,18,128]{2,1,0:T(8,128)} %reshape.212), calls=%async_computation.1 | async-start | bytes 393216 | tf_op jit(solution)/shard_map/all_to_all | solution.py:30
  73.7 10.8 %copy-start.5 = (f32[1,128]{1,0:T(1,128)S(1)}, f32[1,128]{1,0:T(1,128)}, u32[]{:S(2)}) copy-start(f32[1,128]{1,0:T(1,128)} %param.17) | copy-start | bytes 1540
  91.1 15.4 %copy-start.6 = (f32[1,6]{1,0:T(1,128)S(1)}, f32[1,6]{1,0:T(1,128)}, u32[]{:S(2)}) copy-start(f32[1,6]{1,0:T(1,128)} %param.19) | copy-start | bytes 76
  93.5 4.5 %collective-permute-start.12 = (f32[146,128]{1,0:T(8,128)S(1)}, f32[146,128]{1,0:T(8,128)S(1)}, u32[]{:S(2)}, u32[]{:S(2)}) collective-permute-start(f32[146,128]{1,0:T(8,128)S(1)} %concatenate.133), channel_id=1, source_target_pairs={{0,16},{1,17},{2,18},{3,19},{4,20},{5,21},{6,22},{7,23},{8,24},{9,... | collective-permute-start | bytes 224264 | tf_op jit(solution)/shard_map/ppermute | solution.py:26
  98.7 23.1 %all-to-all-start.3 = ((f32[16,10,128]{2,1,0:T(8,128)}), f32[16,10,128]{2,1,0:T(8,128)S(1)}, u32[]{:S(2)}, u32[]{:S(2)}) async-start(f32[16,10,128]{2,1,0:T(8,128)} %reshape.244), calls=%async_computation.3 | async-start | bytes 262144 | tf_op jit(solution)/shard_map/all_to_all | solution.py:30
  109.0 39.4 %copy-start.7 = (s32[16]{0:T(128)S(1)}, s32[16]{0:T(128)}, u32[]{:S(2)}) copy-start(s32[16]{0:T(128)} %get-tuple-element.19.slot_ref) | copy-start | bytes 196
  122.4 20.1 %all-to-all-start.4 = ((f32[16,10,128]{2,1,0:T(8,128)}), f32[16,10,128]{2,1,0:T(8,128)S(1)}, u32[]{:S(2)}, u32[]{:S(2)}) async-start(f32[16,10,128]{2,1,0:T(8,128)} %broadcast_in_dim.31), calls=%async_computation.4 | async-start | bytes 262144 | tf_op jit(solution)/shard_map/all_to_all | solution.py:30
  142.6 14.8 %all-to-all-start.2 = ((f32[16,30,128]{2,1,0:T(8,128)}), f32[16,30,128]{2,1,0:T(8,128)S(1)}, u32[]{:S(2)}, u32[]{:S(2)}) async-start(f32[16,30,128]{2,1,0:T(8,128)} %reshape.216), calls=%async_computation.2 | async-start | bytes 524288 | tf_op jit(solution)/shard_map/all_to_all | solution.py:30
  158.5 13.0 %collective-permute-start.8 = (f32[48,128]{1,0:T(8,128)S(1)}, f32[48,128]{1,0:T(8,128)S(1)}, u32[]{:S(2)}, u32[]{:S(2)}) collective-permute-start(f32[48,128]{1,0:T(8,128)S(1)} %pad_maximum_fusion.37), channel_id=1, source_target_pairs={{0,496},{1,497},{2,498},{3,499},{4,500},{5,501},{6,502},{7,503},{8... | collective-permute-start | bytes 73736 | tf_op jit(solution)/shard_map/ppermute | solution.py:26
  162.2 9.2 %collective-permute-start.6 = (f32[84,128]{1,0:T(8,128)S(1)}, f32[84,128]{1,0:T(8,128)S(1)}, u32[]{:S(2)}, u32[]{:S(2)}) collective-permute-start(f32[84,128]{1,0:T(8,128)S(1)} %pad_maximum_fusion.19), channel_id=1, source_target_pairs={{0,1},{1,2},{2,3},{3,4},{4,5},{5,6},{6,7},{7,8},{8,9},{9,10},{10,1... | collective-permute-start | bytes 129032 | tf_op jit(solution)/shard_map/ppermute | solution.py:26
  164.4 8.1 %collective-permute-start.7 = (f32[84,128]{1,0:T(8,128)S(1)}, f32[84,128]{1,0:T(8,128)S(1)}, u32[]{:S(2)}, u32[]{:S(2)}) collective-permute-start(f32[84,128]{1,0:T(8,128)S(1)} %pad_maximum_fusion.20), channel_id=1, source_target_pairs={{0,15},{1,0},{2,1},{3,2},{4,3},{5,4},{6,5},{7,6},{8,7},{9,8},{10,9... | collective-permute-start | bytes 129032 | tf_op jit(solution)/shard_map/ppermute | solution.py:26
  172.7 4.9 %collective-permute-start.9 = (f32[240,128]{1,0:T(8,128)S(1)}, f32[240,128]{1,0:T(8,128)S(1)}, u32[]{:S(2)}, u32[]{:S(2)}) collective-permute-start(f32[240,128]{1,0:T(8,128)S(1)} %pad_maximum_fusion.1), channel_id=1, source_target_pairs={{0,16},{1,17},{2,18},{3,19},{4,20},{5,21},{6,22},{7,23},{8,24},{9,... | collective-permute-start | bytes 368648 | tf_op jit(solution)/shard_map/ppermute | solution.py:26
  177.7 12.6 %collective-permute-start.10 = (f32[240,128]{1,0:T(8,128)S(1)}, f32[240,128]{1,0:T(8,128)S(1)}, u32[]{:S(2)}, u32[]{:S(2)}) collective-permute-start(f32[240,128]{1,0:T(8,128)S(1)} %pad_maximum_fusion.2), channel_id=1, source_target_pairs={{0,496},{1,497},{2,498},{3,499},{4,500},{5,501},{6,502},{7,503},{8... | collective-permute-start | bytes 368648 | tf_op jit(solution)/shard_map/ppermute | solution.py:26
  190.4 6.5 %collective-permute-start.11 = (f32[144,128]{1,0:T(8,128)S(1)}, f32[144,128]{1,0:T(8,128)S(1)}, u32[]{:S(2)}, u32[]{:S(2)}) collective-permute-start(f32[144,128]{1,0:T(8,128)S(1)} %pad_maximum_fusion.15), channel_id=1, source_target_pairs={{0,16},{1,17},{2,18},{3,19},{4,20},{5,21},{6,22},{7,23},{8,24},{9,... | collective-permute-start | bytes 221192 | tf_op jit(solution)/shard_map/ppermute | solution.py:26
  (3 other events, 3.7 us)

commit v7 on v6

--- a/solution.py
+++ b/solution.py
@@ -127,11 +127,11 @@
 
 
 def stress_kernel(
-    core_ref, owner_ref, cot, low, high, edge, mate, send, slot_ref, c_wide, columns, count
+    core_ref, owner_ref, cot, low, high, edge, mate, columns, slot_ref, c_wide, count
 ):
     core = core_ref[0]
     half = 0.5 * (1 - 2 * core).astype(jnp.float32)
-    send[...] = jnp.zeros_like(send)
+    columns[96:112] = jnp.zeros((16, 128), jnp.float32)
     placed(core, owner_ref, slot_ref, count)
     for x in range(2):
         d = []
@@ -153,18 +153,14 @@
         )
         for k in range(6):
             columns[k * 16 + x * 8 : k * 16 + x * 8 + 8] = SCALE * grads[k]
-    for k in range(16):
-        send[slot_ref[k]] = columns[pl.ds(k, 6, stride=16)]
 
 
 def forward_kernel(
-    core_ref, slot_ref, fields, low, high, mate, near, mate_in,
+    core_ref, slot_ref, grad_columns, fields, low, high, mate, near, mate_in,
     send, own_state, visc,
     work, spare, kx, ky, kz, columns,
 ):
     half = 0.5 * (1 - 2 * core_ref[0]).astype(jnp.float32)
-    work[...] = jnp.zeros_like(work)
-    visc[...] = jnp.zeros_like(visc)
     send[...] = jnp.zeros_like(send)
     for f in range(4):
         row = (lambda i, f=f: visc.at[i]) if f == 3 else (lambda i, f=f: work.at[f, i])
@@ -190,12 +186,12 @@
             columns[at : at + 8] = half * (state[c, 6 + x, 8:16] - state[c, 4 + x, 8:16])
             columns[at + 16 : at + 24] = 0.5 * (state[c, 5 + x, 9:17] - state[c, 5 + x, 7:15])
             columns[at + 32 : at + 40] = 0.5 * (turned(own, -1, 1) - turned(own, 1, 1))
+    columns[144:256] = grad_columns[...]
     for k in range(16):
-        send[slot_ref[k]] = columns[pl.ds(k, 9, stride=16)]
+        send[slot_ref[k]] = columns[pl.ds(k, 16, stride=16)]
 
 
 def adjoint_kernel(core_ref, adjoint, visc, out, work, spare, kx, ky, kz):
-    work[...] = jnp.zeros_like(work)
     for c in range(3):
         for i in range(10):
             work[c, i, 4:20] = adjoint[c, i]
@@ -247,27 +243,27 @@
     near = across(packed(reach + [mate[144:176]]))
     mate_in = to_partner(near[:168])
     f32, i32 = jnp.float32, jnp.int32
-    send_grad, slot = call(
+    grad_columns, slot = call(
         stress_kernel,
-        [((experts * CAP, 6, 128), f32), ((16,), i32)],
-        [pltpu.VMEM((24, 128), f32), pltpu.VMEM((128, 128), f32), pltpu.SMEM((experts,), i32)],
+        [((112, 128), f32), ((16,), i32)],
+        [pltpu.VMEM((24, 128), f32), pltpu.SMEM((experts,), i32)],
         (0, 1),
         (core_arg, assignment.reshape(16), cot, low, high, edge, mate),
         smem_outs=(1,),
-    )
-    got_grad = exchange(send_grad.reshape(experts, CAP * 6, 128), "yz")
+        vmem_outs=(0,),
+    )
     wide_rows = [pltpu.VMEM((12, 24, 128), f32)] * 3
     send, own_state, visc = call(
         forward_kernel,
-        [((experts * CAP, 9, 128), f32), ((3, 2, 8, 128), f32), ((12, 24, 128), f32)],
+        [((experts * CAP, 16, 128), f32), ((3, 2, 8, 128), f32), ((12, 24, 128), f32)],
         [pltpu.VMEM((3, 12, 24, 128), f32)] * 2 + wide_rows + [pltpu.VMEM((256, 128), f32)],
         (0, 1),
-        (core_arg, slot, fields, low, high, mate, near, mate_in),
+        (core_arg, slot, grad_columns, fields, low, high, mate, near, mate_in),
         vmem_outs=(1, 2),
     )
-    recv = exchange(send.reshape(experts, CAP * 9, 128), "yz")
-    x = jnp.transpose(recv.reshape(experts * CAP, 9, 128), (1, 0, 2)).reshape(9, -1)
-    sg = jnp.transpose(got_grad.reshape(experts * CAP, 6, 128), (1, 0, 2)).reshape(6, -1)
+    recv = exchange(send.reshape(experts, CAP * 16, 128), "yz")
+    turn = jnp.transpose(recv.reshape(experts * CAP, 16, 128), (1, 0, 2)).reshape(16, -1)
+    x, sg = turn[:9], turn[9:15]
 
     w1, w2, w3 = w_in[0], w_mid[0], w_out[0]
 

time: 200 us -> 189 us (0.945)
  blocking collectives: 0 us -> 14.1 us
  starting transfers between devices: 99.4 us -> 85.5 us
  waiting for transfers between devices: 65 us -> 57 us
  local copies, waits for them, and re-layouts: 9.51 us -> 6.25 us
    all_to_all x0 -> x1, blocking collectives: none -> 14.1 us  [exchange(): lax.all_to_all(value, axis, 0, 0, axis_index_groups=groups, tiled=True)]
    all_to_all x5 -> x3, starting transfers between devices: 30.4 us -> 16.8 us  [exchange(): lax.all_to_all(value, axis, 0, 0, axis_index_groups=groups, tiled=True)]
    all_to_all x5 -> x3, waiting for transfers between devices: 44.6 us -> 35.9 us  [exchange(): lax.all_to_all(value, axis, 0, 0, axis_index_groups=groups, tiled=True)]
    reshape x4 -> x0, local copies, waits for them, and re-layouts: 3.25 us -> none  [the longest x1 1.65 us: step(): recv = exchange(send.reshape(experts, CAP * 9, 128), 'yz')]
  transfers between devices with their start and end apart: 18 -> 16, of which waited for: 13 -> 11; matrix products, arithmetic and copies ran while one was open for 3% -> 2% of each run, Pallas kernels for 3% -> 1%
where the time goes in v7:
time: 189 us; the launch traced here: 188 us
  starting transfers between devices  85.5 us (45%)
  waiting for transfers between devices  57 us (30%)
  blocking collectives  14.1 us (7%)
  matrix products  10.8 us (6%)
  Pallas kernels  9.8 us (5%)
  local copies, waits for them, and re-layouts  6.25 us (3%)
  other arithmetic  2.91 us (2%)
    ppermute x13, starting transfers between devices, permute(): return lax.ppermute(value, AXES, pairs)  68.7 us
    all_to_all x3, waiting for transfers between devices, exchange(): lax.all_to_all(value, axis, 0, 0, axis_index_groups=groups, tiled=True)  35.9 us
    ppermute x13, waiting for transfers between devices, permute(): return lax.ppermute(value, AXES, pairs)  21.1 us
    all_to_all x3, starting transfers between devices, exchange(): lax.all_to_all(value, axis, 0, 0, axis_index_groups=groups, tiled=True)  16.8 us
    all_to_all x1, blocking collectives, exchange(): lax.all_to_all(value, axis, 0, 0, axis_index_groups=groups, tiled=True)  14.1 us
    dot_general x9, matrix products, dot(): return lax.dot_general(a, b, (((ca,), (cb,)), ((), ())), precision=PREC)  10.8 us
    pallas_call x4, Pallas kernels, call(): pl.pallas_call(kernel, out_shape=[(pltpu.VMEM if i in vmem_outs else jax....  9.8 us
  transfers between devices with their start and end apart: 16, of which 11 were waited for; matrix products, arithmetic and copies ran while one was open for 2% of the time, Pallas kernels for 1%

profile of v7, /device:TPU:1, one launch (start us, length us, event | category | flops | bytes accessed | tf_op | source)
XLA Modules:
  0.0 188.0 jit_solution(5414648733435221943)
XLA Ops:
  2.4 4.0 %collective-permute-start = (f32[46,128]{1,0:T(8,128)S(1)}, f32[46,128]{1,0:T(8,128)S(1)}, u32[]{:S(2)}, u32[]{:S(2)}) collective-permute-start(f32[46,128]{1,0:T(8,128)S(1)} %pad_maximum_fusion.34), channel_id=1, source_target_pairs={{0,1},{1,2},{2,3},{3,4},{4,5},{5,6},{6,7},{7,8},{8,9},{9,10},{10,1... | collective-permute-start | bytes 70664 | tf_op jit(solution)/shard_map/ppermute | solution.py:26
  6.4 7.4 %collective-permute-start.1 = (f32[46,128]{1,0:T(8,128)S(1)}, f32[46,128]{1,0:T(8,128)S(1)}, u32[]{:S(2)}, u32[]{:S(2)}) collective-permute-start(f32[46,128]{1,0:T(8,128)S(1)} %pad_maximum_fusion.35), channel_id=1, source_target_pairs={{0,15},{1,0},{2,1},{3,2},{4,3},{5,4},{6,5},{7,6},{8,7},{9,8},{10,9... | collective-permute-start | bytes 70664 | tf_op jit(solution)/shard_map/ppermute | solution.py:26
  13.9 9.7 %collective-permute-start.2 = (f32[56,128]{1,0:T(8,128)S(1)}, f32[56,128]{1,0:T(8,128)S(1)}, u32[]{:S(2)}, u32[]{:S(2)}) collective-permute-start(f32[56,128]{1,0:T(8,128)S(1)} %pad_maximum_fusion.21), channel_id=1, source_target_pairs={{0,496},{1,497},{2,498},{3,499},{4,500},{5,501},{6,502},{7,503},{8... | collective-permute-start | bytes 86024 | tf_op jit(solution)/shard_map/ppermute | solution.py:26
  25.2 7.0 %collective-permute-start.3 = (f32[200,128]{1,0:T(8,128)S(1)}, f32[200,128]{1,0:T(8,128)S(1)}, u32[]{:S(2)}, u32[]{:S(2)}) collective-permute-start(f32[200,128]{1,0:T(8,128)S(1)} %pad_maximum_fusion.3), channel_id=1, source_target_pairs={{0,16},{1,17},{2,18},{3,19},{4,20},{5,21},{6,22},{7,23},{8,24},{9,... | collective-permute-start | bytes 307208 | tf_op jit(solution)/shard_map/ppermute | solution.py:26
  33.2 3.1 %collective-permute-start.4 = (f32[240,128]{1,0:T(8,128)S(1)}, f32[240,128]{1,0:T(8,128)S(1)}, u32[]{:S(2)}, u32[]{:S(2)}) collective-permute-start(f32[240,128]{1,0:T(8,128)S(1)} %constant_dynamic-update-slice_fusion), channel_id=1, source_target_pairs={{0,496},{1,497},{2,498},{3,499},{4,500},{5,501},{6,502},{7,503},{8... | collective-permute-start | bytes 368648 | tf_op jit(solution)/shard_map/ppermute | solution.py:26
  36.3 8.7 %collective-permute-done.4.near = f32[240,128]{1,0:T(8,128)S(1)} collective-permute-done((f32[240,128]{1,0:T(8,128)S(1)}, f32[240,128]{1,0:T(8,128)S(1)}, u32[]{:S(2)}, u32[]{:S(2)}) %collective-permute-start.4) | collective-permute-done | bytes 122912 | tf_op jit(solution)/shard_map/ppermute | solution.py:26
  45.0 6.6 %collective-permute-start.5 = (f32[168,128]{1,0:T(8,128)S(1)}, f32[168,128]{1,0:T(8,128)S(1)}, u32[]{:S(2)}, u32[]{:S(2)}) collective-permute-start(f32[168,128]{1,0:T(8,128)S(1)} %slice.416), channel_id=1, source_target_pairs={{0,16},{1,17},{2,18},{3,19},{4,20},{5,21},{6,22},{7,23},{8,24},{9,... | collective-permute-start | bytes 258056 | tf_op jit(solution)/shard_map/ppermute | solution.py:26
  52.9 5.5 %shard_map.162 = (f32[32,16,128]{2,1,0:T(8,128)}, f32[3,2,8,128]{3,2,1,0:T(8,128)S(1)}, f32[12,24,128]{2,1,0:T(8,128)S(1)}) custom-call(s32[1]{0:T(128)} %bitcast.core_ref, s32[16]{0:T(128)} %get-tuple-element.19.slot_ref, f32[112,128]{1,0:T(8,128)S(1)} %get-tuple-element.20.grad_columns, f32[4,2,8,128]{3,2,1,0:T(8,128)S(1)} %pad_maximum_fusion.16.fields, ...), custom_call_target="tpu_custom_call" | custom-call | tf_op jit(solution)/shard_map/pallas_call | solution.py:73
  58.5 14.1 %all_to_all.20 = f32[16,32,128]{2,1,0:T(8,128)S(1)} all-to-all(f32[16,32,128]{2,1,0:T(8,128)} %bitcast.157), channel_id=1, replica_groups=mesh['gx'=32,'yz'=16] {'yz'}, dimensions={0} | all-to-all | bytes 524288 | tf_op jit(solution)/shard_map/all_to_all | solution.py:30
  83.8 3.2 %collective-permute-start.12 = (f32[146,128]{1,0:T(8,128)S(1)}, f32[146,128]{1,0:T(8,128)S(1)}, u32[]{:S(2)}, u32[]{:S(2)}) collective-permute-start(f32[146,128]{1,0:T(8,128)S(1)} %concatenate.133), channel_id=1, source_target_pairs={{0,16},{1,17},{2,18},{3,19},{4,20},{5,21},{6,22},{7,23},{8,24},{9,... | collective-permute-start | bytes 224264 | tf_op jit(solution)/shard_map/ppermute | solution.py:26
  88.4 6.6 %all-to-all-start.2 = ((f32[16,10,128]{2,1,0:T(8,128)}), f32[16,10,128]{2,1,0:T(8,128)S(1)}, u32[]{:S(2)}, u32[]{:S(2)}) async-start(f32[16,10,128]{2,1,0:T(8,128)} %reshape.230), calls=%async_computation.2 | async-start | bytes 262144 | tf_op jit(solution)/shard_map/all_to_all | solution.py:30
  97.5 12.7 %all-to-all-done.2 = f32[16,10,128]{2,1,0:T(8,128)S(1)} async-done(((f32[16,10,128]{2,1,0:T(8,128)}), f32[16,10,128]{2,1,0:T(8,128)S(1)}, u32[]{:S(2)}, u32[]{:S(2)}) %all-to-all-start.2) | async-done | bytes 81952 | tf_op jit(solution)/shard_map/all_to_all | solution.py:30
  110.9 4.6 %all-to-all-start.3 = ((f32[16,10,128]{2,1,0:T(8,128)}), f32[16,10,128]{2,1,0:T(8,128)S(1)}, u32[]{:S(2)}, u32[]{:S(2)}) async-start(f32[16,10,128]{2,1,0:T(8,128)} %broadcast_in_dim.31), calls=%async_computation.3 | async-start | bytes 262144 | tf_op jit(solution)/shard_map/all_to_all | solution.py:30
  116.5 14.9 %all-to-all-done.3 = f32[16,10,128]{2,1,0:T(8,128)S(1)} async-done(((f32[16,10,128]{2,1,0:T(8,128)}), f32[16,10,128]{2,1,0:T(8,128)S(1)}, u32[]{:S(2)}, u32[]{:S(2)}) %all-to-all-start.3) | async-done | bytes 81952 | tf_op jit(solution)/shard_map/all_to_all | solution.py:30
  131.4 5.6 %all-to-all-start.1 = ((f32[16,30,128]{2,1,0:T(8,128)}), f32[16,30,128]{2,1,0:T(8,128)S(1)}, u32[]{:S(2)}, u32[]{:S(2)}) async-start(f32[16,30,128]{2,1,0:T(8,128)} %reshape.202), calls=%async_computation.1 | async-start | bytes 524288 | tf_op jit(solution)/shard_map/all_to_all | solution.py:30
  137.8 8.3 %all-to-all-done.1 = f32[16,30,128]{2,1,0:T(8,128)S(1)} async-done(((f32[16,30,128]{2,1,0:T(8,128)}), f32[16,30,128]{2,1,0:T(8,128)S(1)}, u32[]{:S(2)}, u32[]{:S(2)}) %all-to-all-start.1) | async-done | bytes 245792 | tf_op jit(solution)/shard_map/all_to_all | solution.py:30
  147.1 3.8 %collective-permute-start.8 = (f32[48,128]{1,0:T(8,128)S(1)}, f32[48,128]{1,0:T(8,128)S(1)}, u32[]{:S(2)}, u32[]{:S(2)}) collective-permute-start(f32[48,128]{1,0:T(8,128)S(1)} %pad_maximum_fusion.37), channel_id=1, source_target_pairs={{0,496},{1,497},{2,498},{3,499},{4,500},{5,501},{6,502},{7,503},{8... | collective-permute-start | bytes 73736 | tf_op jit(solution)/shard_map/ppermute | solution.py:26
  151.0 2.2 %collective-permute-start.6 = (f32[84,128]{1,0:T(8,128)S(1)}, f32[84,128]{1,0:T(8,128)S(1)}, u32[]{:S(2)}, u32[]{:S(2)}) collective-permute-start(f32[84,128]{1,0:T(8,128)S(1)} %pad_maximum_fusion.19), channel_id=1, source_target_pairs={{0,1},{1,2},{2,3},{3,4},{4,5},{5,6},{6,7},{7,8},{8,9},{9,10},{10,1... | collective-permute-start | bytes 129032 | tf_op jit(solution)/shard_map/ppermute | solution.py:26
  153.3 7.0 %collective-permute-start.7 = (f32[84,128]{1,0:T(8,128)S(1)}, f32[84,128]{1,0:T(8,128)S(1)}, u32[]{:S(2)}, u32[]{:S(2)}) collective-permute-start(f32[84,128]{1,0:T(8,128)S(1)} %pad_maximum_fusion.20), channel_id=1, source_target_pairs={{0,15},{1,0},{2,1},{3,2},{4,3},{5,4},{6,5},{7,6},{8,7},{9,8},{10,9... | collective-permute-start | bytes 129032 | tf_op jit(solution)/shard_map/ppermute | solution.py:26
  161.5 3.8 %collective-permute-start.9 = (f32[240,128]{1,0:T(8,128)S(1)}, f32[240,128]{1,0:T(8,128)S(1)}, u32[]{:S(2)}, u32[]{:S(2)}) collective-permute-start(f32[240,128]{1,0:T(8,128)S(1)} %pad_maximum_fusion.1), channel_id=1, source_target_pairs={{0,16},{1,17},{2,18},{3,19},{4,20},{5,21},{6,22},{7,23},{8,24},{9,... | collective-permute-start | bytes 368648 | tf_op jit(solution)/shard_map/ppermute | solution.py:26
  166.4 5.3 %collective-permute-start.10 = (f32[240,128]{1,0:T(8,128)S(1)}, f32[240,128]{1,0:T(8,128)S(1)}, u32[]{:S(2)}, u32[]{:S(2)}) collective-permute-start(f32[240,128]{1,0:T(8,128)S(1)} %pad_maximum_fusion.2), channel_id=1, source_target_pairs={{0,496},{1,497},{2,498},{3,499},{4,500},{5,501},{6,502},{7,503},{8... | collective-permute-start | bytes 368648 | tf_op jit(solution)/shard_map/ppermute | solution.py:26
  172.4 6.6 %collective-permute-done.10 = f32[240,128]{1,0:T(8,128)S(1)} collective-permute-done((f32[240,128]{1,0:T(8,128)S(1)}, f32[240,128]{1,0:T(8,128)S(1)}, u32[]{:S(2)}, u32[]{:S(2)}) %collective-permute-start.10) | collective-permute-done | bytes 122912 | tf_op jit(solution)/shard_map/ppermute | solution.py:26
  179.1 5.6 %collective-permute-start.11 = (f32[144,128]{1,0:T(8,128)S(1)}, f32[144,128]{1,0:T(8,128)S(1)}, u32[]{:S(2)}, u32[]{:S(2)}) collective-permute-start(f32[144,128]{1,0:T(8,128)S(1)} %pad_maximum_fusion.15), channel_id=1, source_target_pairs={{0,16},{1,17},{2,18},{3,19},{4,20},{5,21},{6,22},{7,23},{8,24},{9,... | collective-permute-start | bytes 221192 | tf_op jit(solution)/shard_map/ppermute | solution.py:26
  185.7 2.4 %shard_map.163 = f32[3,2,8,128]{3,2,1,0:T(8,128)} custom-call(s32[1]{0:T(128)} %bitcast.core_ref, f32[3,10,16,128]{3,2,1,0:T(8,128)S(1)} %reverse_dynamic-update-slice_fusion.adjoint, f32[12,24,128]{2,1,0:T(8,128)S(1)} %get-tuple-element.23.visc), custom_call_target="tpu_custom_call" | custom-call | tf_op jit(solution)/shard_map/pallas_call | solution.py:73
  (162 shorter events, 27.7 us)
Async XLA Ops:
  0.6 74.2 %copy-start = (f32[1,128,128]{2,1,0:T(8,128)S(1)}, f32[1,128,128]{2,1,0:T(8,128)}, u32[]{:S(2)}) copy-start(f32[1,128,128]{2,1,0:T(8,128)} %param.16) | copy-start | bytes 196612
  2.4 21.2 %collective-permute-start = (f32[46,128]{1,0:T(8,128)S(1)}, f32[46,128]{1,0:T(8,128)S(1)}, u32[]{:S(2)}, u32[]{:S(2)}) collective-permute-start(f32[46,128]{1,0:T(8,128)S(1)} %pad_maximum_fusion.34), channel_id=1, source_target_pairs={{0,1},{1,2},{2,3},{3,4},{4,5},{5,6},{6,7},{7,8},{8,9},{9,10},{10,1... | collective-permute-start | bytes 70664 | tf_op jit(solution)/shard_map/ppermute | solution.py:26
  6.4 17.2 %collective-permute-start.1 = (f32[46,128]{1,0:T(8,128)S(1)}, f32[46,128]{1,0:T(8,128)S(1)}, u32[]{:S(2)}, u32[]{:S(2)}) collective-permute-start(f32[46,128]{1,0:T(8,128)S(1)} %pad_maximum_fusion.35), channel_id=1, source_target_pairs={{0,15},{1,0},{2,1},{3,2},{4,3},{5,4},{6,5},{7,6},{8,7},{9,8},{10,9... | collective-permute-start | bytes 70664 | tf_op jit(solution)/shard_map/ppermute | solution.py:26
  13.9 11.3 %collective-permute-start.2 = (f32[56,128]{1,0:T(8,128)S(1)}, f32[56,128]{1,0:T(8,128)S(1)}, u32[]{:S(2)}, u32[]{:S(2)}) collective-permute-start(f32[56,128]{1,0:T(8,128)S(1)} %pad_maximum_fusion.21), channel_id=1, source_target_pairs={{0,496},{1,497},{2,498},{3,499},{4,500},{5,501},{6,502},{7,503},{8... | collective-permute-start | bytes 86024 | tf_op jit(solution)/shard_map/ppermute | solution.py:26
  23.7 49.3 %copy-start.3 = (f32[1,9,128]{2,0,1:T(1,128)S(1)}, f32[1,9,128]{2,0,1:T(1,128)}, u32[]{:S(2)}) copy-start(f32[1,9,128]{2,0,1:T(1,128)} %param.14) | copy-start | bytes 13828
  23.7 49.3 %copy-start.8 = (f32[1,128]{1,0:T(1,128)S(1)}, f32[1,128]{1,0:T(1,128)}, u32[]{:S(2)}) copy-start(f32[1,128]{1,0:T(1,128)} %param.15) | copy-start | bytes 1540
  25.2 7.9 %collective-permute-start.3 = (f32[200,128]{1,0:T(8,128)S(1)}, f32[200,128]{1,0:T(8,128)S(1)}, u32[]{:S(2)}, u32[]{:S(2)}) collective-permute-start(f32[200,128]{1,0:T(8,128)S(1)} %pad_maximum_fusion.3), channel_id=1, source_target_pairs={{0,16},{1,17},{2,18},{3,19},{4,20},{5,21},{6,22},{7,23},{8,24},{9,... | collective-permute-start | bytes 307208 | tf_op jit(solution)/shard_map/ppermute | solution.py:26
  33.2 11.8 %collective-permute-start.4 = (f32[240,128]{1,0:T(8,128)S(1)}, f32[240,128]{1,0:T(8,128)S(1)}, u32[]{:S(2)}, u32[]{:S(2)}) collective-permute-start(f32[240,128]{1,0:T(8,128)S(1)} %constant_dynamic-update-slice_fusion), channel_id=1, source_target_pairs={{0,496},{1,497},{2,498},{3,499},{4,500},{5,501},{6,502},{7,503},{8... | collective-permute-start | bytes 368648 | tf_op jit(solution)/shard_map/ppermute | solution.py:26
  45.0 7.9 %collective-permute-start.5 = (f32[168,128]{1,0:T(8,128)S(1)}, f32[168,128]{1,0:T(8,128)S(1)}, u32[]{:S(2)}, u32[]{:S(2)}) collective-permute-start(f32[168,128]{1,0:T(8,128)S(1)} %slice.416), channel_id=1, source_target_pairs={{0,16},{1,17},{2,18},{3,19},{4,20},{5,21},{6,22},{7,23},{8,24},{9,... | collective-permute-start | bytes 258056 | tf_op jit(solution)/shard_map/ppermute | solution.py:26
  58.5 16.3 %copy-start.5 = (f32[1,128]{1,0:T(1,128)S(1)}, f32[1,128]{1,0:T(1,128)}, u32[]{:S(2)}) copy-start(f32[1,128]{1,0:T(1,128)} %param.17) | copy-start | bytes 1540
  81.3 1.4 copy-start.1
  81.3 13.7 %copy-start.6 = (f32[1,6]{1,0:T(1,128)S(1)}, f32[1,6]{1,0:T(1,128)}, u32[]{:S(2)}) copy-start(f32[1,6]{1,0:T(1,128)} %param.19) | copy-start | bytes 76
  83.8 4.0 %collective-permute-start.12 = (f32[146,128]{1,0:T(8,128)S(1)}, f32[146,128]{1,0:T(8,128)S(1)}, u32[]{:S(2)}, u32[]{:S(2)}) collective-permute-start(f32[146,128]{1,0:T(8,128)S(1)} %concatenate.133), channel_id=1, source_target_pairs={{0,16},{1,17},{2,18},{3,19},{4,20},{5,21},{6,22},{7,23},{8,24},{9,... | collective-permute-start | bytes 224264 | tf_op jit(solution)/shard_map/ppermute | solution.py:26
  88.4 21.8 %all-to-all-start.2 = ((f32[16,10,128]{2,1,0:T(8,128)}), f32[16,10,128]{2,1,0:T(8,128)S(1)}, u32[]{:S(2)}, u32[]{:S(2)}) async-start(f32[16,10,128]{2,1,0:T(8,128)} %reshape.230), calls=%async_computation.2 | async-start | bytes 262144 | tf_op jit(solution)/shard_map/all_to_all | solution.py:30
  95.0 1.6 copy-start.2
  97.5 39.5 %copy-start.7 = (s32[16]{0:T(128)S(1)}, s32[16]{0:T(128)}, u32[]{:S(2)}) copy-start(s32[16]{0:T(128)} %get-tuple-element.19.slot_ref) | copy-start | bytes 196
  110.9 20.5 %all-to-all-start.3 = ((f32[16,10,128]{2,1,0:T(8,128)}), f32[16,10,128]{2,1,0:T(8,128)S(1)}, u32[]{:S(2)}, u32[]{:S(2)}) async-start(f32[16,10,128]{2,1,0:T(8,128)} %broadcast_in_dim.31), calls=%async_computation.3 | async-start | bytes 262144 | tf_op jit(solution)/shard_map/all_to_all | solution.py:30
  131.4 14.6 %all-to-all-start.1 = ((f32[16,30,128]{2,1,0:T(8,128)}), f32[16,30,128]{2,1,0:T(8,128)S(1)}, u32[]{:S(2)}, u32[]{:S(2)}) async-start(f32[16,30,128]{2,1,0:T(8,128)} %reshape.202), calls=%async_computation.1 | async-start | bytes 524288 | tf_op jit(solution)/shard_map/all_to_all | solution.py:30
  147.1 13.2 %collective-permute-start.8 = (f32[48,128]{1,0:T(8,128)S(1)}, f32[48,128]{1,0:T(8,128)S(1)}, u32[]{:S(2)}, u32[]{:S(2)}) collective-permute-start(f32[48,128]{1,0:T(8,128)S(1)} %pad_maximum_fusion.37), channel_id=1, source_target_pairs={{0,496},{1,497},{2,498},{3,499},{4,500},{5,501},{6,502},{7,503},{8... | collective-permute-start | bytes 73736 | tf_op jit(solution)/shard_map/ppermute | solution.py:26
  151.0 9.2 %collective-permute-start.6 = (f32[84,128]{1,0:T(8,128)S(1)}, f32[84,128]{1,0:T(8,128)S(1)}, u32[]{:S(2)}, u32[]{:S(2)}) collective-permute-start(f32[84,128]{1,0:T(8,128)S(1)} %pad_maximum_fusion.19), channel_id=1, source_target_pairs={{0,1},{1,2},{2,3},{3,4},{4,5},{5,6},{6,7},{7,8},{8,9},{9,10},{10,1... | collective-permute-start | bytes 129032 | tf_op jit(solution)/shard_map/ppermute | solution.py:26
  153.3 8.1 %collective-permute-start.7 = (f32[84,128]{1,0:T(8,128)S(1)}, f32[84,128]{1,0:T(8,128)S(1)}, u32[]{:S(2)}, u32[]{:S(2)}) collective-permute-start(f32[84,128]{1,0:T(8,128)S(1)} %pad_maximum_fusion.20), channel_id=1, source_target_pairs={{0,15},{1,0},{2,1},{3,2},{4,3},{5,4},{6,5},{7,6},{8,7},{9,8},{10,9... | collective-permute-start | bytes 129032 | tf_op jit(solution)/shard_map/ppermute | solution.py:26
  161.5 4.8 %collective-permute-start.9 = (f32[240,128]{1,0:T(8,128)S(1)}, f32[240,128]{1,0:T(8,128)S(1)}, u32[]{:S(2)}, u32[]{:S(2)}) collective-permute-start(f32[240,128]{1,0:T(8,128)S(1)} %pad_maximum_fusion.1), channel_id=1, source_target_pairs={{0,16},{1,17},{2,18},{3,19},{4,20},{5,21},{6,22},{7,23},{8,24},{9,... | collective-permute-start | bytes 368648 | tf_op jit(solution)/shard_map/ppermute | solution.py:26
  166.4 12.6 %collective-permute-start.10 = (f32[240,128]{1,0:T(8,128)S(1)}, f32[240,128]{1,0:T(8,128)S(1)}, u32[]{:S(2)}, u32[]{:S(2)}) collective-permute-start(f32[240,128]{1,0:T(8,128)S(1)} %pad_maximum_fusion.2), channel_id=1, source_target_pairs={{0,496},{1,497},{2,498},{3,499},{4,500},{5,501},{6,502},{7,503},{8... | collective-permute-start | bytes 368648 | tf_op jit(solution)/shard_map/ppermute | solution.py:26
  179.1 6.5 %collective-permute-start.11 = (f32[144,128]{1,0:T(8,128)S(1)}, f32[144,128]{1,0:T(8,128)S(1)}, u32[]{:S(2)}, u32[]{:S(2)}) collective-permute-start(f32[144,128]{1,0:T(8,128)S(1)} %pad_maximum_fusion.15), channel_id=1, source_target_pairs={{0,16},{1,17},{2,18},{3,19},{4,20},{5,21},{6,22},{7,23},{8,24},{9,... | collective-permute-start | bytes 221192 | tf_op jit(solution)/shard_map/ppermute | solution.py:26
  (1 other events, 0.7 us)
